TPU v7x, 128 devices: a whole 4x4x4 slice. The times are simulated.
128 devices in a mesh: leaf: 128 (over z, x, y, core).
Axes of the slice: x: 4, y: 4, z: 4, core: 2. Of those that a mesh axis runs over, the one named last changes fastest.
Arguments:
- vectors: float32 [524288, 384], P('leaf'), may hold values from -6 to 6
- slot_frame: int32 [524288], P('leaf'), may hold values from 0 to 4095, as said below
- leaf_sizes: int32 [128, 8], P('leaf'), may hold values from 1 to 512, 3072 in all within a row
- near_field: float32 [1024, 512, 512], P('leaf'), may hold values from -0.25 to 0.25
- leaf_basis: float32 [1024, 512, 128], P('leaf'), may hold values from -0.25 to 0.25
- local_transfer: float32 [128, 15, 128, 128], P('leaf'), may hold values from -0.375 to 0.375
- local_coupling: float32 [128, 7, 128, 128], P('leaf'), may hold values from -1 to 1
- upper_transfer: float32 [128, 5, 128, 128], P('leaf'), as said below
- pair_coupling: float32 [128, 7, 128, 128], P('leaf'), as said below
Outputs:
- products: float32 [524288, 384], P('leaf')
- curvature: float32 [384], replicated
Inputs may be any that keep to these rules, and one draw needn't show every extreme that they name: `slot_frame`: each device's block of 4096 entries is a permutation of 0 to 4095. `leaf_sizes`: each device's 8 sizes sum to 3072. `upper_transfer`: at group level j (entry j - 1) all devices under the same node of 2^j device subtrees hold the same matrix. `pair_coupling`: at group level j (entry j) all 2^(j + 1) devices under the same parent of the pair hold the same matrix.
All inputs are finite; a program needn't handle non-finite values.
Results may differ from a plain program's by a relative error of at most 0.0003.
Values sent between devices are 32-bit elements; how exact they have to be, the bound alone decides.
No kernel may reach another device: no remote copies, remote signals or barrier semaphores. Data moves between devices by JAX's collectives and lax.ppermute only.
A program may use at most 128 MiB of HBM per device.

v0:
```python
import functools

import jax
import jax.numpy as jnp
from jax import lax
from jax.experimental import pallas as pl
from jax.experimental.pallas import tpu as pltpu
from jax.sharding import PartitionSpec as P

LEAF = 512
NL = 8
R = 128
V = 384
HALF = V // 2
QUART = HALF // 4
ROWS = NL * LEAF
S = 8
UN = 32
F32 = jnp.float32
BF16 = jnp.bfloat16
MIB = 1 << 20


def split(a):
    hi = a.astype(BF16)
    return hi, (a - hi.astype(F32)).astype(BF16)


def dot3s(terms, ca, cb):
    lhs, rhs = [], []
    for (ah, al), (bh, bl) in terms:
        lhs += [ah, ah, al]
        rhs += [bh, bl, bh]
    return lax.dot_general(
        jnp.concatenate(lhs, axis=ca),
        jnp.concatenate(rhs, axis=cb),
        (((ca,), (cb,)), ((), ())),
        preferred_element_type=F32,
    )


def dot3(a, b, ca=1, cb=0):
    return dot3s([(split(a), split(b))], ca, cb)


def tile_rows(start, count):
    return pl.ds(pl.multiple_of(start * S, S), count * S)


def rows_up_kernel(
    slot_hbm, sizes_hbm, v_hbm, basis_hbm, trans_hbm,
    xh_hbm, xl_hbm, call_ref, pay_ref,
    slot, sizes, vbuf, vt, xt, xh, xl, basis, trans, sem, vsem, osem,
):
    copies = [
        pltpu.make_async_copy(slot_hbm, slot, sem.at[0]),
        pltpu.make_async_copy(sizes_hbm, sizes, sem.at[1]),
        pltpu.make_async_copy(basis_hbm, basis, sem.at[2]),
        pltpu.make_async_copy(trans_hbm, trans, sem.at[3]),
    ]
    chunks = [
        pltpu.make_async_copy(
            v_hbm.at[pl.ds(c * LEAF, LEAF)], vbuf.at[pl.ds(c * LEAF, LEAF)], vsem.at[c]
        )
        for c in range(NL)
    ]
    copies[0].start()
    copies[1].start()
    for c in range(NL):
        chunks[c].start()
    copies[2].start()
    copies[3].start()
    for c in range(NL):
        chunks[c].wait()

        def spread(i, _, c=c):
            for u in range(4):
                base = pl.multiple_of(c * LEAF + i * 32 + u * 8, 8)
                for k in range(3):
                    vt[pl.ds(pl.multiple_of(base * S, 8) + k, 8, stride=S), :] = vbuf[
                        pl.ds(base, 8), 128 * k : 128 * k + 128
                    ]
            return 0

        lax.fori_loop(0, LEAF // 32, spread, 0)
    for c in copies:
        c.wait()
    outs = []
    coeffs = []
    for leaf in range(NL):
        size = sizes[0, leaf]

        def pick(i, _, leaf=leaf):
            base = pl.multiple_of(i * UN, UN)
            rows = [vt[tile_rows(slot[leaf * LEAF + base + r], 1), :] for r in range(UN)]
            for r in range(UN):
                xt[tile_rows(base + r, 1), :] = rows[r]
            return 0

        lax.fori_loop(0, (size + UN - 1) // UN, pick, 0)

        def pack(i, _, leaf=leaf, size=size):
            for u in range(2):
                base = pl.multiple_of(i * 32 + u * 16, 16)
                row = lax.broadcasted_iota(jnp.int32, (8, 128), 0) + base
                for k in range(3):
                    part = []
                    for half in range(2):
                        val = xt[pl.ds(pl.multiple_of((base + 8 * half) * S, 8) + k, 8, stride=S), :]
                        part.append(jnp.where(row + 8 * half < size, val, 0.0))
                    hi, lo = split(jnp.concatenate(part, axis=0))
                    xh[leaf, pl.ds(base, 16), 128 * k : 128 * k + 128] = hi
                    xl[leaf, pl.ds(base, 16), 128 * k : 128 * k + 128] = lo
            return 0

        lax.fori_loop(0, LEAF // 32, pack, 0)
        for n, (src, dst) in enumerate(((xh, xh_hbm), (xl, xl_hbm))):
            cp = pltpu.make_async_copy(src.at[leaf], dst.at[leaf], osem.at[2 * leaf + n])
            cp.start()
            outs.append(cp)
        c = dot3s([(split(basis[leaf]), (xh[leaf], xl[leaf]))], 0, 0)
        call_ref[leaf] = c
        coeffs.append(split(c))
    offset, at = 0, NL
    while len(coeffs) > 1:
        parents = []
        for m in range(len(coeffs) // 2):
            terms = [(split(trans[offset + 2 * m + t]), coeffs[2 * m + t]) for t in range(2)]
            c = dot3s(terms, 0, 0)
            parents.append(c)
            if len(coeffs) > 2:
                call_ref[at] = c
                at += 1
        offset += len(coeffs)
        coeffs = [split(c) for c in parents]
    pay_ref[0] = parents[0].T
    pay_ref[1] = dot3s([(coeffs[0], split(trans[2 * NL - 2]))], 0, 0)
    for cp in outs:
        cp.wait()


def rows_up(slot, sizes, vectors, basis, trans):
    hbm = pl.BlockSpec(memory_space=pl.ANY)
    vmem = pl.BlockSpec(memory_space=pltpu.VMEM)
    return pl.pallas_call(
        rows_up_kernel,
        out_shape=(
            jax.ShapeDtypeStruct((NL, LEAF, V), BF16),
            jax.ShapeDtypeStruct((NL, LEAF, V), BF16),
            jax.ShapeDtypeStruct((14, R, V), F32),
            jax.ShapeDtypeStruct((2, V, R), F32),
        ),
        in_specs=[hbm] * 5,
        out_specs=(hbm, hbm, vmem, vmem),
        scratch_shapes=[
            pltpu.SMEM((ROWS,), jnp.int32),
            pltpu.SMEM((1, NL), jnp.int32),
            pltpu.VMEM((ROWS, V), F32),
            pltpu.VMEM((ROWS * S, 128), F32),
            pltpu.VMEM((LEAF * S, 128), F32),
            pltpu.VMEM((NL, LEAF, V), BF16),
            pltpu.VMEM((NL, LEAF, V), BF16),
            pltpu.VMEM((NL, LEAF, R), F32),
            pltpu.VMEM((2 * NL - 1, R, R), F32),
            pltpu.SemaphoreType.DMA((4,)),
            pltpu.SemaphoreType.DMA((NL,)),
            pltpu.SemaphoreType.DMA((2 * NL,)),
        ],
        compiler_params=pltpu.CompilerParams(vmem_limit_bytes=48 * MIB),
        cost_estimate=pl.CostEstimate(flops=2 * 10**9, bytes_accessed=18 * 10**6, transcendentals=0),
        name="rows_up",
    )(slot, sizes, vectors, basis, trans)


def near_local_kernel(
    near_ref, xh_ref, xl_ref, basis_ref, call_ref, trans_ref, coup_ref,
    part_ref, eh_ref, el_ref, curv_ref, inc, tmat, near_h, near_l,
):
    leaf = pl.program_id(0)

    @pl.when(leaf == 0)
    def _():
        total = jnp.zeros((1, V), F32)
        starts = (0, 8, 12)
        fields = [None] * 14
        pair = 0
        for height in range(3):
            for m in range(4 >> height):
                a = starts[height] + 2 * m
                bm = split(coup_ref[pair])
                ca, cb = call_ref[a], call_ref[a + 1]
                fields[a] = dot3s([(bm, split(cb))], 1, 0)
                fields[a + 1] = dot3s([(bm, split(ca))], 0, 0)
                total += 2.0 * jnp.sum(ca * fields[a], axis=0, keepdims=True)
                pair += 1
        curv_ref[...] = jnp.broadcast_to(total, (8, V))
        top = [split(fields[12 + m]) for m in range(2)]
        tops = [split(trans_ref[12 + m]) for m in range(2)]
        for m in range(4):
            w = split(trans_ref[8 + m])
            mid = split(fields[8 + m] + dot3s([(w, top[m // 2])], 1, 0))
            tmid = split(dot3s([(w, tops[m // 2])], 1, 0))
            for n in (2 * m, 2 * m + 1):
                wl = split(trans_ref[n])
                inc[n] = fields[n] + dot3s([(wl, mid)], 1, 0)
                tmat[n] = dot3s([(wl, tmid)], 1, 0)

    nh, nlo = split(near_ref[0])
    near_h[...] = nh
    near_l[...] = nlo
    xh, xl = xh_ref[0], xl_ref[0]
    total = jnp.zeros((1, V), F32)
    base = split(basis_ref[0])
    g = split(inc[leaf])
    for blk in range(4):
        rows = slice(128 * blk, 128 * blk + 128)
        prod = dot3s([((near_h[rows, :], near_l[rows, :]), (xh, xl))], 1, 0)
        xb = xh[rows, :].astype(F32) + xl[rows, :].astype(F32)
        total += jnp.sum(prod * xb, axis=0, keepdims=True)
        part_ref[0, rows, :] = prod + dot3s(
            [((base[0][rows, :], base[1][rows, :]), g)], 1, 0
        )
    curv_ref[...] += jnp.broadcast_to(total, (8, V))
    e = dot3s([(base, split(tmat[leaf]))], 1, 0)
    eh, el = split(e)
    eh_ref[0] = eh
    el_ref[0] = el


def near_local(near, xh, xl, basis, call, trans, coup):
    def leafwise(*shape):
        return pl.BlockSpec((1,) + shape, lambda i: (i, 0, 0))

    def whole(*shape):
        return pl.BlockSpec(shape, lambda i: (0,) * len(shape))

    return pl.pallas_call(
        near_local_kernel,
        grid=(NL,),
        out_shape=(
            jax.ShapeDtypeStruct((NL, LEAF, V), F32),
            jax.ShapeDtypeStruct((NL, LEAF, R), BF16),
            jax.ShapeDtypeStruct((NL, LEAF, R), BF16),
            jax.ShapeDtypeStruct((8, V), F32),
        ),
        in_specs=[
            leafwise(LEAF, LEAF),
            leafwise(LEAF, V),
            leafwise(LEAF, V),
            leafwise(LEAF, R),
            whole(14, R, V),
            whole(2 * NL - 1, R, R),
            whole(NL - 1, R, R),
        ],
        out_specs=(leafwise(LEAF, V), leafwise(LEAF, R), leafwise(LEAF, R), whole(8, V)),
        scratch_shapes=[
            pltpu.VMEM((NL, R, V), F32),
            pltpu.VMEM((NL, R, R), F32),
            pltpu.VMEM((LEAF, LEAF), BF16),
            pltpu.VMEM((LEAF, LEAF), BF16),
        ],
        compiler_params=pltpu.CompilerParams(vmem_limit_bytes=40 * MIB),
        cost_estimate=pl.CostEstimate(flops=9 * 10**9, bytes_accessed=28 * 10**6, transcendentals=0),
        name="near_local",
    )(near, xh, xl, basis, call, trans, coup)


def chains_kernel(me, trans_ref, upper_ref, pair_ref, a1_ref, a2_ref, m0_ref, m1_ref, m3_ref):
    dev = me[0]

    def side(level):
        b = pair_ref[level]
        return jnp.where((dev >> level) % 2 == 0, b, b.T)

    m0_ref[0:R] = side(0).T
    m0_ref[R : 2 * R] = trans_ref[0].T
    w1 = upper_ref[0]
    w12 = dot3(w1, upper_ref[1])
    a1_ref[:, 0:R] = w1
    a1_ref[:, R : 2 * R] = w12
    m1_ref[0:R] = side(1).T
    m1_ref[R : 2 * R] = dot3(w1, side(2)).T
    m1_ref[2 * R : 3 * R] = w12.T
    w3 = upper_ref[2]
    w34 = dot3(w3, upper_ref[3])
    w345 = dot3(w34, upper_ref[4])
    a2_ref[:, 0:R] = w3
    a2_ref[:, R : 2 * R] = w34
    a2_ref[:, 2 * R : 3 * R] = w345
    m3_ref[0:R] = side(3).T
    m3_ref[R : 2 * R] = dot3(w3, side(4)).T
    m3_ref[2 * R : 3 * R] = dot3(w34, side(5)).T
    m3_ref[3 * R : 4 * R] = dot3(w345, side(6)).T


def after_core_kernel(me, pay_ref, got_ref, a1_ref, pair2_ref, lift3_ref):
    start = pl.multiple_of((me[0] % 2) * HALF, HALF)
    c1 = pay_ref[1, pl.ds(start, HALF), :] + got_ref[1, pl.ds(start, HALF), :]
    x = dot3(c1, a1_ref[...])
    pair2_ref[0] = c1
    pair2_ref[1] = x[:, 0:R]
    lift3_ref[...] = x[:, R : 2 * R]


def after_y_kernel(me, got_ref, a2_ref, send_ref, c3_ref):
    c3 = got_ref[0:QUART]
    for n in range(1, 4):
        c3 = c3 + got_ref[n * QUART : (n + 1) * QUART]
    c3_ref[...] = c3
    x = dot3(c3, a2_ref[...])
    parts = [c3, x[:, 0:R], x[:, R : 2 * R], x[:, 2 * R : 3 * R]]
    group = me[0] // 8
    for s in range(16):
        d = jnp.bitwise_xor(group, s)
        send_ref[s * QUART : (s + 1) * QUART] = jnp.where(
            d >= 8, parts[3], jnp.where(d >= 4, parts[2], jnp.where(d >= 2, parts[1], parts[0]))
        )


def after_top_kernel(me, got_ref, m3_ref, send_ref):
    group = me[0] // 8
    sums = [jnp.zeros((QUART, R), F32) for _ in range(4)]
    bounds = ((1, 2), (2, 4), (4, 8), (8, 16))
    for s in range(16):
        d = jnp.bitwise_xor(group, s)
        val = got_ref[s * QUART : (s + 1) * QUART]
        for j, (low, high) in enumerate(bounds):
            sums[j] += jnp.where(jnp.logical_and(d >= low, d < high), val, 0.0)
    inc3 = dot3(jnp.concatenate(sums, axis=1), m3_ref[...])
    for n in range(4):
        send_ref[n * QUART : (n + 1) * QUART] = inc3


def after_pair_kernel(pair2_ref, got_ref, c2_ref):
    c2_ref[...] = pair2_ref[1] + got_ref[1]


def to_core_kernel(got_ref, pair_got_ref, quad_got_ref, m1_ref, inc1_ref):
    sums = jnp.concatenate([pair_got_ref[0], quad_got_ref[...], got_ref[...]], axis=1)
    inc1_ref[...] = dot3(sums, m1_ref[...])


def curvature_kernel(
    me, pay_ref, got_ref, pair2_ref, pair_got_ref, c2_ref, quad_got_ref, c3_ref, inc3_ref,
    m0_ref, m1_ref, pair_ref, local_ref, send_ref, z,
):
    dev = me[0]
    z[...] = pay_ref[0] * dot3(got_ref[0], m0_ref[0:R])
    start = pl.multiple_of((dev % 2) * HALF, HALF)
    b2 = pair_ref[2]
    side2 = jnp.where((dev >> 2) % 2 == 0, b2, b2.T)
    field1 = dot3(pair_got_ref[0], m1_ref[0:R])
    field2 = dot3(quad_got_ref[...], side2, 1, 1)
    z[pl.ds(start, HALF), :] += pair2_ref[0] * field1 + 0.5 * (c2_ref[...] * field2)
    at = pl.multiple_of(start + ((dev // 2) % 4) * QUART, QUART)
    z[pl.ds(at, QUART), :] += c3_ref[...] * inc3_ref[0:QUART]
    zh, zl = split(z[...])
    ones = jnp.ones((8, R), BF16)
    total = lax.dot_general(
        jnp.concatenate([ones, ones], axis=1), jnp.concatenate([zh, zl], axis=1),
        (((1,), (1,)), ((), ())), preferred_element_type=F32,
    )
    total = total + local_ref[...]
    for n in range(16):
        send_ref[8 * n : 8 * n + 8] = total


def fold_kernel(count, repeat, scale, got_ref, send_ref):
    total = got_ref[0:8]
    for n in range(1, count):
        total = total + got_ref[8 * n : 8 * n + 8]
    total = total * scale
    for n in range(repeat):
        send_ref[8 * n : 8 * n + 8] = total


def small(body, outs, name, flops, scratch=()):
    vmem = pl.BlockSpec(memory_space=pltpu.VMEM)
    smem = pl.BlockSpec(memory_space=pltpu.SMEM)

    def call(*args):
        return pl.pallas_call(
            body,
            out_shape=tuple(jax.ShapeDtypeStruct(o, F32) for o in outs),
            in_specs=[smem if a.dtype == jnp.int32 else vmem for a in args],
            out_specs=tuple(vmem for _ in outs),
            scratch_shapes=list(scratch),
            compiler_params=pltpu.CompilerParams(vmem_limit_bytes=16 * MIB),
            cost_estimate=pl.CostEstimate(flops=flops, bytes_accessed=10**6, transcendentals=0),
            name=name,
        )(*args)

    return call


def rows_down_kernel(
    me, slot_hbm, sizes_hbm, part_hbm, eh_ref, el_ref, own_ref, other_ref, got_ref, m0_ref, out_hbm,
    slot, sizes, part, ot, pt, res, inct, sem, psem, osem,
):
    copies = [
        pltpu.make_async_copy(slot_hbm, slot, sem.at[0]),
        pltpu.make_async_copy(sizes_hbm, sizes, sem.at[1]),
    ]
    for c in copies:
        c.start()
    loads = [
        pltpu.make_async_copy(part_hbm.at[leaf], part.at[leaf], psem.at[leaf]) for leaf in range(NL)
    ]
    for c in loads:
        c.start()
    half = me[0] % 2
    inct[pl.ds(pl.multiple_of(half * HALF, HALF), HALF), :] = own_ref[...]
    inct[pl.ds(pl.multiple_of((1 - half) * HALF, HALF), HALF), :] = other_ref[...]
    root = dot3(jnp.concatenate([got_ref[0], inct[...]], axis=1), m0_ref[...])
    rh, rl = split(root.T)
    for c in copies:
        c.wait()
    zero = jnp.zeros((S, 128), F32)
    for leaf in range(NL):
        size = sizes[0, leaf]
        loads[leaf].wait()
        for blk in range(4):
            rows = slice(128 * blk, 128 * blk + 128)
            val = part[leaf, rows, :] + dot3s(
                [((eh_ref[leaf, rows, :], el_ref[leaf, rows, :]), (rh, rl))], 1, 0
            )
            row = lax.broadcasted_iota(jnp.int32, (128, V), 0) + 128 * blk
            val = jnp.where(row < size, val, 0.0)
            for b in range(16):
                for k in range(3):
                    ot[pl.ds((128 * blk + 8 * b) * S + k, 8, stride=S), :] = val[
                        8 * b : 8 * b + 8, 128 * k : 128 * k + 128
                    ]
        steps = (size + UN - 1) // UN

        def place(i, _, leaf=leaf):
            base = pl.multiple_of(i * UN, UN)
            rows = [ot[tile_rows(base + r, 1), :] for r in range(UN)]
            for r in range(UN):
                pt[tile_rows(slot[leaf * LEAF + base + r], 1), :] = rows[r]
            return 0

        lax.fori_loop(0, steps, place, 0)

        def blank(i, _, leaf=leaf):
            base = pl.multiple_of(i * UN, UN)
            for r in range(UN):
                pt[tile_rows(slot[leaf * LEAF + base + r], 1), :] = zero
            return 0

        lax.fori_loop(steps, LEAF // UN, blank, 0)
    stores = []
    for c in range(NL):

        def flat(i, _, c=c):
            for u in range(4):
                base = pl.multiple_of(c * LEAF + i * 32 + u * 8, 8)
                for k in range(3):
                    res[pl.ds(base, 8), 128 * k : 128 * k + 128] = pt[
                        pl.ds(pl.multiple_of(base * S, 8) + k, 8, stride=S), :
                    ]
            return 0

        lax.fori_loop(0, LEAF // 32, flat, 0)
        cp = pltpu.make_async_copy(
            res.at[pl.ds(c * LEAF, LEAF)], out_hbm.at[pl.ds(c * LEAF, LEAF)], osem.at[c]
        )
        cp.start()
        stores.append(cp)
    for cp in stores:
        cp.wait()


def rows_down(me, slot, sizes, part, eh, el, own, other, got, m0):
    hbm = pl.BlockSpec(memory_space=pl.ANY)
    vmem = pl.BlockSpec(memory_space=pltpu.VMEM)
    smem = pl.BlockSpec(memory_space=pltpu.SMEM)
    return pl.pallas_call(
        rows_down_kernel,
        out_shape=jax.ShapeDtypeStruct((ROWS, V), F32),
        in_specs=[smem, hbm, hbm, hbm] + [vmem] * 6,
        out_specs=hbm,
        scratch_shapes=[
            pltpu.SMEM((ROWS,), jnp.int32),
            pltpu.SMEM((1, NL), jnp.int32),
            pltpu.VMEM((NL, LEAF, V), F32),
            pltpu.VMEM((LEAF * S, 128), F32),
            pltpu.VMEM((ROWS * S, 128), F32),
            pltpu.VMEM((ROWS, V), F32),
            pltpu.VMEM((V, R), F32),
            pltpu.SemaphoreType.DMA((2,)),
            pltpu.SemaphoreType.DMA((NL,)),
            pltpu.SemaphoreType.DMA((NL,)),
        ],
        compiler_params=pltpu.CompilerParams(vmem_limit_bytes=48 * MIB),
        cost_estimate=pl.CostEstimate(flops=2 * 10**9, bytes_accessed=16 * 10**6, transcendentals=0),
        name="rows_down",
    )(me, slot, sizes, part, eh, el, own, other, got, m0)


def groups_of(bits, count):
    masks = [sum(1 << b for i, b in enumerate(bits) if k >> i & 1) for k in range(1 << len(bits))]
    full = masks[-1]
    return [[base | m for m in masks] for base in range(count) if base & full == 0]


def shards(
    vectors, slot_frame, leaf_sizes, near_field, leaf_basis,
    local_transfer, local_coupling, upper_transfer, pair_coupling,
):
    count = lax.axis_size("leaf")
    me = lax.axis_index("leaf").astype(jnp.int32).reshape(1)

    def swap(value, level):
        return lax.ppermute(value, "leaf", [(s, s ^ (1 << level)) for s in range(count)])

    def exchange(value, bits):
        return lax.all_to_all(
            value, "leaf", 0, 0, axis_index_groups=groups_of(bits, count), tiled=True
        )

    trans, coup, upper, pairs = (
        local_transfer[0], local_coupling[0], upper_transfer[0], pair_coupling[0],
    )
    a1, a2, m0, m1, m3 = small(
        chains_kernel, [(R, 2 * R), (R, 3 * R), (2 * R, R), (3 * R, R), (4 * R, R)], "chains", 10**8
    )(me, trans[2 * NL - 2 :], upper, pairs)
    xh, xl, call, pay = rows_up(slot_frame, leaf_sizes, vectors, leaf_basis, trans)
    core_got = swap(pay, 0)
    pair2, lift3 = small(after_core_kernel, [(2, HALF, R), (HALF, R)], "after_core", 10**8)(
        me, pay, core_got, a1
    )
    y_got = exchange(lift3, (1, 2))
    pair_got = swap(pair2, 1)
    top_send, c3 = small(after_y_kernel, [(16 * QUART, R), (QUART, R)], "after_y", 10**8)(
        me, y_got, a2
    )
    top_got = exchange(top_send, (3, 4, 5, 6))
    (c2,) = small(after_pair_kernel, [(HALF, R)], "after_pair", 10**6)(pair2, pair_got)
    quad_got = swap(c2, 2)
    part, eh, el, local = near_local(near_field, xh, xl, leaf_basis, call, trans, coup)
    (inc3,) = small(after_top_kernel, [(HALF, R)], "after_top", 10**8)(me, top_got, m3)
    inc3_got = exchange(inc3, (1, 2))
    (curv,) = small(curvature_kernel, [(128, V)], "curvature", 10**8, [pltpu.VMEM((V, R), F32)])(
        me, pay, core_got, pair2, pair_got, c2, quad_got, c3, inc3, m0, m1, pairs, local
    )
    curv = exchange(curv, (3, 4, 5, 6))
    (curv,) = small(functools.partial(fold_kernel, 16, 8, 1.0), [(64, V)], "fold_top", 10**5)(curv)
    curv = exchange(curv, (0, 1, 2))
    (curv,) = small(
        functools.partial(fold_kernel, 8, 1, 1.0 / (2.0 * LEAF)), [(8, V)], "fold_low", 10**5
    )(curv)
    (inc1,) = small(to_core_kernel, [(HALF, R)], "to_core", 10**8)(inc3_got, pair_got, quad_got, m1)
    inc1_got = swap(inc1, 0)
    products = rows_down(
        me, slot_frame, leaf_sizes, part, eh, el, inc1, inc1_got, core_got, m0
    )
    return products, curv[0]


def solution(mesh):
    return jax.shard_map(
        shards,
        mesh=mesh,
        in_specs=(
            P("leaf", None),
            P("leaf"),
            P("leaf", None),
            P("leaf", None, None),
            P("leaf", None, None),
            P("leaf", None, None, None),
            P("leaf", None, None, None),
            P("leaf", None, None, None),
            P("leaf", None, None, None),
        ),
        out_specs=(P("leaf", None), P()),
        check_vma=False,
    )
```

profile of v0, /device:TPU:1, one launch (start us, length us, event | category | flops | bytes accessed | tf_op | source)
XLA Modules:
  0.0 124.2 jit_solution(16239923230456360347)
XLA Ops:
  0.6 1.6 %copy-done = f32[8,512,128]{2,1,0:T(8,128)S(1)} copy-done((f32[8,512,128]{2,1,0:T(8,128)S(1)}, f32[8,512,128]{2,1,0:T(8,128)}, u32[]{:S(2)}) %copy-start) | copy-done | bytes 2097176
  2.2 1.2 copy-done.5
  3.4 0.7 copy-done.24
  4.1 0.7 copy-done.28
  4.8 15.6 %rows_up.1 = (bf16[8,512,384]{2,1,0:T(8,128)(2,1)}, bf16[8,512,384]{2,1,0:T(8,128)(2,1)}, f32[14,128,384]{2,1,0:T(8,128)}, f32[2,384,128]{2,1,0:T(8,128)S(1)}) custom-call(s32[4096]{0:T(1024)S(1)} %copy-done.24, s32[1,8]{1,0:T(1,128)S(1)} %copy-done.28, f32[4096,384]{1,0:T(8,128)} %v_hbm.1, f32[8,512,128]{2,1,0:T(8,128)S(1)} %copy-done, ...), custom_call_target="tpu_custom_call" | custom-call | flops 2000000000 | bytes 18000000 | tf_op jit(solution)/shard_map/rows_up/pallas_call | solution.py:145
  20.4 1.5 %collective-permute-start = (f32[2,384,128]{2,1,0:T(8,128)S(1)}, f32[2,384,128]{2,1,0:T(8,128)S(1)}, u32[]{:S(2)}, u32[]{:S(2)}) collective-permute-start(f32[2,384,128]{2,1,0:T(8,128)S(1)} %get-tuple-element.25.pay_ref), channel_id=1, source_target_pairs={{0,1},{1,0},{2,3},{3,2},{4,5},{5,4},{6,7},{7,6},{8,9},{9,8},{10,11... | collective-permute-start | bytes 1179656 | tf_op jit(solution)/shard_map/ppermute | solution.py:515
  21.9 0.8 slice_bitcast_fusion.trans_ref
  22.8 1.0 copy-done.21
  23.7 0.6 chains.1
  24.4 0.7 copy-done.13
  25.1 0.7 copy-done.22
  25.8 0.2 after_core.1
  26.0 0.4 copy-done.18
  26.4 0.7 copy-done.15
  27.1 8.7 %all_to_all.55 = f32[4,48,128]{2,1,0:T(8,128)S(1)} all-to-all(f32[4,48,128]{2,1,0:T(8,128)S(1)} %bitcast.28), channel_id=1, replica_groups={{0,2,4,6},{1,3,5,7},{8,10,12,14},{9,11,13,15},{16,18,20,22},{17,19,21,2..., dimensions={0} | all-to-all | bytes 196608 | tf_op jit(solution)/shard_map/all_to_all | solution.py:518
  35.8 0.2 after_y.1
  36.1 0.7 copy-done.20
  36.8 0.6 copy-done.26
  37.4 7.7 %all-to-all-start.1 = ((f32[16,48,128]{2,1,0:T(8,128)}), f32[16,48,128]{2,1,0:T(8,128)S(1)}, u32[]{:S(2)}, u32[]{:S(2)}) async-start(f32[16,48,128]{2,1,0:T(8,128)} %bitcast.24), calls=%async_computation.1 | async-start | bytes 786432 | tf_op jit(solution)/shard_map/all_to_all | solution.py:518
  45.1 0.5 collective-permute-start.1
  45.5 4.3 %collective-permute-done.1.got_ref.pair_got_ref = f32[2,192,128]{2,1,0:T(8,128)S(1)} collective-permute-done((f32[2,192,128]{2,1,0:T(8,128)}, f32[2,192,128]{2,1,0:T(8,128)S(1)}, u32[]{:S(2)}, u32[]{:S(2)}) %collective-permute-start.1) | collective-permute-done | bytes 196640 | tf_op jit(solution)/shard_map/ppermute | solution.py:515
  49.9 0.9 copy-done.16
  50.8 0.6 after_pair.1.c2_ref
  51.4 1.3 %collective-permute-start.2 = (f32[192,128]{1,0:T(8,128)}, f32[192,128]{1,0:T(8,128)}, u32[]{:S(2)}, u32[]{:S(2)}) collective-permute-start(f32[192,128]{1,0:T(8,128)} %after_pair.1.c2_ref), channel_id=1, source_target_pairs={{0,4},{1,5},{2,6},{3,7},{4,0},{5,1},{6,2},{7,3},{8,12},{9,13},{10,... | collective-permute-start | bytes 294920 | tf_op jit(solution)/shard_map/ppermute | solution.py:515
  52.7 0.6 all-to-all-done.1
  53.3 0.9 copy-done.23
  54.3 0.3 after_top.1.inc3_ref
  54.6 0.6 copy-done.11
  55.2 3.9 %all-to-all-start.2 = ((f32[4,48,128]{2,1,0:T(8,128)}), f32[4,48,128]{2,1,0:T(8,128)}, u32[]{:S(2)}, u32[]{:S(2)}) async-start(f32[4,48,128]{2,1,0:T(8,128)} %bitcast.22), calls=%async_computation.2 | async-start | bytes 196608 | tf_op jit(solution)/shard_map/all_to_all | solution.py:518
  59.2 0.0 copy-start.6
  59.2 1.2 copy-done.6
  60.4 1.9 %copy-done.30 = bf16[8,512,384]{2,1,0:T(8,128)(2,1)S(1)} copy-done((bf16[8,512,384]{2,1,0:T(8,128)(2,1)S(1)}, bf16[8,512,384]{2,1,0:T(8,128)(2,1)}, u32[]{:S(2)}) %copy-start.30) | copy-done | bytes 3145752
  62.3 1.8 %copy-done.31 = f32[14,128,384]{2,1,0:T(8,128)S(1)} copy-done((f32[14,128,384]{2,1,0:T(8,128)S(1)}, f32[14,128,384]{2,1,0:T(8,128)}, u32[]{:S(2)}) %copy-start.31) | copy-done | bytes 2752536
  64.0 1.0 copy-done.32
  65.1 16.3 %near_local.1 = (f32[8,512,384]{2,1,0:T(8,128)}, bf16[8,512,128]{2,1,0:T(8,128)(2,1)S(1)}, bf16[8,512,128]{2,1,0:T(8,128)(2,1)S(1)}, f32[8,384]{1,0:T(8,128)S(1)}) custom-call(f32[8,512,512]{2,1,0:T(8,128)} %near_ref.1, bf16[8,512,384]{2,1,0:T(8,128)(2,1)S(1)} %copy-done.30, bf16[8,512,384]{2,1,0:T(8,128)(2,1)} %get-tuple-element.20.xl_ref, ...), custom_call_target="tpu_custom_call" | custom-call | flops 8999999488 | bytes 28000000 | tf_op jit(solution)/shard_map/near_local/pallas_call | solution.py:237
  81.4 1.0 copy-done.7
  82.4 1.0 copy-done.9
  83.4 2.1 %curvature.1 = f32[128,384]{1,0:T(8,128)} custom-call(s32[1]{0:T(128)} %bitcast.me, f32[2,384,128]{2,1,0:T(8,128)S(1)} %copy-done.4, f32[2,384,128]{2,1,0:T(8,128)S(1)} %collective-permute-done.got_ref, f32[2,192,128]{2,1,0:T(8,128)S(1)} %copy-done.17, f32[2,192,128]{2,1,0:T(8,128)S(1)} %collective-permute-done.1.got_ref.pair_got_ref, ...), custom_call_target="tpu_custom_call" | custom-call | flops 100000000 | bytes 1000000 | tf_op jit(solution)/shard_map/curvature/pallas_call | solution.py:382
  85.5 5.9 %all-to-all-start.3 = ((f32[16,8,384]{2,1,0:T(8,128)}), f32[16,8,384]{2,1,0:T(8,128)S(1)}, u32[]{:S(2)}, u32[]{:S(2)}) async-start(f32[16,8,384]{2,1,0:T(8,128)} %bitcast.12), calls=%async_computation.3 | async-start | bytes 393216 | tf_op jit(solution)/shard_map/all_to_all | solution.py:518
  91.5 1.2 to_core.1.own_ref
  92.7 3.4 %collective-permute-start.3 = (f32[192,128]{1,0:T(8,128)S(1)}, f32[192,128]{1,0:T(8,128)S(1)}, u32[]{:S(2)}, u32[]{:S(2)}) collective-permute-start(f32[192,128]{1,0:T(8,128)S(1)} %to_core.1.own_ref), channel_id=1, source_target_pairs={{0,1},{1,0},{2,3},{3,2},{4,5},{5,4},{6,7},{7,6},{8,9},{9,8},{10,11... | collective-permute-start | bytes 294920 | tf_op jit(solution)/shard_map/ppermute | solution.py:515
  96.1 2.5 %all-to-all-done.3 = f32[16,8,384]{2,1,0:T(8,128)S(1)} async-done(((f32[16,8,384]{2,1,0:T(8,128)}), f32[16,8,384]{2,1,0:T(8,128)S(1)}, u32[]{:S(2)}, u32[]{:S(2)}) %all-to-all-start.3) | async-done | bytes 196640 | tf_op jit(solution)/shard_map/all_to_all | solution.py:518
  98.6 0.7 fold_top.1
  99.3 9.1 %all-to-all-start.4 = ((f32[8,8,384]{2,1,0:T(8,128)}), f32[8,8,384]{2,1,0:T(8,128)S(1)}, u32[]{:S(2)}, u32[]{:S(2)}) async-start(f32[8,8,384]{2,1,0:T(8,128)} %bitcast.14), calls=%async_computation.4 | async-start | bytes 196608 | tf_op jit(solution)/shard_map/all_to_all | solution.py:518
  108.4 1.2 copy-done.8
  109.6 1.2 copy-done.10
  110.9 12.7 %rows_down.1 = f32[4096,384]{1,0:T(8,128)} custom-call(s32[1]{0:T(128)} %bitcast.me, s32[4096]{0:T(1024)S(1)} %copy-done.25, s32[1,8]{1,0:T(1,128)S(1)} %copy-done.29, f32[8,512,384]{2,1,0:T(8,128)} %get-tuple-element.22.part_hbm, bf16[8,512,128]{2,1,0:T(8,128)(2,1)S(1)} %copy-done.8, bf16[8,512,128]{2,1,0:T(8,128)(2,1)S(1)} %copy-done.10, ...), custom_call_target="tpu_custom_call" | custom-call | flops 2000000000 | bytes 16000000 | tf_op jit(solution)/shard_map/rows_down/pallas_call | solution.py:478
  123.6 0.6 slice_reduce_fusion
  (49 shorter events, 0.1 us)
Async XLA Ops:
  0.6 1.6 %copy-start = (f32[8,512,128]{2,1,0:T(8,128)S(1)}, f32[8,512,128]{2,1,0:T(8,128)}, u32[]{:S(2)}) copy-start(f32[8,512,128]{2,1,0:T(8,128)} %basis_ref.1) | copy-start | bytes 6291460
  2.2 1.2 copy-start.5
  3.4 0.7 copy-start.24
  4.1 0.7 copy-start.28
  4.8 18.0 %copy-start.2 = (f32[1,7,128,128]{3,2,1,0:T(8,128)S(1)}, f32[1,7,128,128]{3,2,1,0:T(8,128)}, u32[]{:S(2)}) copy-start(f32[1,7,128,128]{3,2,1,0:T(8,128)} %param.17) | copy-start | bytes 1376260
  4.8 54.4 %copy-start.1 = (f32[8,512,128]{2,1,0:T(8,128)S(1)}, f32[8,512,128]{2,1,0:T(8,128)}, u32[]{:S(2)}) copy-start(f32[8,512,128]{2,1,0:T(8,128)} %basis_ref.1) | copy-start | bytes 6291460
  20.4 17.0 %copy-start.3 = (f32[2,384,128]{2,1,0:T(8,128)}, f32[2,384,128]{2,1,0:T(8,128)S(1)}, u32[]{:S(2)}) copy-start(f32[2,384,128]{2,1,0:T(8,128)S(1)} %get-tuple-element.25.pay_ref) | copy-start | bytes 1179652
  20.4 5.4 %collective-permute-start = (f32[2,384,128]{2,1,0:T(8,128)S(1)}, f32[2,384,128]{2,1,0:T(8,128)S(1)}, u32[]{:S(2)}, u32[]{:S(2)}) collective-permute-start(f32[2,384,128]{2,1,0:T(8,128)S(1)} %get-tuple-element.25.pay_ref), channel_id=1, source_target_pairs={{0,1},{1,0},{2,3},{3,2},{4,5},{5,4},{6,7},{7,6},{8,9},{9,8},{10,11... | collective-permute-start | bytes 1179656 | tf_op jit(solution)/shard_map/ppermute | solution.py:515
  22.8 1.0 copy-start.21
  24.4 0.7 copy-start.13
  25.1 0.7 copy-start.22
  25.8 0.7 copy-start.18
  26.4 0.7 copy-start.15
  36.0 0.7 copy-start.20
  36.8 0.6 copy-start.26
  37.4 15.9 %all-to-all-start.1 = ((f32[16,48,128]{2,1,0:T(8,128)}), f32[16,48,128]{2,1,0:T(8,128)S(1)}, u32[]{:S(2)}, u32[]{:S(2)}) async-start(f32[16,48,128]{2,1,0:T(8,128)} %bitcast.24), calls=%async_computation.1 | async-start | bytes 786432 | tf_op jit(solution)/shard_map/all_to_all | solution.py:518
  45.1 4.8 %collective-permute-start.1 = (f32[2,192,128]{2,1,0:T(8,128)}, f32[2,192,128]{2,1,0:T(8,128)S(1)}, u32[]{:S(2)}, u32[]{:S(2)}) collective-permute-start(f32[2,192,128]{2,1,0:T(8,128)} %copy-done.15), channel_id=1, source_target_pairs={{0,2},{1,3},{2,0},{3,1},{4,6},{5,7},{6,4},{7,5},{8,10},{9,11},{10,... | collective-permute-start | bytes 589832 | tf_op jit(solution)/shard_map/ppermute | solution.py:515
  49.9 0.9 copy-start.16
  51.4 31.9 %collective-permute-start.2 = (f32[192,128]{1,0:T(8,128)}, f32[192,128]{1,0:T(8,128)}, u32[]{:S(2)}, u32[]{:S(2)}) collective-permute-start(f32[192,128]{1,0:T(8,128)} %after_pair.1.c2_ref), channel_id=1, source_target_pairs={{0,4},{1,5},{2,6},{3,7},{4,0},{5,1},{6,2},{7,3},{8,12},{9,13},{10,... | collective-permute-start | bytes 294920 | tf_op jit(solution)/shard_map/ppermute | solution.py:515
  53.3 1.0 copy-start.23
  54.6 0.6 copy-start.11
  55.2 30.3 %all-to-all-start.2 = ((f32[4,48,128]{2,1,0:T(8,128)}), f32[4,48,128]{2,1,0:T(8,128)}, u32[]{:S(2)}, u32[]{:S(2)}) async-start(f32[4,48,128]{2,1,0:T(8,128)} %bitcast.22), calls=%async_computation.2 | async-start | bytes 196608 | tf_op jit(solution)/shard_map/all_to_all | solution.py:518
  59.2 1.2 copy-start.6
  60.4 1.9 %copy-start.30 = (bf16[8,512,384]{2,1,0:T(8,128)(2,1)S(1)}, bf16[8,512,384]{2,1,0:T(8,128)(2,1)}, u32[]{:S(2)}) copy-start(bf16[8,512,384]{2,1,0:T(8,128)(2,1)} %get-tuple-element.19.xh_ref) | copy-start | bytes 9437188
  62.3 1.8 %copy-start.31 = (f32[14,128,384]{2,1,0:T(8,128)S(1)}, f32[14,128,384]{2,1,0:T(8,128)}, u32[]{:S(2)}) copy-start(f32[14,128,384]{2,1,0:T(8,128)} %get-tuple-element.21.call_ref) | copy-start | bytes 8257540
  64.0 1.0 copy-start.32
  65.1 18.3 %copy-start.4 = (f32[2,384,128]{2,1,0:T(8,128)S(1)}, f32[2,384,128]{2,1,0:T(8,128)}, u32[]{:S(2)}) copy-start(f32[2,384,128]{2,1,0:T(8,128)} %copy-done.3) | copy-start | bytes 1179652
  65.1 18.3 %copy-start.12 = (f32[192,128]{1,0:T(8,128)S(1)}, f32[192,128]{1,0:T(8,128)}, u32[]{:S(2)}) copy-start(f32[192,128]{1,0:T(8,128)} %copy-done.11) | copy-start | bytes 294916
  65.1 18.3 %copy-start.14 = (f32[384,128]{1,0:T(8,128)S(1)}, f32[384,128]{1,0:T(8,128)}, u32[]{:S(2)}) copy-start(f32[384,128]{1,0:T(8,128)} %copy-done.13) | copy-start | bytes 589828
  65.1 18.3 %copy-start.17 = (f32[2,192,128]{2,1,0:T(8,128)S(1)}, f32[2,192,128]{2,1,0:T(8,128)}, u32[]{:S(2)}) copy-start(f32[2,192,128]{2,1,0:T(8,128)} %copy-done.15) | copy-start | bytes 589828
  65.1 18.3 %copy-start.19 = (f32[256,128]{1,0:T(8,128)S(1)}, f32[256,128]{1,0:T(8,128)}, u32[]{:S(2)}) copy-start(f32[256,128]{1,0:T(8,128)} %copy-done.18) | copy-start | bytes 393220
  65.1 18.3 %copy-start.27 = (f32[48,128]{1,0:T(8,128)S(1)}, f32[48,128]{1,0:T(8,128)}, u32[]{:S(2)}) copy-start(f32[48,128]{1,0:T(8,128)} %copy-done.26) | copy-start | bytes 73732
  65.1 43.3 %copy-start.25 = (s32[4096]{0:T(1024)S(1)}, s32[4096]{0:T(1024)}, u32[]{:S(2)}) copy-start(s32[4096]{0:T(1024)} %slot_hbm.3) | copy-start | bytes 49156
  65.1 43.3 %copy-start.29 = (s32[1,8]{1,0:T(1,128)S(1)}, s32[1,8]{1,0:T(1,128)}, u32[]{:S(2)}) copy-start(s32[1,8]{1,0:T(1,128)} %sizes_hbm.3) | copy-start | bytes 100
  81.4 1.0 copy-start.7
  82.4 1.0 copy-start.9
  85.5 13.1 %all-to-all-start.3 = ((f32[16,8,384]{2,1,0:T(8,128)}), f32[16,8,384]{2,1,0:T(8,128)S(1)}, u32[]{:S(2)}, u32[]{:S(2)}) async-start(f32[16,8,384]{2,1,0:T(8,128)} %bitcast.12), calls=%async_computation.3 | async-start | bytes 393216 | tf_op jit(solution)/shard_map/all_to_all | solution.py:518
  92.7 15.7 %collective-permute-start.3 = (f32[192,128]{1,0:T(8,128)S(1)}, f32[192,128]{1,0:T(8,128)S(1)}, u32[]{:S(2)}, u32[]{:S(2)}) collective-permute-start(f32[192,128]{1,0:T(8,128)S(1)} %to_core.1.own_ref), channel_id=1, source_target_pairs={{0,1},{1,0},{2,3},{3,2},{4,5},{5,4},{6,7},{7,6},{8,9},{9,8},{10,11... | collective-permute-start | bytes 294920 | tf_op jit(solution)/shard_map/ppermute | solution.py:515
  99.3 24.2 %all-to-all-start.4 = ((f32[8,8,384]{2,1,0:T(8,128)}), f32[8,8,384]{2,1,0:T(8,128)S(1)}, u32[]{:S(2)}, u32[]{:S(2)}) async-start(f32[8,8,384]{2,1,0:T(8,128)} %bitcast.14), calls=%async_computation.4 | async-start | bytes 196608 | tf_op jit(solution)/shard_map/all_to_all | solution.py:518
  108.4 1.2 copy-start.8
  109.6 1.2 copy-start.10
where the time goes:
time: 125 us; the launch traced here: 124 us
  Pallas kernels  50.6 us (40%)
  starting transfers between devices  33.3 us (27%)
  local copies, waits for them, and re-layouts  23.2 us (19%)
  blocking collectives  8.67 us (7%)
  waiting for transfers between devices  7.47 us (6%)
    all_to_all x4, starting transfers between devices, exchange(): lax.all_to_all(value, 'leaf', 0, 0, axis_index_groups=groups_of(bits, cou...  26.6 us
    unnamed x66, local copies, waits for them, and re-layouts  21.8 us
    pallas_call x1, Pallas kernels, near_local(): pl.pallas_call(near_local_kernel, grid=(NL,), out_shape=(jax.ShapeDtypeSt...  16.3 us
    pallas_call x1, Pallas kernels, rows_up(): pl.pallas_call(rows_up_kernel, out_shape=(jax.ShapeDtypeStruct((NL, LEAF,...  15.6 us
    pallas_call x1, Pallas kernels, rows_down(): pl.pallas_call(rows_down_kernel, out_shape=jax.ShapeDtypeStruct((ROWS, V)...  12.7 us
    all_to_all x1, blocking collectives, exchange(): lax.all_to_all(value, 'leaf', 0, 0, axis_index_groups=groups_of(bits, cou...  8.67 us
    ppermute x4, starting transfers between devices, swap(): lax.ppermute(value, 'leaf', [(s, s ^ 1 << level) for s in range(count)])  6.72 us
    pallas_call x9, Pallas kernels, call(): pl.pallas_call(body, out_shape=tuple((jax.ShapeDtypeStruct(o, F32) for o...  6.06 us
  transfers between devices with their start and end apart: 8, of which 3 were waited for; matrix products, arithmetic and copies ran while one was open for 1% of the time, Pallas kernels for 28%

commit v1 on v0

--- a/solution.py
+++ b/solution.py
@@ -14,7 +14,7 @@
 HALF = V // 2
 QUART = HALF // 4
 ROWS = NL * LEAF
-S = 8
+S = 4
 UN = 32
 F32 = jnp.float32
 BF16 = jnp.bfloat16
@@ -47,10 +47,28 @@
     return pl.ds(pl.multiple_of(start * S, S), count * S)
 
 
+def far(x):
+    return pltpu.with_memory_space_constraint(x, pltpu.HBM)
+
+
+def lane_rows(p):
+    parts = [p[0:1, 128 * k : 128 * k + 128] for k in range(3)]
+    return jnp.concatenate(parts + [jnp.zeros((5, 128), F32)], axis=0)
+
+
+def row_sums(z):
+    zh, zl = split(z)
+    ones = jnp.ones((8, 2 * R), BF16)
+    return lax.dot_general(
+        ones, jnp.concatenate([zh, zl], axis=1), (((1,), (1,)), ((), ())),
+        preferred_element_type=F32,
+    )
+
+
 def rows_up_kernel(
     slot_hbm, sizes_hbm, v_hbm, basis_hbm, trans_hbm,
-    xh_hbm, xl_hbm, call_ref, pay_ref,
-    slot, sizes, vbuf, vt, xt, xh, xl, basis, trans, sem, vsem, osem,
+    xh_hbm, xl_hbm, call_hbm, pay_ref,
+    slot, sizes, vbuf, vt, xt, basis, trans, xh, xl, call_ref, sem, vsem, osem,
 ):
     copies = [
         pltpu.make_async_copy(slot_hbm, slot, sem.at[0]),
@@ -100,20 +118,21 @@
         lax.fori_loop(0, (size + UN - 1) // UN, pick, 0)
 
         def pack(i, _, leaf=leaf, size=size):
-            for u in range(2):
-                base = pl.multiple_of(i * 32 + u * 16, 16)
+            for u in range(8):
+                base = pl.multiple_of(i * 128 + u * 16, 16)
                 row = lax.broadcasted_iota(jnp.int32, (8, 128), 0) + base
                 for k in range(3):
                     part = []
                     for half in range(2):
-                        val = xt[pl.ds(pl.multiple_of((base + 8 * half) * S, 8) + k, 8, stride=S), :]
+                        at = pl.multiple_of((base + 8 * half) * S, 8) + k
+                        val = xt[pl.ds(at, 8, stride=S), :]
                         part.append(jnp.where(row + 8 * half < size, val, 0.0))
                     hi, lo = split(jnp.concatenate(part, axis=0))
                     xh[leaf, pl.ds(base, 16), 128 * k : 128 * k + 128] = hi
                     xl[leaf, pl.ds(base, 16), 128 * k : 128 * k + 128] = lo
             return 0
 
-        lax.fori_loop(0, LEAF // 32, pack, 0)
+        lax.fori_loop(0, LEAF // 128, pack, 0)
         for n, (src, dst) in enumerate(((xh, xh_hbm), (xl, xl_hbm))):
             cp = pltpu.make_async_copy(src.at[leaf], dst.at[leaf], osem.at[2 * leaf + n])
             cp.start()
@@ -133,6 +152,9 @@
                 at += 1
         offset += len(coeffs)
         coeffs = [split(c) for c in parents]
+    cp = pltpu.make_async_copy(call_ref, call_hbm, osem.at[2 * NL])
+    cp.start()
+    outs.append(cp)
     pay_ref[0] = parents[0].T
     pay_ref[1] = dot3s([(coeffs[0], split(trans[2 * NL - 2]))], 0, 0)
     for cp in outs:
@@ -140,46 +162,60 @@
 
 
 def rows_up(slot, sizes, vectors, basis, trans):
-    hbm = pl.BlockSpec(memory_space=pl.ANY)
+    hbm = pl.BlockSpec(memory_space=pltpu.HBM)
     vmem = pl.BlockSpec(memory_space=pltpu.VMEM)
     return pl.pallas_call(
         rows_up_kernel,
         out_shape=(
-            jax.ShapeDtypeStruct((NL, LEAF, V), BF16),
-            jax.ShapeDtypeStruct((NL, LEAF, V), BF16),
-            jax.ShapeDtypeStruct((14, R, V), F32),
+            pltpu.HBM((NL, LEAF, V), BF16),
+            pltpu.HBM((NL, LEAF, V), BF16),
+            pltpu.HBM((14, R, V), F32),
             jax.ShapeDtypeStruct((2, V, R), F32),
         ),
         in_specs=[hbm] * 5,
-        out_specs=(hbm, hbm, vmem, vmem),
+        out_specs=(hbm, hbm, hbm, vmem),
         scratch_shapes=[
             pltpu.SMEM((ROWS,), jnp.int32),
             pltpu.SMEM((1, NL), jnp.int32),
             pltpu.VMEM((ROWS, V), F32),
             pltpu.VMEM((ROWS * S, 128), F32),
             pltpu.VMEM((LEAF * S, 128), F32),
+            pltpu.VMEM((NL, LEAF, R), F32),
+            pltpu.VMEM((2 * NL - 1, R, R), F32),
             pltpu.VMEM((NL, LEAF, V), BF16),
             pltpu.VMEM((NL, LEAF, V), BF16),
-            pltpu.VMEM((NL, LEAF, R), F32),
-            pltpu.VMEM((2 * NL - 1, R, R), F32),
+            pltpu.VMEM((14, R, V), F32),
             pltpu.SemaphoreType.DMA((4,)),
             pltpu.SemaphoreType.DMA((NL,)),
-            pltpu.SemaphoreType.DMA((2 * NL,)),
+            pltpu.SemaphoreType.DMA((2 * NL + 1,)),
         ],
-        compiler_params=pltpu.CompilerParams(vmem_limit_bytes=48 * MIB),
+        compiler_params=pltpu.CompilerParams(vmem_limit_bytes=32 * MIB),
         cost_estimate=pl.CostEstimate(flops=2 * 10**9, bytes_accessed=18 * 10**6, transcendentals=0),
         name="rows_up",
-    )(slot, sizes, vectors, basis, trans)
+    )(far(slot), far(sizes), far(vectors), far(basis), far(trans))
 
 
 def near_local_kernel(
-    near_ref, xh_ref, xl_ref, basis_ref, call_ref, trans_ref, coup_ref,
-    part_ref, eh_ref, el_ref, curv_ref, inc, tmat, near_h, near_l,
+    me, near_ref, xh_ref, xl_ref, call_hbm, trans_hbm, coup_hbm,
+    pay_ref, got_ref, pair2_ref, pair_got_ref, c2_ref, m0_ref, m1_ref,
+    part_ref, inc_ref, tmat_ref, curv_ref, near_h, near_l, call_ref, trans_ref, coup_ref, z, sem,
 ):
     leaf = pl.program_id(0)
 
     @pl.when(leaf == 0)
     def _():
+        copies = [
+            pltpu.make_async_copy(trans_hbm, trans_ref, sem.at[0]),
+            pltpu.make_async_copy(coup_hbm, coup_ref, sem.at[1]),
+            pltpu.make_async_copy(call_hbm, call_ref, sem.at[2]),
+        ]
+        for c in copies:
+            c.start()
+        z[...] = pay_ref[0] * dot3(got_ref[0], m0_ref[0:R])
+        start = pl.multiple_of((me[0] % 2) * HALF, HALF)
+        z[pl.ds(start, HALF), :] += pair2_ref[0] * dot3(pair_got_ref[0], m1_ref[0:R])
+        for c in copies:
+            c.wait()
         total = jnp.zeros((1, V), F32)
         starts = (0, 8, 12)
         fields = [None] * 14
@@ -193,7 +229,7 @@
                 fields[a + 1] = dot3s([(bm, split(ca))], 0, 0)
                 total += 2.0 * jnp.sum(ca * fields[a], axis=0, keepdims=True)
                 pair += 1
-        curv_ref[...] = jnp.broadcast_to(total, (8, V))
+        curv_ref[...] = row_sums(z[...]) + jnp.broadcast_to(total, (8, V))
         top = [split(fields[12 + m]) for m in range(2)]
         tops = [split(trans_ref[12 + m]) for m in range(2)]
         for m in range(4):
@@ -202,71 +238,71 @@
             tmid = split(dot3s([(w, tops[m // 2])], 1, 0))
             for n in (2 * m, 2 * m + 1):
                 wl = split(trans_ref[n])
-                inc[n] = fields[n] + dot3s([(wl, mid)], 1, 0)
-                tmat[n] = dot3s([(wl, tmid)], 1, 0)
+                inc_ref[n] = fields[n] + dot3s([(wl, mid)], 1, 0)
+                tmat_ref[n] = dot3s([(wl, tmid)], 1, 0)
 
     nh, nlo = split(near_ref[0])
     near_h[...] = nh
     near_l[...] = nlo
     xh, xl = xh_ref[0], xl_ref[0]
     total = jnp.zeros((1, V), F32)
-    base = split(basis_ref[0])
-    g = split(inc[leaf])
     for blk in range(4):
         rows = slice(128 * blk, 128 * blk + 128)
         prod = dot3s([((near_h[rows, :], near_l[rows, :]), (xh, xl))], 1, 0)
         xb = xh[rows, :].astype(F32) + xl[rows, :].astype(F32)
         total += jnp.sum(prod * xb, axis=0, keepdims=True)
-        part_ref[0, rows, :] = prod + dot3s(
-            [((base[0][rows, :], base[1][rows, :]), g)], 1, 0
-        )
+        part_ref[0, rows, :] = prod
     curv_ref[...] += jnp.broadcast_to(total, (8, V))
-    e = dot3s([(base, split(tmat[leaf]))], 1, 0)
-    eh, el = split(e)
-    eh_ref[0] = eh
-    el_ref[0] = el
-
-
-def near_local(near, xh, xl, basis, call, trans, coup):
-    def leafwise(*shape):
-        return pl.BlockSpec((1,) + shape, lambda i: (i, 0, 0))
-
-    def whole(*shape):
-        return pl.BlockSpec(shape, lambda i: (0,) * len(shape))
-
+
+
+def near_local(me, near, xh, xl, call, trans, coup, *rest):
+    def leafwise(width):
+        return pl.BlockSpec((1, LEAF, width), lambda i: (i, 0, 0))
+
+    vmem = pl.BlockSpec(memory_space=pltpu.VMEM)
+    hbm = pl.BlockSpec(memory_space=pltpu.HBM)
+    smem = pl.BlockSpec(memory_space=pltpu.SMEM)
     return pl.pallas_call(
         near_local_kernel,
         grid=(NL,),
         out_shape=(
-            jax.ShapeDtypeStruct((NL, LEAF, V), F32),
-            jax.ShapeDtypeStruct((NL, LEAF, R), BF16),
-            jax.ShapeDtypeStruct((NL, LEAF, R), BF16),
+            pltpu.HBM((NL, LEAF, V), F32),
+            pltpu.HBM((NL, R, V), F32),
+            pltpu.HBM((NL, R, R), F32),
             jax.ShapeDtypeStruct((8, V), F32),
         ),
-        in_specs=[
-            leafwise(LEAF, LEAF),
-            leafwise(LEAF, V),
-            leafwise(LEAF, V),
-            leafwise(LEAF, R),
-            whole(14, R, V),
-            whole(2 * NL - 1, R, R),
-            whole(NL - 1, R, R),
-        ],
-        out_specs=(leafwise(LEAF, V), leafwise(LEAF, R), leafwise(LEAF, R), whole(8, V)),
+        in_specs=[smem, leafwise(LEAF), leafwise(V), leafwise(V), hbm, hbm, hbm]
+        + [vmem] * len(rest),
+        out_specs=(leafwise(V), vmem, vmem, vmem),
         scratch_shapes=[
-            pltpu.VMEM((NL, R, V), F32),
-            pltpu.VMEM((NL, R, R), F32),
             pltpu.VMEM((LEAF, LEAF), BF16),
             pltpu.VMEM((LEAF, LEAF), BF16),
+            pltpu.VMEM((14, R, V), F32),
+            pltpu.VMEM((2 * NL - 1, R, R), F32),
+            pltpu.VMEM((NL - 1, R, R), F32),
+            pltpu.VMEM((V, R), F32),
+            pltpu.SemaphoreType.DMA((3,)),
         ],
-        compiler_params=pltpu.CompilerParams(vmem_limit_bytes=40 * MIB),
-        cost_estimate=pl.CostEstimate(flops=9 * 10**9, bytes_accessed=28 * 10**6, transcendentals=0),
+        compiler_params=pltpu.CompilerParams(vmem_limit_bytes=32 * MIB),
+        cost_estimate=pl.CostEstimate(flops=7 * 10**9, bytes_accessed=10 * 10**6, transcendentals=0),
         name="near_local",
-    )(near, xh, xl, basis, call, trans, coup)
-
-
-def chains_kernel(me, trans_ref, upper_ref, pair_ref, a1_ref, a2_ref, m0_ref, m1_ref, m3_ref):
+    )(me, far(near), far(xh), far(xl), far(call), far(trans), far(coup), *rest)
+
+
+def chains_kernel(
+    me, trans_hbm, upper_hbm, pair_hbm, a1_ref, a2_ref, m0_ref, m1_ref, m3_ref, side2_ref,
+    trans_ref, upper_ref, pair_ref, sem,
+):
     dev = me[0]
+    copies = [
+        pltpu.make_async_copy(trans_hbm.at[pl.ds(2 * NL - 2, 1)], trans_ref, sem.at[0]),
+        pltpu.make_async_copy(upper_hbm, upper_ref, sem.at[1]),
+        pltpu.make_async_copy(pair_hbm, pair_ref, sem.at[2]),
+    ]
+    for c in copies:
+        c.start()
+    for c in copies:
+        c.wait()
 
     def side(level):
         b = pair_ref[level]
@@ -291,6 +327,7 @@
     m3_ref[R : 2 * R] = dot3(w3, side(4)).T
     m3_ref[2 * R : 3 * R] = dot3(w34, side(5)).T
     m3_ref[3 * R : 4 * R] = dot3(w345, side(6)).T
+    side2_ref[...] = side(2).T
 
 
 def after_core_kernel(me, pay_ref, got_ref, a1_ref, pair2_ref, lift3_ref):
@@ -317,8 +354,11 @@
         )
 
 
-def after_top_kernel(me, got_ref, m3_ref, send_ref):
-    group = me[0] // 8
+def after_top_kernel(
+    me, got_ref, m3_ref, side2_ref, c2_ref, quad_got_ref, c3_ref, local_ref, send_ref, z
+):
+    dev = me[0]
+    group = dev // 8
     sums = [jnp.zeros((QUART, R), F32) for _ in range(4)]
     bounds = ((1, 2), (2, 4), (4, 8), (8, 16))
     for s in range(16):
@@ -327,62 +367,57 @@
         for j, (low, high) in enumerate(bounds):
             sums[j] += jnp.where(jnp.logical_and(d >= low, d < high), val, 0.0)
     inc3 = dot3(jnp.concatenate(sums, axis=1), m3_ref[...])
+    z[...] = jnp.zeros((V, R), F32)
+    start = pl.multiple_of((dev % 2) * HALF, HALF)
+    z[pl.ds(start, HALF), :] = 0.5 * (c2_ref[...] * dot3(quad_got_ref[...], side2_ref[...]))
+    at = pl.multiple_of(start + ((dev // 2) % 4) * QUART, QUART)
+    z[pl.ds(at, QUART), :] += c3_ref[...] * inc3
+    share = lane_rows(local_ref[...] + row_sums(z[...]))
     for n in range(4):
-        send_ref[n * QUART : (n + 1) * QUART] = inc3
+        send_ref[n, 0:QUART] = inc3
+        send_ref[n, QUART : QUART + 8] = share
 
 
 def after_pair_kernel(pair2_ref, got_ref, c2_ref):
     c2_ref[...] = pair2_ref[1] + got_ref[1]
 
 
-def to_core_kernel(got_ref, pair_got_ref, quad_got_ref, m1_ref, inc1_ref):
-    sums = jnp.concatenate([pair_got_ref[0], quad_got_ref[...], got_ref[...]], axis=1)
-    inc1_ref[...] = dot3(sums, m1_ref[...])
-
-
-def curvature_kernel(
-    me, pay_ref, got_ref, pair2_ref, pair_got_ref, c2_ref, quad_got_ref, c3_ref, inc3_ref,
-    m0_ref, m1_ref, pair_ref, local_ref, send_ref, z,
-):
-    dev = me[0]
-    z[...] = pay_ref[0] * dot3(got_ref[0], m0_ref[0:R])
-    start = pl.multiple_of((dev % 2) * HALF, HALF)
-    b2 = pair_ref[2]
-    side2 = jnp.where((dev >> 2) % 2 == 0, b2, b2.T)
-    field1 = dot3(pair_got_ref[0], m1_ref[0:R])
-    field2 = dot3(quad_got_ref[...], side2, 1, 1)
-    z[pl.ds(start, HALF), :] += pair2_ref[0] * field1 + 0.5 * (c2_ref[...] * field2)
-    at = pl.multiple_of(start + ((dev // 2) % 4) * QUART, QUART)
-    z[pl.ds(at, QUART), :] += c3_ref[...] * inc3_ref[0:QUART]
-    zh, zl = split(z[...])
-    ones = jnp.ones((8, R), BF16)
-    total = lax.dot_general(
-        jnp.concatenate([ones, ones], axis=1), jnp.concatenate([zh, zl], axis=1),
-        (((1,), (1,)), ((), ())), preferred_element_type=F32,
-    )
-    total = total + local_ref[...]
+def to_core_kernel(got_ref, pair_got_ref, quad_got_ref, m1_ref, out_ref):
+    inc3 = jnp.concatenate([got_ref[n, 0:QUART] for n in range(4)], axis=0)
+    sums = jnp.concatenate([pair_got_ref[0], quad_got_ref[...], inc3], axis=1)
+    out_ref[0:HALF] = dot3(sums, m1_ref[...])
+    share = got_ref[0, QUART : QUART + 8]
+    for n in range(1, 4):
+        share = share + got_ref[n, QUART : QUART + 8]
+    out_ref[HALF : HALF + 8] = share
+
+
+def core_share_kernel(own_ref, other_ref, send_ref):
+    total = own_ref[HALF : HALF + 8] + other_ref[HALF : HALF + 8]
     for n in range(16):
-        send_ref[8 * n : 8 * n + 8] = total
-
-
-def fold_kernel(count, repeat, scale, got_ref, send_ref):
-    total = got_ref[0:8]
-    for n in range(1, count):
-        total = total + got_ref[8 * n : 8 * n + 8]
-    total = total * scale
-    for n in range(repeat):
-        send_ref[8 * n : 8 * n + 8] = total
-
-
-def small(body, outs, name, flops, scratch=()):
+        send_ref[n] = total
+
+
+def all_share_kernel(got_ref, out_ref):
+    total = got_ref[0]
+    for n in range(1, 16):
+        total = total + got_ref[n]
+    out_ref[...] = total * (1.0 / (2.0 * LEAF))
+
+
+def small(body, outs, name, flops, scratch=(), hbm_args=()):
     vmem = pl.BlockSpec(memory_space=pltpu.VMEM)
     smem = pl.BlockSpec(memory_space=pltpu.SMEM)
+    hbm = pl.BlockSpec(memory_space=pltpu.HBM)
 
     def call(*args):
         return pl.pallas_call(
             body,
             out_shape=tuple(jax.ShapeDtypeStruct(o, F32) for o in outs),
-            in_specs=[smem if a.dtype == jnp.int32 else vmem for a in args],
+            in_specs=[
+                smem if a.dtype == jnp.int32 else (hbm if n in hbm_args else vmem)
+                for n, a in enumerate(args)
+            ],
             out_specs=tuple(vmem for _ in outs),
             scratch_shapes=list(scratch),
             compiler_params=pltpu.CompilerParams(vmem_limit_bytes=16 * MIB),
@@ -394,12 +429,16 @@
 
 
 def rows_down_kernel(
-    me, slot_hbm, sizes_hbm, part_hbm, eh_ref, el_ref, own_ref, other_ref, got_ref, m0_ref, out_hbm,
-    slot, sizes, part, ot, pt, res, inct, sem, psem, osem,
+    me, slot_hbm, sizes_hbm, basis_hbm, part_hbm, local_hbm, tmat_hbm,
+    own_ref, other_ref, got_ref, m0_ref, out_hbm,
+    slot, sizes, basis, part, local_ref, tmat_ref, ot, pt, res, inct, sem, psem, osem,
 ):
     copies = [
         pltpu.make_async_copy(slot_hbm, slot, sem.at[0]),
         pltpu.make_async_copy(sizes_hbm, sizes, sem.at[1]),
+        pltpu.make_async_copy(tmat_hbm, tmat_ref, sem.at[2]),
+        pltpu.make_async_copy(local_hbm, local_ref, sem.at[3]),
+        pltpu.make_async_copy(basis_hbm, basis, sem.at[4]),
     ]
     for c in copies:
         c.start()
@@ -409,21 +448,20 @@
     for c in loads:
         c.start()
     half = me[0] % 2
-    inct[pl.ds(pl.multiple_of(half * HALF, HALF), HALF), :] = own_ref[...]
-    inct[pl.ds(pl.multiple_of((1 - half) * HALF, HALF), HALF), :] = other_ref[...]
+    inct[pl.ds(pl.multiple_of(half * HALF, HALF), HALF), :] = own_ref[0:HALF]
+    inct[pl.ds(pl.multiple_of((1 - half) * HALF, HALF), HALF), :] = other_ref[0:HALF]
     root = dot3(jnp.concatenate([got_ref[0], inct[...]], axis=1), m0_ref[...])
-    rh, rl = split(root.T)
+    rsplit = split(root.T)
     for c in copies:
         c.wait()
     zero = jnp.zeros((S, 128), F32)
     for leaf in range(NL):
         size = sizes[0, leaf]
         loads[leaf].wait()
+        inc = split(local_ref[leaf] + dot3s([(split(tmat_ref[leaf]), rsplit)], 1, 0))
         for blk in range(4):
             rows = slice(128 * blk, 128 * blk + 128)
-            val = part[leaf, rows, :] + dot3s(
-                [((eh_ref[leaf, rows, :], el_ref[leaf, rows, :]), (rh, rl))], 1, 0
-            )
+            val = part[leaf, rows, :] + dot3s([(split(basis[leaf, rows, :]), inc)], 1, 0)
             row = lax.broadcasted_iota(jnp.int32, (128, V), 0) + 128 * blk
             val = jnp.where(row < size, val, 0.0)
             for b in range(16):
@@ -471,31 +509,34 @@
         cp.wait()
 
 
-def rows_down(me, slot, sizes, part, eh, el, own, other, got, m0):
-    hbm = pl.BlockSpec(memory_space=pl.ANY)
+def rows_down(me, slot, sizes, basis, part, local, tmat, *rest):
+    hbm = pl.BlockSpec(memory_space=pltpu.HBM)
     vmem = pl.BlockSpec(memory_space=pltpu.VMEM)
     smem = pl.BlockSpec(memory_space=pltpu.SMEM)
     return pl.pallas_call(
         rows_down_kernel,
-        out_shape=jax.ShapeDtypeStruct((ROWS, V), F32),
-        in_specs=[smem, hbm, hbm, hbm] + [vmem] * 6,
+        out_shape=pltpu.HBM((ROWS, V), F32),
+        in_specs=[smem] + [hbm] * 6 + [vmem] * len(rest),
         out_specs=hbm,
         scratch_shapes=[
             pltpu.SMEM((ROWS,), jnp.int32),
             pltpu.SMEM((1, NL), jnp.int32),
+            pltpu.VMEM((NL, LEAF, R), F32),
             pltpu.VMEM((NL, LEAF, V), F32),
+            pltpu.VMEM((NL, R, V), F32),
+            pltpu.VMEM((NL, R, R), F32),
             pltpu.VMEM((LEAF * S, 128), F32),
             pltpu.VMEM((ROWS * S, 128), F32),
             pltpu.VMEM((ROWS, V), F32),
             pltpu.VMEM((V, R), F32),
-            pltpu.SemaphoreType.DMA((2,)),
+            pltpu.SemaphoreType.DMA((5,)),
             pltpu.SemaphoreType.DMA((NL,)),
             pltpu.SemaphoreType.DMA((NL,)),
         ],
-        compiler_params=pltpu.CompilerParams(vmem_limit_bytes=48 * MIB),
+        compiler_params=pltpu.CompilerParams(vmem_limit_bytes=36 * MIB),
         cost_estimate=pl.CostEstimate(flops=2 * 10**9, bytes_accessed=16 * 10**6, transcendentals=0),
         name="rows_down",
-    )(me, slot, sizes, part, eh, el, own, other, got, m0)
+    )(me, far(slot), far(sizes), far(basis), far(part), far(local), far(tmat), *rest)
 
 
 def groups_of(bits, count):
@@ -522,9 +563,19 @@
     trans, coup, upper, pairs = (
         local_transfer[0], local_coupling[0], upper_transfer[0], pair_coupling[0],
     )
-    a1, a2, m0, m1, m3 = small(
-        chains_kernel, [(R, 2 * R), (R, 3 * R), (2 * R, R), (3 * R, R), (4 * R, R)], "chains", 10**8
-    )(me, trans[2 * NL - 2 :], upper, pairs)
+    a1, a2, m0, m1, m3, side2 = small(
+        chains_kernel,
+        [(R, 2 * R), (R, 3 * R), (2 * R, R), (3 * R, R), (4 * R, R), (R, R)],
+        "chains",
+        10**8,
+        [
+            pltpu.VMEM((1, R, R), F32),
+            pltpu.VMEM((5, R, R), F32),
+            pltpu.VMEM((7, R, R), F32),
+            pltpu.SemaphoreType.DMA((3,)),
+        ],
+        (1, 2, 3),
+    )(me, far(trans), far(upper), far(pairs))
     xh, xl, call, pay = rows_up(slot_frame, leaf_sizes, vectors, leaf_basis, trans)
     core_got = swap(pay, 0)
     pair2, lift3 = small(after_core_kernel, [(2, HALF, R), (HALF, R)], "after_core", 10**8)(
@@ -538,24 +589,24 @@
     top_got = exchange(top_send, (3, 4, 5, 6))
     (c2,) = small(after_pair_kernel, [(HALF, R)], "after_pair", 10**6)(pair2, pair_got)
     quad_got = swap(c2, 2)
-    part, eh, el, local = near_local(near_field, xh, xl, leaf_basis, call, trans, coup)
-    (inc3,) = small(after_top_kernel, [(HALF, R)], "after_top", 10**8)(me, top_got, m3)
+    part, local, tmat, curv = near_local(
+        me, near_field, xh, xl, call, trans, coup, pay, core_got, pair2, pair_got, c2, m0, m1
+    )
+    (inc3,) = small(
+        after_top_kernel, [(4, QUART + 8, R)], "after_top", 10**8, [pltpu.VMEM((V, R), F32)]
+    )(me, top_got, m3, side2, c2, quad_got, c3, curv)
     inc3_got = exchange(inc3, (1, 2))
-    (curv,) = small(curvature_kernel, [(128, V)], "curvature", 10**8, [pltpu.VMEM((V, R), F32)])(
-        me, pay, core_got, pair2, pair_got, c2, quad_got, c3, inc3, m0, m1, pairs, local
-    )
-    curv = exchange(curv, (3, 4, 5, 6))
-    (curv,) = small(functools.partial(fold_kernel, 16, 8, 1.0), [(64, V)], "fold_top", 10**5)(curv)
-    curv = exchange(curv, (0, 1, 2))
-    (curv,) = small(
-        functools.partial(fold_kernel, 8, 1, 1.0 / (2.0 * LEAF)), [(8, V)], "fold_low", 10**5
-    )(curv)
-    (inc1,) = small(to_core_kernel, [(HALF, R)], "to_core", 10**8)(inc3_got, pair_got, quad_got, m1)
+    (inc1,) = small(to_core_kernel, [(HALF + 8, R)], "to_core", 10**8)(
+        inc3_got, pair_got, quad_got, m1
+    )
     inc1_got = swap(inc1, 0)
+    (share,) = small(core_share_kernel, [(16, 8, R)], "core_share", 10**5)(inc1, inc1_got)
+    share = exchange(share, (3, 4, 5, 6))
     products = rows_down(
-        me, slot_frame, leaf_sizes, part, eh, el, inc1, inc1_got, core_got, m0
-    )
-    return products, curv[0]
+        me, slot_frame, leaf_sizes, leaf_basis, part, local, tmat, inc1, inc1_got, core_got, m0
+    )
+    (curvature,) = small(all_share_kernel, [(8, R)], "all_share", 10**5)(share)
+    return products, curvature[0:3].reshape(V)
 
 
 def solution(mesh):

time: 125 us -> 96.1 us (0.77)
  local copies, waits for them, and re-layouts: 23.2 us -> 0.58 us
  starting transfers between devices: 33.3 us -> 22.4 us
  blocking collectives: 8.67 us -> 16.1 us
  waiting for transfers between devices: 7.47 us -> 0.96 us
  Pallas kernels: 50.6 us -> 54.6 us
    unnamed x66 -> x0, local copies, waits for them, and re-layouts: 21.8 us -> none
    all_to_all x4 -> x2, starting transfers between devices: 26.6 us -> 14.6 us  [exchange(): lax.all_to_all(value, 'leaf', 0, 0, axis_index_groups=groups_of(bits, cou...]
    all_to_all x1 -> x2, blocking collectives: 8.67 us -> 16.1 us  [exchange(): lax.all_to_all(value, 'leaf', 0, 0, axis_index_groups=groups_of(bits, cou...]
    pallas_call x3, Pallas kernels: 44.6 us -> 50.1 us  [the longest x1 18.4 us: near_local(): pl.pallas_call(near_local_kernel, grid=(NL,), out_shape=(pltpu.HBM((NL, L...]
    ppermute x4, waiting for transfers between devices: 4.35 us -> 0.96 us  [swap(): lax.ppermute(value, 'leaf', [(s, s ^ 1 << level) for s in range(count)])]
    all_to_all x4 -> x2, waiting for transfers between devices: 3.12 us -> 0.01 us  [exchange(): lax.all_to_all(value, 'leaf', 0, 0, axis_index_groups=groups_of(bits, cou...]
    pallas_call x9 -> x8, Pallas kernels: 6.06 us -> 4.53 us  [call(): pl.pallas_call(body, out_shape=tuple((jax.ShapeDtypeStruct(o, F32) for o...]
    slice x2 -> x0, local copies, waits for them, and re-layouts: 1.44 us -> none  [the longest x1 0.84 us: shards(): trans[2 * NL - 2:]]
  transfers between devices with their start and end apart: 8 -> 6, of which waited for: 3 -> 1; matrix products, arithmetic and copies ran while one was open for 1% -> 0% of each run, Pallas kernels for 28% -> 40%
where the time goes in v1:
time: 96.1 us; the launch traced here: 95.4 us
  Pallas kernels  54.6 us (57%)
  starting transfers between devices  22.4 us (23%)
  blocking collectives  16.1 us (17%)
    pallas_call x1, Pallas kernels, near_local(): pl.pallas_call(near_local_kernel, grid=(NL,), out_shape=(pltpu.HBM((NL, L...  18.4 us
    pallas_call x1, Pallas kernels, rows_down(): pl.pallas_call(rows_down_kernel, out_shape=pltpu.HBM((ROWS, V), F32), in_...  16.8 us
    all_to_all x2, blocking collectives, exchange(): lax.all_to_all(value, 'leaf', 0, 0, axis_index_groups=groups_of(bits, cou...  16.1 us
    pallas_call x1, Pallas kernels, rows_up(): pl.pallas_call(rows_up_kernel, out_shape=(pltpu.HBM((NL, LEAF, V), BF16),...  14.8 us
    all_to_all x2, starting transfers between devices, exchange(): lax.all_to_all(value, 'leaf', 0, 0, axis_index_groups=groups_of(bits, cou...  14.6 us
    ppermute x4, starting transfers between devices, swap(): lax.ppermute(value, 'leaf', [(s, s ^ 1 << level) for s in range(count)])  7.81 us
    pallas_call x8, Pallas kernels, call(): pl.pallas_call(body, out_shape=tuple((jax.ShapeDtypeStruct(o, F32) for o...  4.53 us
  transfers between devices with their start and end apart: 6, of which 1 were waited for; matrix products, arithmetic and copies ran while one was open for 0% of the time, Pallas kernels for 40%

profile of v1, /device:TPU:1, one launch (start us, length us, event | category | flops | bytes accessed | tf_op | source)
XLA Modules:
  0.0 95.4 jit_solution(18220715316063475720)
XLA Ops:
  0.6 14.8 %rows_up.1 = (bf16[8,512,384]{2,1,0:T(8,128)(2,1)}, bf16[8,512,384]{2,1,0:T(8,128)(2,1)}, f32[14,128,384]{2,1,0:T(8,128)}, f32[2,384,128]{2,1,0:T(8,128)S(1)}) custom-call(s32[4096]{0:T(1024)} %slot_hbm.3, s32[1,8]{1,0:T(1,128)} %sizes_hbm.3, f32[4096,384]{1,0:T(8,128)} %v_hbm.1, f32[8,512,128]{2,1,0:T(8,128)} %basis_hbm.3, f32[15,128,128]{2,1,0:T(8,128)} %bitcast.14), custom_call_target="tpu_custom_call" | custom-call | flops 2000000000 | bytes 18000000 | tf_op jit(solution)/shard_map/rows_up/pallas_call | solution.py:167
  15.5 1.5 %collective-permute-start = (f32[2,384,128]{2,1,0:T(8,128)S(1)}, f32[2,384,128]{2,1,0:T(8,128)S(1)}, u32[]{:S(2)}, u32[]{:S(2)}) collective-permute-start(f32[2,384,128]{2,1,0:T(8,128)S(1)} %get-tuple-element.23.pay_ref), channel_id=1, source_target_pairs={{0,1},{1,0},{2,3},{3,2},{4,5},{5,4},{6,7},{7,6},{8,9},{9,8},{10,11... | collective-permute-start | bytes 1179656 | tf_op jit(solution)/shard_map/ppermute | solution.py:556
  17.0 1.9 %chains.1 = (f32[128,256]{1,0:T(8,128)S(1)}, f32[128,384]{1,0:T(8,128)S(1)}, f32[256,128]{1,0:T(8,128)S(1)}, f32[384,128]{1,0:T(8,128)S(1)}, f32[512,128]{1,0:T(8,128)S(1)}, /*index=5*/f32[128,128]{1,0:T(8,128)S(1)}) custom-call(s32[1]{0:T(128)} %bitcast.me, f32[15,128,128]{2,1,0:T(8,128)} %bitcast.15, f32[5,128,128]{2,1,0:T(8,128)} %bitcast.18, ...), custom_call_target="tpu_custom_call" | custom-call | flops 100000000 | bytes 1000000 | tf_op jit(solution)/shard_map/chains/pallas_call | solution.py:414
  18.9 0.0 collective-permute-done.got_ref
  18.9 0.2 after_core.1
  19.1 1.5 %collective-permute-start.1 = (f32[2,192,128]{2,1,0:T(8,128)S(1)}, f32[2,192,128]{2,1,0:T(8,128)S(1)}, u32[]{:S(2)}, u32[]{:S(2)}) collective-permute-start(f32[2,192,128]{2,1,0:T(8,128)S(1)} %get-tuple-element.25.pair2_ref), channel_id=1, source_target_pairs={{0,2},{1,3},{2,0},{3,1},{4,6},{5,7},{6,4},{7,5},{8,10},{9,11},{10,... | collective-permute-start | bytes 589832 | tf_op jit(solution)/shard_map/ppermute | solution.py:556
  20.6 8.2 %all_to_all.32 = f32[4,48,128]{2,1,0:T(8,128)S(1)} all-to-all(f32[4,48,128]{2,1,0:T(8,128)S(1)} %bitcast.12), channel_id=1, replica_groups={{0,2,4,6},{1,3,5,7},{8,10,12,14},{9,11,13,15},{16,18,20,22},{17,19,21,2..., dimensions={0} | all-to-all | bytes 196608 | tf_op jit(solution)/shard_map/all_to_all | solution.py:559
  28.8 1.0 %after_y.1 = (f32[768,128]{1,0:T(8,128)}, f32[48,128]{1,0:T(8,128)S(1)}) custom-call(s32[1]{0:T(128)} %bitcast.me, f32[192,128]{1,0:T(8,128)S(1)} %bitcast.13, f32[128,384]{1,0:T(8,128)S(1)} %get-tuple-element.32.a2_ref), custom_call_target="tpu_custom_call" | custom-call | flops 100000000 | bytes 1000000 | tf_op jit(solution)/shard_map/after_y/pallas_call | solution.py:414
  29.8 7.6 %all-to-all-start.1 = ((f32[16,48,128]{2,1,0:T(8,128)}), f32[16,48,128]{2,1,0:T(8,128)S(1)}, u32[]{:S(2)}, u32[]{:S(2)}) async-start(f32[16,48,128]{2,1,0:T(8,128)} %bitcast.7), calls=%async_computation.1 | async-start | bytes 786432 | tf_op jit(solution)/shard_map/all_to_all | solution.py:559
  37.4 0.0 collective-permute-done.1.got_ref.pair_got_ref
  37.5 1.0 %collective-permute-start.2 = (f32[192,128]{1,0:T(8,128)S(1)}, f32[192,128]{1,0:T(8,128)S(1)}, u32[]{:S(2)}, u32[]{:S(2)}) collective-permute-start(f32[192,128]{1,0:T(8,128)S(1)} %after_pair.1.c2_ref), channel_id=1, source_target_pairs={{0,4},{1,5},{2,6},{3,7},{4,0},{5,1},{6,2},{7,3},{8,12},{9,13},{10,... | collective-permute-start | bytes 294920 | tf_op jit(solution)/shard_map/ppermute | solution.py:556
  38.5 18.4 %near_local.1 = (f32[8,512,384]{2,1,0:T(8,128)}, f32[8,128,384]{2,1,0:T(8,128)}, f32[8,128,128]{2,1,0:T(8,128)}, f32[8,384]{1,0:T(8,128)S(1)}) custom-call(s32[1]{0:T(128)} %bitcast.me, f32[8,512,512]{2,1,0:T(8,128)} %near_ref.1, bf16[8,512,384]{2,1,0:T(8,128)(2,1)} %get-tuple-element.20.xh_ref, bf16[8,512,384]{2,1,0:T(8,128)(2,1)} %get-tuple-element.21.xl_ref, ...), custom_call_target="tpu_custom_call" | custom-call | flops 7000000000 | bytes 10000000 | tf_op jit(solution)/shard_map/near_local/pallas_call | solution.py:265
  56.9 0.0 collective-permute-done.2.quad_got_ref
  56.9 0.0 all-to-all-done.1
  56.9 0.6 after_top.1
  57.5 7.9 %all_to_all.33.got_ref = f32[4,56,128]{2,1,0:T(8,128)S(1)} all-to-all(f32[4,56,128]{2,1,0:T(8,128)S(1)} %after_top.1), channel_id=1, replica_groups={{0,2,4,6},{1,3,5,7},{8,10,12,14},{9,11,13,15},{16,18,20,22},{17,19,21,2..., dimensions={0} | all-to-all | bytes 229376 | tf_op jit(solution)/shard_map/all_to_all | solution.py:559
  65.4 0.3 to_core.1.own_ref
  65.7 3.8 %collective-permute-start.3 = (f32[200,128]{1,0:T(8,128)S(1)}, f32[200,128]{1,0:T(8,128)S(1)}, u32[]{:S(2)}, u32[]{:S(2)}) collective-permute-start(f32[200,128]{1,0:T(8,128)S(1)} %to_core.1.own_ref), channel_id=1, source_target_pairs={{0,1},{1,0},{2,3},{3,2},{4,5},{5,4},{6,7},{7,6},{8,9},{9,8},{10,11... | collective-permute-start | bytes 307208 | tf_op jit(solution)/shard_map/ppermute | solution.py:556
  69.5 0.9 collective-permute-done.3.other_ref
  70.4 0.6 core_share.1
  71.1 6.9 %all-to-all-start.3 = ((f32[16,8,128]{2,1,0:T(8,128)}), f32[16,8,128]{2,1,0:T(8,128)S(1)}, u32[]{:S(2)}, u32[]{:S(2)}) async-start(f32[16,8,128]{2,1,0:T(8,128)} %core_share.1), calls=%async_computation.3 | async-start | bytes 131072 | tf_op jit(solution)/shard_map/all_to_all | solution.py:559
  78.0 16.8 %rows_down.1 = f32[4096,384]{1,0:T(8,128)} custom-call(s32[1]{0:T(128)} %bitcast.me, s32[4096]{0:T(1024)} %slot_hbm.3, s32[1,8]{1,0:T(1,128)} %sizes_hbm.3, f32[8,512,128]{2,1,0:T(8,128)} %basis_hbm.3, f32[8,512,384]{2,1,0:T(8,128)} %get-tuple-element.28.part_hbm, f32[8,128,384]{2,1,0:T(8,128)} %get-tuple-element.29.local_hbm, ...), custom_call_target="tpu_custom_call" | custom-call | flops 2000000000 | bytes 16000000 | tf_op jit(solution)/shard_map/rows_down/pallas_call | solution.py:516
  94.8 0.0 all-to-all-done.3.got_ref
  94.9 0.6 slice_bitcast_fusion
  (2 shorter events, 0.0 us)
Async XLA Ops:
  15.5 3.4 %collective-permute-start = (f32[2,384,128]{2,1,0:T(8,128)S(1)}, f32[2,384,128]{2,1,0:T(8,128)S(1)}, u32[]{:S(2)}, u32[]{:S(2)}) collective-permute-start(f32[2,384,128]{2,1,0:T(8,128)S(1)} %get-tuple-element.23.pay_ref), channel_id=1, source_target_pairs={{0,1},{1,0},{2,3},{3,2},{4,5},{5,4},{6,7},{7,6},{8,9},{9,8},{10,11... | collective-permute-start | bytes 1179656 | tf_op jit(solution)/shard_map/ppermute | solution.py:556
  19.1 18.4 %collective-permute-start.1 = (f32[2,192,128]{2,1,0:T(8,128)S(1)}, f32[2,192,128]{2,1,0:T(8,128)S(1)}, u32[]{:S(2)}, u32[]{:S(2)}) collective-permute-start(f32[2,192,128]{2,1,0:T(8,128)S(1)} %get-tuple-element.25.pair2_ref), channel_id=1, source_target_pairs={{0,2},{1,3},{2,0},{3,1},{4,6},{5,7},{6,4},{7,5},{8,10},{9,11},{10,... | collective-permute-start | bytes 589832 | tf_op jit(solution)/shard_map/ppermute | solution.py:556
  29.8 27.1 %all-to-all-start.1 = ((f32[16,48,128]{2,1,0:T(8,128)}), f32[16,48,128]{2,1,0:T(8,128)S(1)}, u32[]{:S(2)}, u32[]{:S(2)}) async-start(f32[16,48,128]{2,1,0:T(8,128)} %bitcast.7), calls=%async_computation.1 | async-start | bytes 786432 | tf_op jit(solution)/shard_map/all_to_all | solution.py:559
  37.5 19.5 %collective-permute-start.2 = (f32[192,128]{1,0:T(8,128)S(1)}, f32[192,128]{1,0:T(8,128)S(1)}, u32[]{:S(2)}, u32[]{:S(2)}) collective-permute-start(f32[192,128]{1,0:T(8,128)S(1)} %after_pair.1.c2_ref), channel_id=1, source_target_pairs={{0,4},{1,5},{2,6},{3,7},{4,0},{5,1},{6,2},{7,3},{8,12},{9,13},{10,... | collective-permute-start | bytes 294920 | tf_op jit(solution)/shard_map/ppermute | solution.py:556
  65.7 4.8 %collective-permute-start.3 = (f32[200,128]{1,0:T(8,128)S(1)}, f32[200,128]{1,0:T(8,128)S(1)}, u32[]{:S(2)}, u32[]{:S(2)}) collective-permute-start(f32[200,128]{1,0:T(8,128)S(1)} %to_core.1.own_ref), channel_id=1, source_target_pairs={{0,1},{1,0},{2,3},{3,2},{4,5},{5,4},{6,7},{7,6},{8,9},{9,8},{10,11... | collective-permute-start | bytes 307208 | tf_op jit(solution)/shard_map/ppermute | solution.py:556
  71.1 23.8 %all-to-all-start.3 = ((f32[16,8,128]{2,1,0:T(8,128)}), f32[16,8,128]{2,1,0:T(8,128)S(1)}, u32[]{:S(2)}, u32[]{:S(2)}) async-start(f32[16,8,128]{2,1,0:T(8,128)} %core_share.1), calls=%async_computation.3 | async-start | bytes 131072 | tf_op jit(solution)/shard_map/all_to_all | solution.py:559

commit v2 on v1

v2 whole, which is shorter than its diff:
```python
import functools

import jax
import jax.numpy as jnp
from jax import lax
from jax.experimental import pallas as pl
from jax.experimental.pallas import tpu as pltpu
from jax.sharding import PartitionSpec as P

LEAF = 512
NL = 8
R = 128
V = 384
HALF = V // 2
QUART = HALF // 4
SHARE = 64
ROWS = NL * LEAF
S = 4
MB = 256
UN = 32
F32 = jnp.float32
BF16 = jnp.bfloat16
MIB = 1 << 20


def split(a):
    hi = a.astype(BF16)
    return hi, (a - hi.astype(F32)).astype(BF16)


def dot3s(terms, ca, cb):
    lhs, rhs = [], []
    for (ah, al), (bh, bl) in terms:
        lhs += [ah, ah, al]
        rhs += [bh, bl, bh]
    return lax.dot_general(
        jnp.concatenate(lhs, axis=ca),
        jnp.concatenate(rhs, axis=cb),
        (((ca,), (cb,)), ((), ())),
        preferred_element_type=F32,
    )


def dot3(a, b, ca=1, cb=0):
    return dot3s([(split(a), split(b))], ca, cb)


def tile_rows(start, count):
    return pl.ds(pl.multiple_of(start * S, S), count * S)


def far(x):
    return pltpu.with_memory_space_constraint(x, pltpu.HBM)


def lane_rows(p):
    parts = [p[0:1, 128 * k : 128 * k + 128] for k in range(3)]
    return jnp.concatenate(parts + [jnp.zeros((5, 128), F32)], axis=0)


def row_sums(z):
    zh, zl = split(z)
    ones = jnp.ones((8, 2 * R), BF16)
    return lax.dot_general(
        ones, jnp.concatenate([zh, zl], axis=1), (((1,), (1,)), ((), ())),
        preferred_element_type=F32,
    )


def rows_up_kernel(
    slot_hbm, sizes_hbm, v_hbm, basis_hbm, trans_hbm, near_hbm,
    part_hbm, call_hbm, pay_ref, curv_ref,
    slot, sizes, vbuf, vt, xt, basis, trans, near, xh, xl, call_ref,
    sem, vsem, nsem, osem,
):
    copies = [
        pltpu.make_async_copy(slot_hbm, slot, sem.at[0]),
        pltpu.make_async_copy(sizes_hbm, sizes, sem.at[1]),
        pltpu.make_async_copy(basis_hbm, basis, sem.at[2]),
        pltpu.make_async_copy(trans_hbm, trans, sem.at[3]),
    ]
    chunks = [
        pltpu.make_async_copy(
            v_hbm.at[pl.ds(c * LEAF, LEAF)], vbuf.at[pl.ds(c * LEAF, LEAF)], vsem.at[c]
        )
        for c in range(NL)
    ]
    copies[0].start()
    copies[1].start()
    for c in range(NL):
        chunks[c].start()
    nears = [
        pltpu.make_async_copy(near_hbm.at[leaf], near.at[leaf], nsem.at[leaf]) for leaf in range(NL)
    ]
    for c in range(NL):
        chunks[c].wait()
        if c == NL - 2:
            copies[2].start()
            for n in nears:
                n.start()
            copies[3].start()

        def spread(i, _, c=c):
            for u in range(8):
                base = pl.multiple_of(c * LEAF + i * 64 + u * 8, 8)
                for k in range(3):
                    vt[pl.ds(pl.multiple_of(base * S, 8) + k, 8, stride=S), :] = vbuf[
                        pl.ds(base, 8), 128 * k : 128 * k + 128
                    ]
            return 0

        lax.fori_loop(0, LEAF // 64, spread, 0)
    copies[0].wait()
    copies[1].wait()
    for leaf in range(NL):

        def pick(i, _, leaf=leaf):
            base = pl.multiple_of(leaf * LEAF + i * UN, UN)
            rows = [vt[tile_rows(slot[base + r], 1), :] for r in range(UN)]
            for r in range(UN):
                xt[tile_rows(base + r, 1), :] = rows[r]
            return 0

        lax.fori_loop(0, (sizes[0, leaf] + UN - 1) // UN, pick, 0)
    copies[2].wait()
    for c in nears[0:4]:
        c.wait()
    lane_row = lax.broadcasted_iota(jnp.int32, (8, 128), 0)

    def pack(leaf, first=0, last=LEAF):
        size = sizes[0, leaf]
        for base in range(first, last, 16):
            for k in range(3):
                pieces = []
                for half in (0, 8):
                    val = xt[pl.ds((leaf * LEAF + base + half) * S + k, 8, stride=S), :]
                    pieces.append(jnp.where(lane_row < size - (base + half), val, 0.0))
                hi, lo = split(jnp.concatenate(pieces, axis=0))
                xh[leaf, base : base + 16, 128 * k : 128 * k + 128] = hi
                xl[leaf, base : base + 16, 128 * k : 128 * k + 128] = lo

    outs = []
    coeffs = []
    total = jnp.zeros((1, V), F32)
    pack(0)
    for leaf in range(NL):
        x = (xh[leaf], xl[leaf])
        c = dot3s([(split(basis[leaf]), x)], 0, 0)
        call_ref[leaf] = c
        coeffs.append(split(c))
        for blk in range(LEAF // MB):
            rows = slice(MB * blk, MB * blk + MB)
            prod = dot3s([(split(near[leaf, rows, :]), x)], 1, 0)
            xb = xh[leaf, rows, :].astype(F32) + xl[leaf, rows, :].astype(F32)
            total += jnp.sum(prod * xb, axis=0, keepdims=True)
            vbuf[leaf * LEAF + MB * blk : leaf * LEAF + MB * blk + MB, :] = prod
            if leaf + 1 < NL:
                pack(leaf + 1, MB * blk, MB * blk + MB)
        if leaf % 4 == 3:
            for n in range(leaf - 3, leaf + 1):
                cp = pltpu.make_async_copy(
                    vbuf.at[pl.ds(n * LEAF, LEAF)], part_hbm.at[n], osem.at[n]
                )
                cp.start()
                outs.append(cp)
        if leaf == 3:
            for cp in nears[4:]:
                cp.wait()
    copies[3].wait()
    offset, at = 0, NL
    while len(coeffs) > 1:
        parents = []
        for m in range(len(coeffs) // 2):
            terms = [(split(trans[offset + 2 * m + t]), coeffs[2 * m + t]) for t in range(2)]
            c = dot3s(terms, 0, 0)
            parents.append(c)
            if len(coeffs) > 2:
                call_ref[at] = c
                at += 1
        offset += len(coeffs)
        coeffs = [split(c) for c in parents]
    cp = pltpu.make_async_copy(call_ref, call_hbm, osem.at[NL])
    cp.start()
    outs.append(cp)
    curv_ref[...] = jnp.broadcast_to(total, (8, V))
    pay_ref[0] = parents[0].T
    pay_ref[1] = dot3s([(coeffs[0], split(trans[2 * NL - 2]))], 0, 0)
    for cp in outs:
        cp.wait()


def rows_up(slot, sizes, vectors, basis, trans, near):
    hbm = pl.BlockSpec(memory_space=pltpu.HBM)
    vmem = pl.BlockSpec(memory_space=pltpu.VMEM)
    return pl.pallas_call(
        rows_up_kernel,
        out_shape=(
            pltpu.HBM((NL, LEAF, V), F32),
            pltpu.HBM((14, R, V), F32),
            jax.ShapeDtypeStruct((2, V, R), F32),
            jax.ShapeDtypeStruct((8, V), F32),
        ),
        in_specs=[hbm] * 6,
        out_specs=(hbm, hbm, vmem, vmem),
        scratch_shapes=[
            pltpu.SMEM((ROWS,), jnp.int32),
            pltpu.SMEM((1, NL), jnp.int32),
            pltpu.VMEM((ROWS, V), F32),
            pltpu.VMEM((ROWS * S, 128), F32),
            pltpu.VMEM((ROWS * S, 128), F32),
            pltpu.VMEM((NL, LEAF, R), F32),
            pltpu.VMEM((2 * NL - 1, R, R), F32),
            pltpu.VMEM((NL, LEAF, LEAF), F32),
            pltpu.VMEM((NL, LEAF, V), BF16),
            pltpu.VMEM((NL, LEAF, V), BF16),
            pltpu.VMEM((14, R, V), F32),
            pltpu.SemaphoreType.DMA((4,)),
            pltpu.SemaphoreType.DMA((NL,)),
            pltpu.SemaphoreType.DMA((NL,)),
            pltpu.SemaphoreType.DMA((NL + 1,)),
        ],
        compiler_params=pltpu.CompilerParams(vmem_limit_bytes=50 * MIB),
        cost_estimate=pl.CostEstimate(flops=7 * 10**9, bytes_accessed=28 * 10**6, transcendentals=0),
        name="rows_up",
    )(far(slot), far(sizes), far(vectors), far(basis), far(trans), far(near))


def fields_kernel(
    me, call_hbm, trans_hbm, coup_hbm,
    pay_ref, got_ref, pair2_ref, pair_got_ref, c2_ref, m0_ref, m1_ref, near_ref,
    inc_ref, tmat_ref, curv_ref, call_ref, trans_ref, coup_ref, z, sem,
):
    copies = [
        pltpu.make_async_copy(call_hbm, call_ref, sem.at[0]),
        pltpu.make_async_copy(trans_hbm, trans_ref, sem.at[1]),
        pltpu.make_async_copy(coup_hbm, coup_ref, sem.at[2]),
    ]
    for c in copies:
        c.start()
    z[...] = pay_ref[0] * dot3(got_ref[0], m0_ref[0:R])
    start = pl.multiple_of((me[0] % 2) * HALF, HALF)
    z[pl.ds(start, HALF), :] += pair2_ref[0] * dot3(pair_got_ref[0], m1_ref[0:R])
    for c in copies:
        c.wait()
    total = jnp.zeros((1, V), F32)
    starts = (0, 8, 12)
    fields = [None] * 14
    pair = 0
    for height in range(3):
        for m in range(4 >> height):
            a = starts[height] + 2 * m
            bm = split(coup_ref[pair])
            ca, cb = call_ref[a], call_ref[a + 1]
            fields[a] = dot3s([(bm, split(cb))], 1, 0)
            fields[a + 1] = dot3s([(bm, split(ca))], 0, 0)
            total += 2.0 * jnp.sum(ca * fields[a], axis=0, keepdims=True)
            pair += 1
    curv_ref[...] = near_ref[...] + row_sums(z[...]) + jnp.broadcast_to(total, (8, V))
    top = [split(fields[12 + m]) for m in range(2)]
    tops = [split(trans_ref[12 + m]) for m in range(2)]
    for m in range(4):
        w = split(trans_ref[8 + m])
        mid = split(fields[8 + m] + dot3s([(w, top[m // 2])], 1, 0))
        tmid = split(dot3s([(w, tops[m // 2])], 1, 0))
        for n in (2 * m, 2 * m + 1):
            wl = split(trans_ref[n])
            inc_ref[n] = fields[n] + dot3s([(wl, mid)], 1, 0)
            tmat_ref[n] = dot3s([(wl, tmid)], 1, 0)


def fields(me, call, trans, coup, *rest):
    vmem = pl.BlockSpec(memory_space=pltpu.VMEM)
    hbm = pl.BlockSpec(memory_space=pltpu.HBM)
    smem = pl.BlockSpec(memory_space=pltpu.SMEM)
    return pl.pallas_call(
        fields_kernel,
        out_shape=(
            pltpu.HBM((NL, R, V), F32),
            pltpu.HBM((NL, R, R), F32),
            jax.ShapeDtypeStruct((8, V), F32),
        ),
        in_specs=[smem, hbm, hbm, hbm] + [vmem] * len(rest),
        out_specs=(vmem, vmem, vmem),
        scratch_shapes=[
            pltpu.VMEM((14, R, V), F32),
            pltpu.VMEM((2 * NL - 1, R, R), F32),
            pltpu.VMEM((NL - 1, R, R), F32),
            pltpu.VMEM((V, R), F32),
            pltpu.SemaphoreType.DMA((3,)),
        ],
        compiler_params=pltpu.CompilerParams(vmem_limit_bytes=24 * MIB),
        cost_estimate=pl.CostEstimate(flops=2 * 10**9, bytes_accessed=8 * 10**6, transcendentals=0),
        name="fields",
    )(me, far(call), far(trans), far(coup), *rest)


def chains_kernel(
    me, trans_hbm, upper_hbm, pair_hbm, a1_ref, a2_ref, m0_ref, m1_ref, m3_ref, side2_ref,
    trans_ref, upper_ref, pair_ref, sem,
):
    dev = me[0]
    copies = [
        pltpu.make_async_copy(trans_hbm.at[pl.ds(2 * NL - 2, 1)], trans_ref, sem.at[0]),
        pltpu.make_async_copy(upper_hbm, upper_ref, sem.at[1]),
        pltpu.make_async_copy(pair_hbm, pair_ref, sem.at[2]),
    ]
    for c in copies:
        c.start()
    for c in copies:
        c.wait()

    def side(level):
        b = pair_ref[level]
        return jnp.where((dev >> level) % 2 == 0, b, b.T)

    m0_ref[0:R] = side(0).T
    m0_ref[R : 2 * R] = trans_ref[0].T
    w1 = upper_ref[0]
    w12 = dot3(w1, upper_ref[1])
    a1_ref[:, 0:R] = w1
    a1_ref[:, R : 2 * R] = w12
    m1_ref[0:R] = side(1).T
    m1_ref[R : 2 * R] = dot3(w1, side(2)).T
    m1_ref[2 * R : 3 * R] = w12.T
    w3 = upper_ref[2]
    w34 = dot3(w3, upper_ref[3])
    w345 = dot3(w34, upper_ref[4])
    a2_ref[:, 0:R] = w3
    a2_ref[:, R : 2 * R] = w34
    a2_ref[:, 2 * R : 3 * R] = w345
    m3_ref[0:R] = side(3).T
    m3_ref[R : 2 * R] = dot3(w3, side(4)).T
    m3_ref[2 * R : 3 * R] = dot3(w34, side(5)).T
    m3_ref[3 * R : 4 * R] = dot3(w345, side(6)).T
    side2_ref[...] = side(2).T


def after_core_kernel(me, pay_ref, got_ref, a1_ref, pair2_ref, lift3_ref):
    start = pl.multiple_of((me[0] % 2) * HALF, HALF)
    c1 = pay_ref[1, pl.ds(start, HALF), :] + got_ref[1, pl.ds(start, HALF), :]
    x = dot3(c1, a1_ref[...])
    pair2_ref[0] = c1
    pair2_ref[1] = x[:, 0:R]
    lift3_ref[...] = x[:, R : 2 * R]


def after_y_kernel(me, got_ref, a2_ref, send_ref, c3_ref):
    c3 = got_ref[0:QUART]
    for n in range(1, 4):
        c3 = c3 + got_ref[n * QUART : (n + 1) * QUART]
    c3_ref[...] = c3
    x = dot3(c3, a2_ref[...])
    parts = [c3, x[:, 0:R], x[:, R : 2 * R], x[:, 2 * R : 3 * R]]
    group = me[0] // 8
    for s in range(16):
        d = jnp.bitwise_xor(group, s)
        send_ref[s * QUART : (s + 1) * QUART] = jnp.where(
            d >= 8, parts[3], jnp.where(d >= 4, parts[2], jnp.where(d >= 2, parts[1], parts[0]))
        )


def after_top_kernel(
    me, got_ref, m3_ref, side2_ref, c2_ref, quad_got_ref, c3_ref, local_ref, send_ref, share_ref, z
):
    dev = me[0]
    group = dev // 8
    sums = [jnp.zeros((QUART, R), F32) for _ in range(4)]
    bounds = ((1, 2), (2, 4), (4, 8), (8, 16))
    for s in range(16):
        d = jnp.bitwise_xor(group, s)
        val = got_ref[s * QUART : (s + 1) * QUART]
        for j, (low, high) in enumerate(bounds):
            sums[j] += jnp.where(jnp.logical_and(d >= low, d < high), val, 0.0)
    inc3 = dot3(jnp.concatenate(sums, axis=1), m3_ref[...])
    z[...] = jnp.zeros((V, R), F32)
    start = pl.multiple_of((dev % 2) * HALF, HALF)
    z[pl.ds(start, HALF), :] = 0.5 * (c2_ref[...] * dot3(quad_got_ref[...], side2_ref[...]))
    at = pl.multiple_of(start + ((dev // 2) % 4) * QUART, QUART)
    z[pl.ds(at, QUART), :] += c3_ref[...] * inc3
    share = lane_rows(local_ref[...] + row_sums(z[...]))
    for n in range(4):
        send_ref[n * QUART : (n + 1) * QUART] = inc3
    for n in range(SHARE // 8):
        share_ref[8 * n : 8 * n + 8] = share


def after_pair_kernel(pair2_ref, got_ref, c2_ref):
    c2_ref[...] = pair2_ref[1] + got_ref[1]


def to_core_kernel(got_ref, pair_got_ref, quad_got_ref, m1_ref, out_ref):
    sums = jnp.concatenate([pair_got_ref[0], quad_got_ref[...], got_ref[...]], axis=1)
    out_ref[...] = dot3(sums, m1_ref[...])


def all_share_kernel(got_hbm, out_ref, got, sem):
    cp = pltpu.make_async_copy(got_hbm.at[:, pl.ds(0, 8)], got, sem)
    cp.start()
    cp.wait()
    out_ref[...] = jnp.sum(got[...], axis=0) * (1.0 / (2.0 * LEAF))


def small(body, outs, name, flops, scratch=(), hbm_args=()):
    vmem = pl.BlockSpec(memory_space=pltpu.VMEM)
    smem = pl.BlockSpec(memory_space=pltpu.SMEM)
    hbm = pl.BlockSpec(memory_space=pltpu.HBM)

    def call(*args):
        return pl.pallas_call(
            body,
            out_shape=tuple(jax.ShapeDtypeStruct(o, F32) for o in outs),
            in_specs=[
                smem if a.dtype == jnp.int32 else (hbm if n in hbm_args else vmem)
                for n, a in enumerate(args)
            ],
            out_specs=tuple(vmem for _ in outs),
            scratch_shapes=list(scratch),
            compiler_params=pltpu.CompilerParams(vmem_limit_bytes=16 * MIB),
            cost_estimate=pl.CostEstimate(flops=flops, bytes_accessed=10**6, transcendentals=0),
            name=name,
        )(*args)

    return call


def rows_down_kernel(
    me, slot_hbm, sizes_hbm, basis_hbm, part_hbm, local_hbm, tmat_hbm,
    own_ref, other_ref, got_ref, m0_ref, out_hbm,
    slot, sizes, basis, part, local_ref, tmat_ref, ot, pt, res, inct, sem, psem, osem,
):
    copies = [
        pltpu.make_async_copy(slot_hbm, slot, sem.at[0]),
        pltpu.make_async_copy(sizes_hbm, sizes, sem.at[1]),
        pltpu.make_async_copy(tmat_hbm, tmat_ref, sem.at[2]),
        pltpu.make_async_copy(local_hbm, local_ref, sem.at[3]),
        pltpu.make_async_copy(basis_hbm, basis, sem.at[4]),
    ]
    for c in copies:
        c.start()
    loads = [
        pltpu.make_async_copy(part_hbm.at[leaf], part.at[leaf], psem.at[leaf]) for leaf in range(NL)
    ]
    for c in loads:
        c.start()
    half = me[0] % 2
    inct[pl.ds(pl.multiple_of(half * HALF, HALF), HALF), :] = own_ref[...]
    inct[pl.ds(pl.multiple_of((1 - half) * HALF, HALF), HALF), :] = other_ref[...]
    root = dot3(jnp.concatenate([got_ref[0], inct[...]], axis=1), m0_ref[...])
    rsplit = split(root.T)
    for c in copies:
        c.wait()
    incs = [
        split(local_ref[leaf] + dot3s([(split(tmat_ref[leaf]), rsplit)], 1, 0)) for leaf in range(NL)
    ]
    for c in loads:
        c.wait()
    lane_row = lax.broadcasted_iota(jnp.int32, (8, 128), 0)
    for leaf in range(NL):
        size = sizes[0, leaf]
        for blk in range(LEAF // 128):
            rows = slice(128 * blk, 128 * blk + 128)
            val = part[leaf, rows, :] + dot3s([(split(basis[leaf, rows, :]), incs[leaf])], 1, 0)
            for b in range(16):
                keep = lane_row < size - (128 * blk + 8 * b)
                for k in range(3):
                    ot[pl.ds((leaf * LEAF + 128 * blk + 8 * b) * S + k, 8, stride=S), :] = jnp.where(
                        keep, val[8 * b : 8 * b + 8, 128 * k : 128 * k + 128], 0.0
                    )
    zero = jnp.zeros((S, 128), F32)
    for leaf in range(NL):
        steps = (sizes[0, leaf] + UN - 1) // UN

        def place(i, _, leaf=leaf):
            base = pl.multiple_of(leaf * LEAF + i * UN, UN)
            rows = [ot[tile_rows(base + r, 1), :] for r in range(UN)]
            for r in range(UN):
                pt[tile_rows(slot[base + r], 1), :] = rows[r]
            return 0

        lax.fori_loop(0, steps, place, 0)

        def blank(i, _, leaf=leaf):
            base = pl.multiple_of(leaf * LEAF + i * UN, UN)
            for r in range(UN):
                pt[tile_rows(slot[base + r], 1), :] = zero
            return 0

        lax.fori_loop(steps, LEAF // UN, blank, 0)
    stores = []
    for c in range(NL):

        def flat(i, _, c=c):
            for u in range(16):
                base = pl.multiple_of(c * LEAF + i * 128 + u * 8, 8)
                for k in range(3):
                    res[pl.ds(base, 8), 128 * k : 128 * k + 128] = pt[
                        pl.ds(pl.multiple_of(base * S, 8) + k, 8, stride=S), :
                    ]
            return 0

        lax.fori_loop(0, LEAF // 128, flat, 0)
        cp = pltpu.make_async_copy(
            res.at[pl.ds(c * LEAF, LEAF)], out_hbm.at[pl.ds(c * LEAF, LEAF)], osem.at[c]
        )
        cp.start()
        stores.append(cp)
    for cp in stores:
        cp.wait()


def rows_down(me, slot, sizes, basis, part, local, tmat, *rest):
    hbm = pl.BlockSpec(memory_space=pltpu.HBM)
    vmem = pl.BlockSpec(memory_space=pltpu.VMEM)
    smem = pl.BlockSpec(memory_space=pltpu.SMEM)
    return pl.pallas_call(
        rows_down_kernel,
        out_shape=pltpu.HBM((ROWS, V), F32),
        in_specs=[smem] + [hbm] * 6 + [vmem] * len(rest),
        out_specs=hbm,
        scratch_shapes=[
            pltpu.SMEM((ROWS,), jnp.int32),
            pltpu.SMEM((1, NL), jnp.int32),
            pltpu.VMEM((NL, LEAF, R), F32),
            pltpu.VMEM((NL, LEAF, V), F32),
            pltpu.VMEM((NL, R, V), F32),
            pltpu.VMEM((NL, R, R), F32),
            pltpu.VMEM((ROWS * S, 128), F32),
            pltpu.VMEM((ROWS * S, 128), F32),
            pltpu.VMEM((ROWS, V), F32),
            pltpu.VMEM((V, R), F32),
            pltpu.SemaphoreType.DMA((5,)),
            pltpu.SemaphoreType.DMA((NL,)),
            pltpu.SemaphoreType.DMA((NL,)),
        ],
        compiler_params=pltpu.CompilerParams(vmem_limit_bytes=44 * MIB),
        cost_estimate=pl.CostEstimate(flops=2 * 10**9, bytes_accessed=16 * 10**6, transcendentals=0),
        name="rows_down",
    )(me, far(slot), far(sizes), far(basis), far(part), far(local), far(tmat), *rest)


def groups_of(bits, count):
    masks = [sum(1 << b for i, b in enumerate(bits) if k >> i & 1) for k in range(1 << len(bits))]
    full = masks[-1]
    return [[base | m for m in masks] for base in range(count) if base & full == 0]


def shards(
    vectors, slot_frame, leaf_sizes, near_field, leaf_basis,
    local_transfer, local_coupling, upper_transfer, pair_coupling,
):
    count = lax.axis_size("leaf")
    me = lax.axis_index("leaf").astype(jnp.int32).reshape(1)

    def swap(value, level):
        return lax.ppermute(value, "leaf", [(s, s ^ (1 << level)) for s in range(count)])

    def exchange(value, bits):
        return lax.all_to_all(
            value, "leaf", 0, 0, axis_index_groups=groups_of(bits, count), tiled=True
        )

    trans, coup, upper, pairs = (
        local_transfer[0], local_coupling[0], upper_transfer[0], pair_coupling[0],
    )
    a1, a2, m0, m1, m3, side2 = small(
        chains_kernel,
        [(R, 2 * R), (R, 3 * R), (2 * R, R), (3 * R, R), (4 * R, R), (R, R)],
        "chains",
        10**8,
        [
            pltpu.VMEM((1, R, R), F32),
            pltpu.VMEM((5, R, R), F32),
            pltpu.VMEM((7, R, R), F32),
            pltpu.SemaphoreType.DMA((3,)),
        ],
        (1, 2, 3),
    )(me, far(trans), far(upper), far(pairs))
    part, call, pay, curv = rows_up(
        slot_frame, leaf_sizes, vectors, leaf_basis, trans, near_field
    )
    core_got = swap(pay, 0)
    pair2, lift3 = small(after_core_kernel, [(2, HALF, R), (HALF, R)], "after_core", 10**8)(
        me, pay, core_got, a1
    )
    y_got = exchange(lift3, (1, 2))
    pair_got = swap(pair2, 1)
    top_send, c3 = small(after_y_kernel, [(16 * QUART, R), (QUART, R)], "after_y", 10**8)(
        me, y_got, a2
    )
    top_got = exchange(top_send, (3, 4, 5, 6))
    (c2,) = small(after_pair_kernel, [(HALF, R)], "after_pair", 10**6)(pair2, pair_got)
    quad_got = swap(c2, 2)
    local, tmat, curv = fields(
        me, call, trans, coup, pay, core_got, pair2, pair_got, c2, m0, m1, curv
    )
    inc3, share = small(
        after_top_kernel, [(HALF, R), (SHARE, R)], "after_top", 10**8, [pltpu.VMEM((V, R), F32)]
    )(me, top_got, m3, side2, c2, quad_got, c3, curv)
    inc3_got = exchange(inc3, (1, 2))
    (inc1,) = small(to_core_kernel, [(HALF, R)], "to_core", 10**8)(
        inc3_got, pair_got, quad_got, m1
    )
    inc1_got = swap(inc1, 0)
    share = lax.all_gather(share, "leaf")
    products = rows_down(
        me, slot_frame, leaf_sizes, leaf_basis, part, local, tmat, inc1, inc1_got, core_got, m0
    )
    (curvature,) = small(
        all_share_kernel, [(8, R)], "all_share", 10**5,
        [pltpu.VMEM((count, 8, R), F32), pltpu.SemaphoreType.DMA], (0,),
    )(far(share))
    return products, curvature[0:3].reshape(V)


def solution(mesh):
    return jax.shard_map(
        shards,
        mesh=mesh,
        in_specs=(
            P("leaf", None),
            P("leaf"),
            P("leaf", None),
            P("leaf", None, None),
            P("leaf", None, None),
            P("leaf", None, None, None),
            P("leaf", None, None, None),
            P("leaf", None, None, None),
            P("leaf", None, None, None),
        ),
        out_specs=(P("leaf", None), P()),
        check_vma=False,
    )
```

time: 96.1 us -> 136 us (1.42)
  waiting for transfers between devices: 0.96 us -> 46.6 us
  between operations: 0.74 us -> 14.1 us
  blocking collectives: 16.1 us -> 7.03 us
  Pallas kernels: 54.6 us -> 46.9 us
  starting transfers between devices: 22.4 us -> 20.6 us
    all_gather x0 -> x1, waiting for transfers between devices: none -> 41.3 us  [shards(): share = lax.all_gather(share, 'leaf')]
    all_to_all x2 -> x1, blocking collectives: 16.1 us -> 7.03 us  [exchange(): lax.all_to_all(value, 'leaf', 0, 0, axis_index_groups=groups_of(bits, cou...]
    pallas_call x2, Pallas kernels: 33.3 us -> 25.6 us  [the longest x1 19.5 us: rows_up(): pl.pallas_call(rows_up_kernel, out_shape=(pltpu.HBM((NL, LEAF, V), F32),...]
    all_to_all x2, waiting for transfers between devices: 0.01 us -> 4.29 us  [exchange(): lax.all_to_all(value, 'leaf', 0, 0, axis_index_groups=groups_of(bits, cou...]
    all_to_all x2, starting transfers between devices: 14.6 us -> 11.8 us  [exchange(): lax.all_to_all(value, 'leaf', 0, 0, axis_index_groups=groups_of(bits, cou...]
    pallas_call x1, Pallas kernels: 16.8 us -> 14.9 us  [rows_down(): pl.pallas_call(rows_down_kernel, out_shape=pltpu.HBM((ROWS, V), F32), in_...]
    pallas_call x8 -> x7, Pallas kernels: 4.53 us -> 6.34 us  [call(): pl.pallas_call(body, out_shape=tuple((jax.ShapeDtypeStruct(o, F32) for o...]
  transfers between devices with their start and end apart: 6 -> 7, of which waited for: 1 -> 4; matrix products, arithmetic and copies ran while one was open for 0% -> 0% of each run, Pallas kernels for 40% -> 18%
where the time goes in v2:
time: 136 us
  Pallas kernels  46.9 us (34%)
  waiting for transfers between devices  46.6 us (34%)
  starting transfers between devices  20.6 us (15%)
  between operations  14.1 us (10%)
  blocking collectives  7.03 us (5%)
    all_gather x1, waiting for transfers between devices, shards(): share = lax.all_gather(share, 'leaf')  41.3 us
    pallas_call x1, Pallas kernels, rows_up(): pl.pallas_call(rows_up_kernel, out_shape=(pltpu.HBM((NL, LEAF, V), F32),...  19.5 us
    pallas_call x1, Pallas kernels, rows_down(): pl.pallas_call(rows_down_kernel, out_shape=pltpu.HBM((ROWS, V), F32), in_...  14.9 us
    all_to_all x2, starting transfers between devices, exchange(): lax.all_to_all(value, 'leaf', 0, 0, axis_index_groups=groups_of(bits, cou...  11.8 us
    ppermute x4, starting transfers between devices, swap(): lax.ppermute(value, 'leaf', [(s, s ^ 1 << level) for s in range(count)])  8.72 us
    all_to_all x1, blocking collectives, exchange(): lax.all_to_all(value, 'leaf', 0, 0, axis_index_groups=groups_of(bits, cou...  7.03 us
    pallas_call x7, Pallas kernels, call(): pl.pallas_call(body, out_shape=tuple((jax.ShapeDtypeStruct(o, F32) for o...  6.34 us
    pallas_call x1, Pallas kernels, fields(): pl.pallas_call(fields_kernel, out_shape=(pltpu.HBM((NL, R, V), F32), pltp...  6.14 us
  transfers between devices with their start and end apart: 7, of which 4 were waited for; matrix products, arithmetic and copies ran while one was open for 0% of the time, Pallas kernels for 18%

profile of v2, /device:TPU:1, one launch (start us, length us, event | category | flops | bytes accessed | tf_op | source)
XLA Modules:
  0.0 135.8 jit_solution(12633790064721044535)
XLA Ops:
  7.2 19.5 %rows_up.1 = (f32[8,512,384]{2,1,0:T(8,128)}, f32[14,128,384]{2,1,0:T(8,128)}, f32[2,384,128]{2,1,0:T(8,128)S(1)}, f32[8,384]{1,0:T(8,128)S(1)}) custom-call(s32[4096]{0:T(1024)} %slot_hbm.3, s32[1,8]{1,0:T(1,128)} %sizes_hbm.3, f32[4096,384]{1,0:T(8,128)} %v_hbm.1, f32[8,512,128]{2,1,0:T(8,128)} %basis_hbm.3, f32[15,128,128]{2,1,0:T(8,128)} %bitcast.19, ...), custom_call_target="tpu_custom_call" | custom-call | flops 7000000000 | bytes 28000000 | tf_op jit(solution)/shard_map/rows_up/pallas_call | solution.py:195
  26.7 1.7 %collective-permute-start = (f32[2,384,128]{2,1,0:T(8,128)S(1)}, f32[2,384,128]{2,1,0:T(8,128)S(1)}, u32[]{:S(2)}, u32[]{:S(2)}) collective-permute-start(f32[2,384,128]{2,1,0:T(8,128)S(1)} %get-tuple-element.23.pay_ref), channel_id=1, source_target_pairs={{0,1},{1,0},{2,3},{3,2},{4,5},{5,4},{6,7},{7,6},{8,9},{9,8},{10,11... | collective-permute-start | bytes 1179656 | tf_op jit(solution)/shard_map/ppermute | solution.py:555
  28.4 1.8 %chains.1 = (f32[128,256]{1,0:T(8,128)S(1)}, f32[128,384]{1,0:T(8,128)S(1)}, f32[256,128]{1,0:T(8,128)S(1)}, f32[384,128]{1,0:T(8,128)S(1)}, f32[512,128]{1,0:T(8,128)S(1)}, /*index=5*/f32[128,128]{1,0:T(8,128)S(1)}) custom-call(s32[1]{0:T(128)} %bitcast.me, f32[15,128,128]{2,1,0:T(8,128)} %bitcast.20, f32[5,128,128]{2,1,0:T(8,128)} %bitcast.23, ...), custom_call_target="tpu_custom_call" | custom-call | flops 100000000 | bytes 1000000 | tf_op jit(solution)/shard_map/chains/pallas_call | solution.py:409
  30.2 0.0 collective-permute-done.got_ref
  30.3 0.8 after_core.1
  31.1 4.2 %all-to-all-start = ((f32[4,48,128]{2,1,0:T(8,128)}), f32[4,48,128]{2,1,0:T(8,128)S(1)}, u32[]{:S(2)}, u32[]{:S(2)}) async-start(f32[4,48,128]{2,1,0:T(8,128)} %bitcast.5), calls=%async_computation | async-start | bytes 196608 | tf_op jit(solution)/shard_map/all_to_all | solution.py:558
  35.3 1.5 %collective-permute-start.1 = (f32[2,192,128]{2,1,0:T(8,128)S(1)}, f32[2,192,128]{2,1,0:T(8,128)S(1)}, u32[]{:S(2)}, u32[]{:S(2)}) collective-permute-start(f32[2,192,128]{2,1,0:T(8,128)S(1)} %get-tuple-element.25.pair2_ref), channel_id=1, source_target_pairs={{0,2},{1,3},{2,0},{3,1},{4,6},{5,7},{6,4},{7,5},{8,10},{9,11},{10,... | collective-permute-start | bytes 589832 | tf_op jit(solution)/shard_map/ppermute | solution.py:555
  36.7 3.2 %all-to-all-done = f32[4,48,128]{2,1,0:T(8,128)S(1)} async-done(((f32[4,48,128]{2,1,0:T(8,128)}), f32[4,48,128]{2,1,0:T(8,128)S(1)}, u32[]{:S(2)}, u32[]{:S(2)}) %all-to-all-start) | async-done | bytes 98336 | tf_op jit(solution)/shard_map/all_to_all | solution.py:558
  39.9 1.0 after_y.1
  40.9 7.6 %all-to-all-start.1 = ((f32[16,48,128]{2,1,0:T(8,128)}), f32[16,48,128]{2,1,0:T(8,128)S(1)}, u32[]{:S(2)}, u32[]{:S(2)}) async-start(f32[16,48,128]{2,1,0:T(8,128)} %bitcast.7), calls=%async_computation.1 | async-start | bytes 786432 | tf_op jit(solution)/shard_map/all_to_all | solution.py:558
  48.6 0.0 all-gather.3.cloned.1.call-start
  48.6 0.0 collective-permute-done.1.got_ref.pair_got_ref
  48.7 1.0 collective-permute-start.2
  49.7 6.1 %fields.1 = (f32[8,128,384]{2,1,0:T(8,128)}, f32[8,128,128]{2,1,0:T(8,128)}, f32[8,384]{1,0:T(8,128)S(1)}) custom-call(s32[1]{0:T(128)} %bitcast.me, f32[14,128,384]{2,1,0:T(8,128)} %get-tuple-element.22.call_hbm, f32[15,128,128]{2,1,0:T(8,128)} %bitcast.21, f32[7,128,128]{2,1,0:T(8,128)} %bitcast.24, f32[2,384,128]{2,1,0:T(8,128)S(1)} %get-tuple-element.23.pay_ref, ...), custom_call_target="tpu_custom_call" | custom-call | flops 2000000000 | bytes 8000000 | tf_op jit(solution)/shard_map/fields/pallas_call | solution.py:275
  55.8 0.0 collective-permute-done.2.quad_got_ref
  55.8 1.1 all-to-all-done.1
  56.9 1.2 after_top.1
  58.1 0.0 all-gather.3.cloned.1.call-update
  58.1 7.0 %all_to_all.33 = f32[4,48,128]{2,1,0:T(8,128)S(1)} all-to-all(f32[4,48,128]{2,1,0:T(8,128)S(1)} %bitcast.17), channel_id=1, replica_groups={{0,2,4,6},{1,3,5,7},{8,10,12,14},{9,11,13,15},{16,18,20,22},{17,19,21,2..., dimensions={0} | all-to-all | bytes 196608 | tf_op jit(solution)/shard_map/all_to_all | solution.py:558
  65.2 0.3 to_core.1.own_ref
  65.4 4.5 %collective-permute-start.3 = (f32[192,128]{1,0:T(8,128)S(1)}, f32[192,128]{1,0:T(8,128)S(1)}, u32[]{:S(2)}, u32[]{:S(2)}) collective-permute-start(f32[192,128]{1,0:T(8,128)S(1)} %to_core.1.own_ref), channel_id=1, source_target_pairs={{0,1},{1,0},{2,3},{3,2},{4,5},{5,4},{6,7},{7,6},{8,9},{9,8},{10,11... | collective-permute-start | bytes 294920 | tf_op jit(solution)/shard_map/ppermute | solution.py:555
  70.0 0.9 collective-permute-done.3.other_ref
  70.9 14.9 %rows_down.1 = f32[4096,384]{1,0:T(8,128)} custom-call(s32[1]{0:T(128)} %bitcast.me, s32[4096]{0:T(1024)} %slot_hbm.3, s32[1,8]{1,0:T(1,128)} %sizes_hbm.3, f32[8,512,128]{2,1,0:T(8,128)} %basis_hbm.3, f32[8,512,384]{2,1,0:T(8,128)} %get-tuple-element.21.part_hbm, f32[8,128,384]{2,1,0:T(8,128)} %get-tuple-element.29.local_hbm, ...), custom_call_target="tpu_custom_call" | custom-call | flops 2000000000 | bytes 16000000 | tf_op jit(solution)/shard_map/rows_down/pallas_call | solution.py:515
  85.9 41.3 %all-gather.3.cloned.1.call-done = f32[8192,128]{1,0:T(8,128)} async-done(((f32[64,128]{1,0:T(8,128)}), f32[8192,128]{1,0:T(8,128)}) %all-gather.3.cloned.1.call-update) | async-done | bytes 4194320 | tf_op jit(solution)/shard_map/all_gather | solution.py:604
  127.2 1.2 all_share.1
  128.4 0.6 slice_bitcast_fusion
  (1 shorter events, 0.0 us)
Async XLA Ops:
  26.7 3.6 %collective-permute-start = (f32[2,384,128]{2,1,0:T(8,128)S(1)}, f32[2,384,128]{2,1,0:T(8,128)S(1)}, u32[]{:S(2)}, u32[]{:S(2)}) collective-permute-start(f32[2,384,128]{2,1,0:T(8,128)S(1)} %get-tuple-element.23.pay_ref), channel_id=1, source_target_pairs={{0,1},{1,0},{2,3},{3,2},{4,5},{5,4},{6,7},{7,6},{8,9},{9,8},{10,11... | collective-permute-start | bytes 1179656 | tf_op jit(solution)/shard_map/ppermute | solution.py:555
  31.1 8.8 %all-to-all-start = ((f32[4,48,128]{2,1,0:T(8,128)}), f32[4,48,128]{2,1,0:T(8,128)S(1)}, u32[]{:S(2)}, u32[]{:S(2)}) async-start(f32[4,48,128]{2,1,0:T(8,128)} %bitcast.5), calls=%async_computation | async-start | bytes 196608 | tf_op jit(solution)/shard_map/all_to_all | solution.py:558
  35.3 13.3 %collective-permute-start.1 = (f32[2,192,128]{2,1,0:T(8,128)S(1)}, f32[2,192,128]{2,1,0:T(8,128)S(1)}, u32[]{:S(2)}, u32[]{:S(2)}) collective-permute-start(f32[2,192,128]{2,1,0:T(8,128)S(1)} %get-tuple-element.25.pair2_ref), channel_id=1, source_target_pairs={{0,2},{1,3},{2,0},{3,1},{4,6},{5,7},{6,4},{7,5},{8,10},{9,11},{10,... | collective-permute-start | bytes 589832 | tf_op jit(solution)/shard_map/ppermute | solution.py:555
  40.9 16.0 %all-to-all-start.1 = ((f32[16,48,128]{2,1,0:T(8,128)}), f32[16,48,128]{2,1,0:T(8,128)S(1)}, u32[]{:S(2)}, u32[]{:S(2)}) async-start(f32[16,48,128]{2,1,0:T(8,128)} %bitcast.7), calls=%async_computation.1 | async-start | bytes 786432 | tf_op jit(solution)/shard_map/all_to_all | solution.py:558
  48.6 78.6 %all-gather.3.cloned.1.call-start = ((), (), s32[]{:S(2)}) async-start(), calls=%async_computation.3 | async-start | bytes 4227072 | tf_op jit(solution)/shard_map/all_gather | solution.py:604
  48.7 7.1 %collective-permute-start.2 = (f32[192,128]{1,0:T(8,128)S(1)}, f32[192,128]{1,0:T(8,128)S(1)}, u32[]{:S(2)}, u32[]{:S(2)}) collective-permute-start(f32[192,128]{1,0:T(8,128)S(1)} %after_pair.1.c2_ref), channel_id=1, source_target_pairs={{0,4},{1,5},{2,6},{3,7},{4,0},{5,1},{6,2},{7,3},{8,12},{9,13},{10,... | collective-permute-start | bytes 294920 | tf_op jit(solution)/shard_map/ppermute | solution.py:555
  65.4 5.5 %collective-permute-start.3 = (f32[192,128]{1,0:T(8,128)S(1)}, f32[192,128]{1,0:T(8,128)S(1)}, u32[]{:S(2)}, u32[]{:S(2)}) collective-permute-start(f32[192,128]{1,0:T(8,128)S(1)} %to_core.1.own_ref), channel_id=1, source_target_pairs={{0,1},{1,0},{2,3},{3,2},{4,5},{5,4},{6,7},{7,6},{8,9},{9,8},{10,11... | collective-permute-start | bytes 294920 | tf_op jit(solution)/shard_map/ppermute | solution.py:555
Sparse Core Ops, SparseCore 0:
  58.3 68.8 all-gather.2

commit v3 on v2

--- a/solution.py
+++ b/solution.py
@@ -13,7 +13,6 @@
 V = 384
 HALF = V // 2
 QUART = HALF // 4
-SHARE = 64
 ROWS = NL * LEAF
 S = 4
 MB = 256
@@ -360,7 +359,7 @@
 
 
 def after_top_kernel(
-    me, got_ref, m3_ref, side2_ref, c2_ref, quad_got_ref, c3_ref, local_ref, send_ref, share_ref, z
+    me, got_ref, m3_ref, side2_ref, c2_ref, quad_got_ref, c3_ref, local_ref, send_ref, z
 ):
     dev = me[0]
     group = dev // 8
@@ -379,9 +378,8 @@
     z[pl.ds(at, QUART), :] += c3_ref[...] * inc3
     share = lane_rows(local_ref[...] + row_sums(z[...]))
     for n in range(4):
-        send_ref[n * QUART : (n + 1) * QUART] = inc3
-    for n in range(SHARE // 8):
-        share_ref[8 * n : 8 * n + 8] = share
+        send_ref[n, 0:QUART] = inc3
+        send_ref[n, QUART : QUART + 8] = share
 
 
 def after_pair_kernel(pair2_ref, got_ref, c2_ref):
@@ -389,15 +387,26 @@
 
 
 def to_core_kernel(got_ref, pair_got_ref, quad_got_ref, m1_ref, out_ref):
-    sums = jnp.concatenate([pair_got_ref[0], quad_got_ref[...], got_ref[...]], axis=1)
-    out_ref[...] = dot3(sums, m1_ref[...])
-
-
-def all_share_kernel(got_hbm, out_ref, got, sem):
-    cp = pltpu.make_async_copy(got_hbm.at[:, pl.ds(0, 8)], got, sem)
-    cp.start()
-    cp.wait()
-    out_ref[...] = jnp.sum(got[...], axis=0) * (1.0 / (2.0 * LEAF))
+    inc3 = jnp.concatenate([got_ref[n, 0:QUART] for n in range(4)], axis=0)
+    sums = jnp.concatenate([pair_got_ref[0], quad_got_ref[...], inc3], axis=1)
+    out_ref[0:HALF] = dot3(sums, m1_ref[...])
+    share = got_ref[0, QUART : QUART + 8]
+    for n in range(1, 4):
+        share = share + got_ref[n, QUART : QUART + 8]
+    out_ref[HALF : HALF + 8] = share
+
+
+def core_share_kernel(own_ref, other_ref, send_ref):
+    total = own_ref[HALF : HALF + 8] + other_ref[HALF : HALF + 8]
+    for n in range(16):
+        send_ref[n] = total
+
+
+def all_share_kernel(got_ref, out_ref):
+    total = got_ref[0]
+    for n in range(1, 16):
+        total = total + got_ref[n]
+    out_ref[...] = total * (1.0 / (2.0 * LEAF))
 
 
 def small(body, outs, name, flops, scratch=(), hbm_args=()):
@@ -443,8 +452,8 @@
     for c in loads:
         c.start()
     half = me[0] % 2
-    inct[pl.ds(pl.multiple_of(half * HALF, HALF), HALF), :] = own_ref[...]
-    inct[pl.ds(pl.multiple_of((1 - half) * HALF, HALF), HALF), :] = other_ref[...]
+    inct[pl.ds(pl.multiple_of(half * HALF, HALF), HALF), :] = own_ref[0:HALF]
+    inct[pl.ds(pl.multiple_of((1 - half) * HALF, HALF), HALF), :] = other_ref[0:HALF]
     root = dot3(jnp.concatenate([got_ref[0], inct[...]], axis=1), m0_ref[...])
     rsplit = split(root.T)
     for c in copies:
@@ -593,22 +602,20 @@
     local, tmat, curv = fields(
         me, call, trans, coup, pay, core_got, pair2, pair_got, c2, m0, m1, curv
     )
-    inc3, share = small(
-        after_top_kernel, [(HALF, R), (SHARE, R)], "after_top", 10**8, [pltpu.VMEM((V, R), F32)]
+    (inc3,) = small(
+        after_top_kernel, [(4, QUART + 8, R)], "after_top", 10**8, [pltpu.VMEM((V, R), F32)]
     )(me, top_got, m3, side2, c2, quad_got, c3, curv)
     inc3_got = exchange(inc3, (1, 2))
-    (inc1,) = small(to_core_kernel, [(HALF, R)], "to_core", 10**8)(
+    (inc1,) = small(to_core_kernel, [(HALF + 8, R)], "to_core", 10**8)(
         inc3_got, pair_got, quad_got, m1
     )
     inc1_got = swap(inc1, 0)
-    share = lax.all_gather(share, "leaf")
+    (share,) = small(core_share_kernel, [(16, 8, R)], "core_share", 10**5)(inc1, inc1_got)
+    share = exchange(share, (3, 4, 5, 6))
     products = rows_down(
         me, slot_frame, leaf_sizes, leaf_basis, part, local, tmat, inc1, inc1_got, core_got, m0
     )
-    (curvature,) = small(
-        all_share_kernel, [(8, R)], "all_share", 10**5,
-        [pltpu.VMEM((count, 8, R), F32), pltpu.SemaphoreType.DMA], (0,),
-    )(far(share))
+    (curvature,) = small(all_share_kernel, [(8, R)], "all_share", 10**5)(share)
     return products, curvature[0:3].reshape(V)
 
 

time: 136 us -> 86.5 us (0.64)
  waiting for transfers between devices: 46.6 us -> 5.3 us
  between operations: 14.1 us -> 0.73 us
  starting transfers between devices: 20.6 us -> 26.6 us
    all_gather x1 -> x0, waiting for transfers between devices: 41.3 us -> none  [shards(): share = lax.all_gather(share, 'leaf')]
    all_to_all x2 -> x3, starting transfers between devices: 11.8 us -> 17.9 us  [exchange(): lax.all_to_all(value, 'leaf', 0, 0, axis_index_groups=groups_of(bits, cou...]
    pallas_call x7 -> x8, Pallas kernels: 6.34 us -> 5.17 us  [call(): pl.pallas_call(body, out_shape=tuple((jax.ShapeDtypeStruct(o, F32) for o...]
    all_to_all x2 -> x3, waiting for transfers between devices: 4.29 us -> 4.34 us  [exchange(): lax.all_to_all(value, 'leaf', 0, 0, axis_index_groups=groups_of(bits, cou...]
  transfers between devices with their start and end apart: 7 -> 7, of which waited for: 4 -> 3; matrix products, arithmetic and copies ran while one was open for 0% -> 0% of each run, Pallas kernels for 18% -> 28%
where the time goes in v3:
time: 86.5 us; the launch traced here: 86.1 us
  Pallas kernels  45.7 us (53%)
  starting transfers between devices  26.6 us (31%)
  blocking collectives  7.14 us (8%)
  waiting for transfers between devices  5.3 us (6%)
    pallas_call x1, Pallas kernels, rows_up(): pl.pallas_call(rows_up_kernel, out_shape=(pltpu.HBM((NL, LEAF, V), F32),...  19.5 us
    all_to_all x3, starting transfers between devices, exchange(): lax.all_to_all(value, 'leaf', 0, 0, axis_index_groups=groups_of(bits, cou...  17.9 us
    pallas_call x1, Pallas kernels, rows_down(): pl.pallas_call(rows_down_kernel, out_shape=pltpu.HBM((ROWS, V), F32), in_...  14.9 us
    ppermute x4, starting transfers between devices, swap(): lax.ppermute(value, 'leaf', [(s, s ^ 1 << level) for s in range(count)])  8.72 us
    all_to_all x1, blocking collectives, exchange(): lax.all_to_all(value, 'leaf', 0, 0, axis_index_groups=groups_of(bits, cou...  7.14 us
    pallas_call x1, Pallas kernels, fields(): pl.pallas_call(fields_kernel, out_shape=(pltpu.HBM((NL, R, V), F32), pltp...  6.14 us
    pallas_call x8, Pallas kernels, call(): pl.pallas_call(body, out_shape=tuple((jax.ShapeDtypeStruct(o, F32) for o...  5.17 us
    all_to_all x3, waiting for transfers between devices, exchange(): lax.all_to_all(value, 'leaf', 0, 0, axis_index_groups=groups_of(bits, cou...  4.34 us
  transfers between devices with their start and end apart: 7, of which 3 were waited for; matrix products, arithmetic and copies ran while one was open for 0% of the time, Pallas kernels for 28%

profile of v3, /device:TPU:1, one launch (start us, length us, event | category | flops | bytes accessed | tf_op | source)
XLA Modules:
  0.0 86.1 jit_solution(13967214613037697841)
XLA Ops:
  0.6 19.5 %rows_up.1 = (f32[8,512,384]{2,1,0:T(8,128)}, f32[14,128,384]{2,1,0:T(8,128)}, f32[2,384,128]{2,1,0:T(8,128)S(1)}, f32[8,384]{1,0:T(8,128)S(1)}) custom-call(s32[4096]{0:T(1024)} %slot_hbm.3, s32[1,8]{1,0:T(1,128)} %sizes_hbm.3, f32[4096,384]{1,0:T(8,128)} %v_hbm.1, f32[8,512,128]{2,1,0:T(8,128)} %basis_hbm.3, f32[15,128,128]{2,1,0:T(8,128)} %bitcast.13, ...), custom_call_target="tpu_custom_call" | custom-call | flops 7000000000 | bytes 28000000 | tf_op jit(solution)/shard_map/rows_up/pallas_call | solution.py:194
  20.1 1.7 %collective-permute-start = (f32[2,384,128]{2,1,0:T(8,128)S(1)}, f32[2,384,128]{2,1,0:T(8,128)S(1)}, u32[]{:S(2)}, u32[]{:S(2)}) collective-permute-start(f32[2,384,128]{2,1,0:T(8,128)S(1)} %get-tuple-element.21.pay_ref), channel_id=1, source_target_pairs={{0,1},{1,0},{2,3},{3,2},{4,5},{5,4},{6,7},{7,6},{8,9},{9,8},{10,11... | collective-permute-start | bytes 1179656 | tf_op jit(solution)/shard_map/ppermute | solution.py:564
  21.8 1.9 %chains.1 = (f32[128,256]{1,0:T(8,128)S(1)}, f32[128,384]{1,0:T(8,128)S(1)}, f32[256,128]{1,0:T(8,128)S(1)}, f32[384,128]{1,0:T(8,128)S(1)}, f32[512,128]{1,0:T(8,128)S(1)}, /*index=5*/f32[128,128]{1,0:T(8,128)S(1)}) custom-call(s32[1]{0:T(128)} %bitcast.me, f32[15,128,128]{2,1,0:T(8,128)} %bitcast.14, f32[5,128,128]{2,1,0:T(8,128)} %bitcast.17, ...), custom_call_target="tpu_custom_call" | custom-call | flops 100000000 | bytes 1000000 | tf_op jit(solution)/shard_map/chains/pallas_call | solution.py:418
  23.7 0.0 collective-permute-done.got_ref
  23.7 0.8 after_core.1
  24.5 4.3 %all-to-all-start = ((f32[4,48,128]{2,1,0:T(8,128)}), f32[4,48,128]{2,1,0:T(8,128)S(1)}, u32[]{:S(2)}, u32[]{:S(2)}) async-start(f32[4,48,128]{2,1,0:T(8,128)} %bitcast.5), calls=%async_computation | async-start | bytes 196608 | tf_op jit(solution)/shard_map/all_to_all | solution.py:567
  28.8 1.5 %collective-permute-start.1 = (f32[2,192,128]{2,1,0:T(8,128)S(1)}, f32[2,192,128]{2,1,0:T(8,128)S(1)}, u32[]{:S(2)}, u32[]{:S(2)}) collective-permute-start(f32[2,192,128]{2,1,0:T(8,128)S(1)} %get-tuple-element.23.pair2_ref), channel_id=1, source_target_pairs={{0,2},{1,3},{2,0},{3,1},{4,6},{5,7},{6,4},{7,5},{8,10},{9,11},{10,... | collective-permute-start | bytes 589832 | tf_op jit(solution)/shard_map/ppermute | solution.py:564
  30.3 3.2 %all-to-all-done = f32[4,48,128]{2,1,0:T(8,128)S(1)} async-done(((f32[4,48,128]{2,1,0:T(8,128)}), f32[4,48,128]{2,1,0:T(8,128)S(1)}, u32[]{:S(2)}, u32[]{:S(2)}) %all-to-all-start) | async-done | bytes 98336 | tf_op jit(solution)/shard_map/all_to_all | solution.py:567
  33.5 1.0 %after_y.1 = (f32[768,128]{1,0:T(8,128)}, f32[48,128]{1,0:T(8,128)S(1)}) custom-call(s32[1]{0:T(128)} %bitcast.me, f32[192,128]{1,0:T(8,128)S(1)} %bitcast.12, f32[128,384]{1,0:T(8,128)S(1)} %get-tuple-element.30.a2_ref), custom_call_target="tpu_custom_call" | custom-call | flops 100000000 | bytes 1000000 | tf_op jit(solution)/shard_map/after_y/pallas_call | solution.py:418
  34.5 7.6 %all-to-all-start.1 = ((f32[16,48,128]{2,1,0:T(8,128)}), f32[16,48,128]{2,1,0:T(8,128)S(1)}, u32[]{:S(2)}, u32[]{:S(2)}) async-start(f32[16,48,128]{2,1,0:T(8,128)} %bitcast.7), calls=%async_computation.1 | async-start | bytes 786432 | tf_op jit(solution)/shard_map/all_to_all | solution.py:567
  42.1 0.0 collective-permute-done.1.got_ref.pair_got_ref
  42.1 1.0 %collective-permute-start.2 = (f32[192,128]{1,0:T(8,128)S(1)}, f32[192,128]{1,0:T(8,128)S(1)}, u32[]{:S(2)}, u32[]{:S(2)}) collective-permute-start(f32[192,128]{1,0:T(8,128)S(1)} %after_pair.1.c2_ref), channel_id=1, source_target_pairs={{0,4},{1,5},{2,6},{3,7},{4,0},{5,1},{6,2},{7,3},{8,12},{9,13},{10,... | collective-permute-start | bytes 294920 | tf_op jit(solution)/shard_map/ppermute | solution.py:564
  43.1 6.1 %fields.1 = (f32[8,128,384]{2,1,0:T(8,128)}, f32[8,128,128]{2,1,0:T(8,128)}, f32[8,384]{1,0:T(8,128)S(1)}) custom-call(s32[1]{0:T(128)} %bitcast.me, f32[14,128,384]{2,1,0:T(8,128)} %get-tuple-element.20.call_hbm, f32[15,128,128]{2,1,0:T(8,128)} %bitcast.15, f32[7,128,128]{2,1,0:T(8,128)} %bitcast.18, f32[2,384,128]{2,1,0:T(8,128)S(1)} %get-tuple-element.21.pay_ref, ...), custom_call_target="tpu_custom_call" | custom-call | flops 2000000000 | bytes 8000000 | tf_op jit(solution)/shard_map/fields/pallas_call | solution.py:274
  49.2 0.0 collective-permute-done.2.quad_got_ref
  49.2 1.2 %all-to-all-done.1 = f32[16,48,128]{2,1,0:T(8,128)S(1)} async-done(((f32[16,48,128]{2,1,0:T(8,128)}), f32[16,48,128]{2,1,0:T(8,128)S(1)}, u32[]{:S(2)}, u32[]{:S(2)}) %all-to-all-start.1) | async-done | bytes 393248 | tf_op jit(solution)/shard_map/all_to_all | solution.py:567
  50.4 0.5 after_top.1
  50.9 7.1 %all_to_all.32.got_ref = f32[4,56,128]{2,1,0:T(8,128)S(1)} all-to-all(f32[4,56,128]{2,1,0:T(8,128)S(1)} %after_top.1), channel_id=1, replica_groups={{0,2,4,6},{1,3,5,7},{8,10,12,14},{9,11,13,15},{16,18,20,22},{17,19,21,2..., dimensions={0} | all-to-all | bytes 229376 | tf_op jit(solution)/shard_map/all_to_all | solution.py:567
  58.1 0.3 to_core.1.own_ref
  58.4 4.5 %collective-permute-start.3 = (f32[200,128]{1,0:T(8,128)S(1)}, f32[200,128]{1,0:T(8,128)S(1)}, u32[]{:S(2)}, u32[]{:S(2)}) collective-permute-start(f32[200,128]{1,0:T(8,128)S(1)} %to_core.1.own_ref), channel_id=1, source_target_pairs={{0,1},{1,0},{2,3},{3,2},{4,5},{5,4},{6,7},{7,6},{8,9},{9,8},{10,11... | collective-permute-start | bytes 307208 | tf_op jit(solution)/shard_map/ppermute | solution.py:564
  62.9 0.9 %collective-permute-done.3.other_ref = f32[200,128]{1,0:T(8,128)S(1)} collective-permute-done((f32[200,128]{1,0:T(8,128)S(1)}, f32[200,128]{1,0:T(8,128)S(1)}, u32[]{:S(2)}, u32[]{:S(2)}) %collective-permute-start.3) | collective-permute-done | bytes 102432 | tf_op jit(solution)/shard_map/ppermute | solution.py:564
  63.9 0.6 core_share.1
  64.5 6.0 %all-to-all-start.3 = ((f32[16,8,128]{2,1,0:T(8,128)}), f32[16,8,128]{2,1,0:T(8,128)S(1)}, u32[]{:S(2)}, u32[]{:S(2)}) async-start(f32[16,8,128]{2,1,0:T(8,128)} %core_share.1), calls=%async_computation.3 | async-start | bytes 131072 | tf_op jit(solution)/shard_map/all_to_all | solution.py:567
  70.5 14.9 %rows_down.1 = f32[4096,384]{1,0:T(8,128)} custom-call(s32[1]{0:T(128)} %bitcast.me, s32[4096]{0:T(1024)} %slot_hbm.3, s32[1,8]{1,0:T(1,128)} %sizes_hbm.3, f32[8,512,128]{2,1,0:T(8,128)} %basis_hbm.3, f32[8,512,384]{2,1,0:T(8,128)} %get-tuple-element.19.part_hbm, f32[8,128,384]{2,1,0:T(8,128)} %get-tuple-element.27.local_hbm, ...), custom_call_target="tpu_custom_call" | custom-call | flops 2000000000 | bytes 16000000 | tf_op jit(solution)/shard_map/rows_down/pallas_call | solution.py:524
  85.5 0.0 all-to-all-done.3.got_ref
  85.5 0.6 slice_bitcast_fusion
  (2 shorter events, 0.0 us)
Async XLA Ops:
  20.1 3.6 %collective-permute-start = (f32[2,384,128]{2,1,0:T(8,128)S(1)}, f32[2,384,128]{2,1,0:T(8,128)S(1)}, u32[]{:S(2)}, u32[]{:S(2)}) collective-permute-start(f32[2,384,128]{2,1,0:T(8,128)S(1)} %get-tuple-element.21.pay_ref), channel_id=1, source_target_pairs={{0,1},{1,0},{2,3},{3,2},{4,5},{5,4},{6,7},{7,6},{8,9},{9,8},{10,11... | collective-permute-start | bytes 1179656 | tf_op jit(solution)/shard_map/ppermute | solution.py:564
  24.5 9.0 %all-to-all-start = ((f32[4,48,128]{2,1,0:T(8,128)}), f32[4,48,128]{2,1,0:T(8,128)S(1)}, u32[]{:S(2)}, u32[]{:S(2)}) async-start(f32[4,48,128]{2,1,0:T(8,128)} %bitcast.5), calls=%async_computation | async-start | bytes 196608 | tf_op jit(solution)/shard_map/all_to_all | solution.py:567
  28.8 13.2 %collective-permute-start.1 = (f32[2,192,128]{2,1,0:T(8,128)S(1)}, f32[2,192,128]{2,1,0:T(8,128)S(1)}, u32[]{:S(2)}, u32[]{:S(2)}) collective-permute-start(f32[2,192,128]{2,1,0:T(8,128)S(1)} %get-tuple-element.23.pair2_ref), channel_id=1, source_target_pairs={{0,2},{1,3},{2,0},{3,1},{4,6},{5,7},{6,4},{7,5},{8,10},{9,11},{10,... | collective-permute-start | bytes 589832 | tf_op jit(solution)/shard_map/ppermute | solution.py:564
  34.5 15.9 %all-to-all-start.1 = ((f32[16,48,128]{2,1,0:T(8,128)}), f32[16,48,128]{2,1,0:T(8,128)S(1)}, u32[]{:S(2)}, u32[]{:S(2)}) async-start(f32[16,48,128]{2,1,0:T(8,128)} %bitcast.7), calls=%async_computation.1 | async-start | bytes 786432 | tf_op jit(solution)/shard_map/all_to_all | solution.py:567
  42.1 7.2 %collective-permute-start.2 = (f32[192,128]{1,0:T(8,128)S(1)}, f32[192,128]{1,0:T(8,128)S(1)}, u32[]{:S(2)}, u32[]{:S(2)}) collective-permute-start(f32[192,128]{1,0:T(8,128)S(1)} %after_pair.1.c2_ref), channel_id=1, source_target_pairs={{0,4},{1,5},{2,6},{3,7},{4,0},{5,1},{6,2},{7,3},{8,12},{9,13},{10,... | collective-permute-start | bytes 294920 | tf_op jit(solution)/shard_map/ppermute | solution.py:564
  58.4 5.5 %collective-permute-start.3 = (f32[200,128]{1,0:T(8,128)S(1)}, f32[200,128]{1,0:T(8,128)S(1)}, u32[]{:S(2)}, u32[]{:S(2)}) collective-permute-start(f32[200,128]{1,0:T(8,128)S(1)} %to_core.1.own_ref), channel_id=1, source_target_pairs={{0,1},{1,0},{2,3},{3,2},{4,5},{5,4},{6,7},{7,6},{8,9},{9,8},{10,11... | collective-permute-start | bytes 307208 | tf_op jit(solution)/shard_map/ppermute | solution.py:564
  64.5 21.0 %all-to-all-start.3 = ((f32[16,8,128]{2,1,0:T(8,128)}), f32[16,8,128]{2,1,0:T(8,128)S(1)}, u32[]{:S(2)}, u32[]{:S(2)}) async-start(f32[16,8,128]{2,1,0:T(8,128)} %core_share.1), calls=%async_computation.3 | async-start | bytes 131072 | tf_op jit(solution)/shard_map/all_to_all | solution.py:567

commit v4 on v3

--- a/solution.py
+++ b/solution.py
@@ -15,7 +15,8 @@
 QUART = HALF // 4
 ROWS = NL * LEAF
 S = 4
-MB = 256
+MB = 128
+BT = 16
 UN = 32
 F32 = jnp.float32
 BF16 = jnp.bfloat16
@@ -67,9 +68,9 @@
 
 
 def rows_up_kernel(
-    slot_hbm, sizes_hbm, v_hbm, basis_hbm, trans_hbm, near_hbm,
-    part_hbm, call_hbm, pay_ref, curv_ref,
-    slot, sizes, vbuf, vt, xt, basis, trans, near, xh, xl, call_ref,
+    slot_hbm, sizes_hbm, v_hbm, basis_hbm, trans_hbm, near_hbm, upper_hbm,
+    part_hbm, call_hbm, pay_ref, curv_ref, lift_ref,
+    slot, sizes, vbuf, vt, xt, basis, trans, near, xh, xl, call_ref, upper,
     sem, vsem, nsem, osem,
 ):
     copies = [
@@ -77,6 +78,7 @@
         pltpu.make_async_copy(sizes_hbm, sizes, sem.at[1]),
         pltpu.make_async_copy(basis_hbm, basis, sem.at[2]),
         pltpu.make_async_copy(trans_hbm, trans, sem.at[3]),
+        pltpu.make_async_copy(upper_hbm.at[pl.ds(0, 2)], upper, sem.at[4]),
     ]
     chunks = [
         pltpu.make_async_copy(
@@ -98,6 +100,7 @@
             for n in nears:
                 n.start()
             copies[3].start()
+            copies[4].start()
 
         def spread(i, _, c=c):
             for u in range(8):
@@ -155,8 +158,8 @@
             vbuf[leaf * LEAF + MB * blk : leaf * LEAF + MB * blk + MB, :] = prod
             if leaf + 1 < NL:
                 pack(leaf + 1, MB * blk, MB * blk + MB)
-        if leaf % 4 == 3:
-            for n in range(leaf - 3, leaf + 1):
+        if leaf % 2 == 1:
+            for n in range(leaf - 1, leaf + 1):
                 cp = pltpu.make_async_copy(
                     vbuf.at[pl.ds(n * LEAF, LEAF)], part_hbm.at[n], osem.at[n]
                 )
@@ -166,6 +169,7 @@
             for cp in nears[4:]:
                 cp.wait()
     copies[3].wait()
+    copies[4].wait()
     offset, at = 0, NL
     while len(coeffs) > 1:
         parents = []
@@ -183,12 +187,14 @@
     outs.append(cp)
     curv_ref[...] = jnp.broadcast_to(total, (8, V))
     pay_ref[0] = parents[0].T
-    pay_ref[1] = dot3s([(coeffs[0], split(trans[2 * NL - 2]))], 0, 0)
+    lift = dot3s([(coeffs[0], split(trans[2 * NL - 2]))], 0, 0)
+    pay_ref[1] = lift
+    lift_ref[...] = dot3(dot3(lift, upper[0]), upper[1])
     for cp in outs:
         cp.wait()
 
 
-def rows_up(slot, sizes, vectors, basis, trans, near):
+def rows_up(slot, sizes, vectors, basis, trans, near, upper):
     hbm = pl.BlockSpec(memory_space=pltpu.HBM)
     vmem = pl.BlockSpec(memory_space=pltpu.VMEM)
     return pl.pallas_call(
@@ -198,9 +204,10 @@
             pltpu.HBM((14, R, V), F32),
             jax.ShapeDtypeStruct((2, V, R), F32),
             jax.ShapeDtypeStruct((8, V), F32),
+            jax.ShapeDtypeStruct((V, R), F32),
         ),
-        in_specs=[hbm] * 6,
-        out_specs=(hbm, hbm, vmem, vmem),
+        in_specs=[hbm] * 7,
+        out_specs=(hbm, hbm, vmem, vmem, vmem),
         scratch_shapes=[
             pltpu.SMEM((ROWS,), jnp.int32),
             pltpu.SMEM((1, NL), jnp.int32),
@@ -213,7 +220,8 @@
             pltpu.VMEM((NL, LEAF, V), BF16),
             pltpu.VMEM((NL, LEAF, V), BF16),
             pltpu.VMEM((14, R, V), F32),
-            pltpu.SemaphoreType.DMA((4,)),
+            pltpu.VMEM((2, R, R), F32),
+            pltpu.SemaphoreType.DMA((5,)),
             pltpu.SemaphoreType.DMA((NL,)),
             pltpu.SemaphoreType.DMA((NL,)),
             pltpu.SemaphoreType.DMA((NL + 1,)),
@@ -221,7 +229,7 @@
         compiler_params=pltpu.CompilerParams(vmem_limit_bytes=50 * MIB),
         cost_estimate=pl.CostEstimate(flops=7 * 10**9, bytes_accessed=28 * 10**6, transcendentals=0),
         name="rows_up",
-    )(far(slot), far(sizes), far(vectors), far(basis), far(trans), far(near))
+    )(far(slot), far(sizes), far(vectors), far(basis), far(trans), far(near), far(upper))
 
 
 def fields_kernel(
@@ -316,8 +324,7 @@
     m0_ref[R : 2 * R] = trans_ref[0].T
     w1 = upper_ref[0]
     w12 = dot3(w1, upper_ref[1])
-    a1_ref[:, 0:R] = w1
-    a1_ref[:, R : 2 * R] = w12
+    a1_ref[...] = w1
     m1_ref[0:R] = side(1).T
     m1_ref[R : 2 * R] = dot3(w1, side(2)).T
     m1_ref[2 * R : 3 * R] = w12.T
@@ -334,18 +341,16 @@
     side2_ref[...] = side(2).T
 
 
-def after_core_kernel(me, pay_ref, got_ref, a1_ref, pair2_ref, lift3_ref):
+def after_core_kernel(me, pay_ref, got_ref, a1_ref, pair2_ref):
     start = pl.multiple_of((me[0] % 2) * HALF, HALF)
     c1 = pay_ref[1, pl.ds(start, HALF), :] + got_ref[1, pl.ds(start, HALF), :]
-    x = dot3(c1, a1_ref[...])
     pair2_ref[0] = c1
-    pair2_ref[1] = x[:, 0:R]
-    lift3_ref[...] = x[:, R : 2 * R]
+    pair2_ref[1] = dot3(c1, a1_ref[...])
 
 
 def after_y_kernel(me, got_ref, a2_ref, send_ref, c3_ref):
     c3 = got_ref[0:QUART]
-    for n in range(1, 4):
+    for n in range(1, 8):
         c3 = c3 + got_ref[n * QUART : (n + 1) * QUART]
     c3_ref[...] = c3
     x = dot3(c3, a2_ref[...])
@@ -374,10 +379,10 @@
     z[...] = jnp.zeros((V, R), F32)
     start = pl.multiple_of((dev % 2) * HALF, HALF)
     z[pl.ds(start, HALF), :] = 0.5 * (c2_ref[...] * dot3(quad_got_ref[...], side2_ref[...]))
-    at = pl.multiple_of(start + ((dev // 2) % 4) * QUART, QUART)
+    at = pl.multiple_of((dev % 8) * QUART, QUART)
     z[pl.ds(at, QUART), :] += c3_ref[...] * inc3
     share = lane_rows(local_ref[...] + row_sums(z[...]))
-    for n in range(4):
+    for n in range(8):
         send_ref[n, 0:QUART] = inc3
         send_ref[n, QUART : QUART + 8] = share
 
@@ -386,27 +391,26 @@
     c2_ref[...] = pair2_ref[1] + got_ref[1]
 
 
-def to_core_kernel(got_ref, pair_got_ref, quad_got_ref, m1_ref, out_ref):
-    inc3 = jnp.concatenate([got_ref[n, 0:QUART] for n in range(4)], axis=0)
-    sums = jnp.concatenate([pair_got_ref[0], quad_got_ref[...], inc3], axis=1)
-    out_ref[0:HALF] = dot3(sums, m1_ref[...])
+def pair_field_kernel(pair_got_ref, quad_got_ref, m1_ref, out_ref):
+    sums = jnp.concatenate([pair_got_ref[0], quad_got_ref[...]], axis=1)
+    out_ref[...] = dot3(sums, m1_ref[0 : 2 * R])
+
+
+def part_share_kernel(got_ref, send_ref):
     share = got_ref[0, QUART : QUART + 8]
-    for n in range(1, 4):
+    for n in range(1, 8):
         share = share + got_ref[n, QUART : QUART + 8]
-    out_ref[HALF : HALF + 8] = share
-
-
-def core_share_kernel(own_ref, other_ref, send_ref):
-    total = own_ref[HALF : HALF + 8] + other_ref[HALF : HALF + 8]
     for n in range(16):
-        send_ref[n] = total
+        send_ref[n] = share
 
 
 def all_share_kernel(got_ref, out_ref):
     total = got_ref[0]
     for n in range(1, 16):
         total = total + got_ref[n]
-    out_ref[...] = total * (1.0 / (2.0 * LEAF))
+    total = total * (1.0 / (2.0 * LEAF))
+    for k in range(3):
+        out_ref[128 * k : 128 * k + 128] = total[k]
 
 
 def small(body, outs, name, flops, scratch=(), hbm_args=()):
@@ -434,7 +438,7 @@
 
 def rows_down_kernel(
     me, slot_hbm, sizes_hbm, basis_hbm, part_hbm, local_hbm, tmat_hbm,
-    own_ref, other_ref, got_ref, m0_ref, out_hbm,
+    own_ref, other_ref, inc3_ref, got_ref, m0_ref, m1_ref, out_hbm,
     slot, sizes, basis, part, local_ref, tmat_ref, ot, pt, res, inct, sem, psem, osem,
 ):
     copies = [
@@ -452,9 +456,11 @@
     for c in loads:
         c.start()
     half = me[0] % 2
-    inct[pl.ds(pl.multiple_of(half * HALF, HALF), HALF), :] = own_ref[0:HALF]
-    inct[pl.ds(pl.multiple_of((1 - half) * HALF, HALF), HALF), :] = other_ref[0:HALF]
-    root = dot3(jnp.concatenate([got_ref[0], inct[...]], axis=1), m0_ref[...])
+    inct[pl.ds(pl.multiple_of(half * HALF, HALF), HALF), :] = own_ref[...]
+    inct[pl.ds(pl.multiple_of((1 - half) * HALF, HALF), HALF), :] = other_ref[...]
+    inc3 = jnp.concatenate([inc3_ref[n, 0:QUART] for n in range(8)], axis=0)
+    inc1 = inct[...] + dot3(inc3, m1_ref[2 * R : 3 * R])
+    root = dot3(jnp.concatenate([got_ref[0], inc1], axis=1), m0_ref[...])
     rsplit = split(root.T)
     for c in copies:
         c.wait()
@@ -464,6 +470,13 @@
     for c in loads:
         c.wait()
     lane_row = lax.broadcasted_iota(jnp.int32, (8, 128), 0)
+
+    def place(leaf, first, last):
+        for base in range(leaf * LEAF + first, leaf * LEAF + last, BT):
+            rows = [ot[at * S : at * S + S, :] for at in range(base, base + BT)]
+            for r in range(BT):
+                pt[tile_rows(slot[base + r], 1), :] = rows[r]
+
     for leaf in range(NL):
         size = sizes[0, leaf]
         for blk in range(LEAF // 128):
@@ -475,26 +488,9 @@
                     ot[pl.ds((leaf * LEAF + 128 * blk + 8 * b) * S + k, 8, stride=S), :] = jnp.where(
                         keep, val[8 * b : 8 * b + 8, 128 * k : 128 * k + 128], 0.0
                     )
-    zero = jnp.zeros((S, 128), F32)
-    for leaf in range(NL):
-        steps = (sizes[0, leaf] + UN - 1) // UN
-
-        def place(i, _, leaf=leaf):
-            base = pl.multiple_of(leaf * LEAF + i * UN, UN)
-            rows = [ot[tile_rows(base + r, 1), :] for r in range(UN)]
-            for r in range(UN):
-                pt[tile_rows(slot[base + r], 1), :] = rows[r]
-            return 0
-
-        lax.fori_loop(0, steps, place, 0)
-
-        def blank(i, _, leaf=leaf):
-            base = pl.multiple_of(leaf * LEAF + i * UN, UN)
-            for r in range(UN):
-                pt[tile_rows(slot[base + r], 1), :] = zero
-            return 0
-
-        lax.fori_loop(steps, LEAF // UN, blank, 0)
+            if leaf > 0:
+                place(leaf - 1, 128 * blk, 128 * blk + 128)
+    place(NL - 1, 0, LEAF)
     stores = []
     for c in range(NL):
 
@@ -573,7 +569,7 @@
     )
     a1, a2, m0, m1, m3, side2 = small(
         chains_kernel,
-        [(R, 2 * R), (R, 3 * R), (2 * R, R), (3 * R, R), (4 * R, R), (R, R)],
+        [(R, R), (R, 3 * R), (2 * R, R), (3 * R, R), (4 * R, R), (R, R)],
         "chains",
         10**8,
         [
@@ -584,14 +580,12 @@
         ],
         (1, 2, 3),
     )(me, far(trans), far(upper), far(pairs))
-    part, call, pay, curv = rows_up(
-        slot_frame, leaf_sizes, vectors, leaf_basis, trans, near_field
+    part, call, pay, curv, lift3 = rows_up(
+        slot_frame, leaf_sizes, vectors, leaf_basis, trans, near_field, upper
     )
     core_got = swap(pay, 0)
-    pair2, lift3 = small(after_core_kernel, [(2, HALF, R), (HALF, R)], "after_core", 10**8)(
-        me, pay, core_got, a1
-    )
-    y_got = exchange(lift3, (1, 2))
+    y_got = exchange(lift3, (0, 1, 2))
+    (pair2,) = small(after_core_kernel, [(2, HALF, R)], "after_core", 10**8)(me, pay, core_got, a1)
     pair_got = swap(pair2, 1)
     top_send, c3 = small(after_y_kernel, [(16 * QUART, R), (QUART, R)], "after_y", 10**8)(
         me, y_got, a2
@@ -602,21 +596,20 @@
     local, tmat, curv = fields(
         me, call, trans, coup, pay, core_got, pair2, pair_got, c2, m0, m1, curv
     )
+    (field1,) = small(pair_field_kernel, [(HALF, R)], "pair_field", 10**8)(pair_got, quad_got, m1)
+    field1_got = swap(field1, 0)
     (inc3,) = small(
-        after_top_kernel, [(4, QUART + 8, R)], "after_top", 10**8, [pltpu.VMEM((V, R), F32)]
+        after_top_kernel, [(8, QUART + 8, R)], "after_top", 10**8, [pltpu.VMEM((V, R), F32)]
     )(me, top_got, m3, side2, c2, quad_got, c3, curv)
-    inc3_got = exchange(inc3, (1, 2))
-    (inc1,) = small(to_core_kernel, [(HALF + 8, R)], "to_core", 10**8)(
-        inc3_got, pair_got, quad_got, m1
-    )
-    inc1_got = swap(inc1, 0)
-    (share,) = small(core_share_kernel, [(16, 8, R)], "core_share", 10**5)(inc1, inc1_got)
+    inc3_got = exchange(inc3, (0, 1, 2))
+    (share,) = small(part_share_kernel, [(16, 8, R)], "part_share", 10**5)(inc3_got)
     share = exchange(share, (3, 4, 5, 6))
     products = rows_down(
-        me, slot_frame, leaf_sizes, leaf_basis, part, local, tmat, inc1, inc1_got, core_got, m0
-    )
-    (curvature,) = small(all_share_kernel, [(8, R)], "all_share", 10**5)(share)
-    return products, curvature[0:3].reshape(V)
+        me, slot_frame, leaf_sizes, leaf_basis, part, local, tmat,
+        field1, field1_got, inc3_got, core_got, m0, m1,
+    )
+    (curvature,) = small(all_share_kernel, [(V,)], "all_share", 10**5)(share)
+    return products, curvature
 
 
 def solution(mesh):

time: 86.5 us -> 84 us (0.971)
  blocking collectives: 7.14 us -> 0 us
  waiting for transfers between devices: 5.3 us -> 10.4 us
    all_to_all x1 -> x0, blocking collectives: 7.14 us -> none  [exchange(): lax.all_to_all(value, 'leaf', 0, 0, axis_index_groups=groups_of(bits, cou...]
    all_to_all x3 -> x4, waiting for transfers between devices: 4.34 us -> 10.3 us  [exchange(): lax.all_to_all(value, 'leaf', 0, 0, axis_index_groups=groups_of(bits, cou...]
    ppermute x4, starting transfers between devices: 8.72 us -> 3.84 us  [swap(): lax.ppermute(value, 'leaf', [(s, s ^ 1 << level) for s in range(count)])]
    all_to_all x3 -> x4, starting transfers between devices: 17.9 us -> 22.7 us  [exchange(): lax.all_to_all(value, 'leaf', 0, 0, axis_index_groups=groups_of(bits, cou...]
    pallas_call x1, Pallas kernels: 14.9 us -> 13.9 us  [rows_down(): pl.pallas_call(rows_down_kernel, out_shape=pltpu.HBM((ROWS, V), F32), in_...]
    ppermute x4, waiting for transfers between devices: 0.96 us -> 0.01 us  [swap(): lax.ppermute(value, 'leaf', [(s, s ^ 1 << level) for s in range(count)])]
  transfers between devices with their start and end apart: 7 -> 8, of which waited for: 3 -> 3; matrix products, arithmetic and copies ran while one was open for 0% -> 0% of each run, Pallas kernels for 28% -> 29%
where the time goes in v4:
time: 84 us; the launch traced here: 83.3 us
  Pallas kernels  45.7 us (54%)
  starting transfers between devices  26.5 us (32%)
  waiting for transfers between devices  10.4 us (12%)
    all_to_all x4, starting transfers between devices, exchange(): lax.all_to_all(value, 'leaf', 0, 0, axis_index_groups=groups_of(bits, cou...  22.7 us
    pallas_call x1, Pallas kernels, rows_up(): pl.pallas_call(rows_up_kernel, out_shape=(pltpu.HBM((NL, LEAF, V), F32),...  19.9 us
    pallas_call x1, Pallas kernels, rows_down(): pl.pallas_call(rows_down_kernel, out_shape=pltpu.HBM((ROWS, V), F32), in_...  13.9 us
    all_to_all x4, waiting for transfers between devices, exchange(): lax.all_to_all(value, 'leaf', 0, 0, axis_index_groups=groups_of(bits, cou...  10.3 us
    pallas_call x1, Pallas kernels, fields(): pl.pallas_call(fields_kernel, out_shape=(pltpu.HBM((NL, R, V), F32), pltp...  6.13 us
    pallas_call x8, Pallas kernels, call(): pl.pallas_call(body, out_shape=tuple((jax.ShapeDtypeStruct(o, F32) for o...  5.76 us
    ppermute x4, starting transfers between devices, swap(): lax.ppermute(value, 'leaf', [(s, s ^ 1 << level) for s in range(count)])  3.84 us
  transfers between devices with their start and end apart: 8, of which 3 were waited for; matrix products, arithmetic and copies ran while one was open for 0% of the time, Pallas kernels for 29%

profile of v4, /device:TPU:1, one launch (start us, length us, event | category | flops | bytes accessed | tf_op | source)
XLA Modules:
  0.0 83.3 jit_solution(16504702600797045027)
XLA Ops:
  0.6 19.9 %rows_up.1 = (f32[8,512,384]{2,1,0:T(8,128)}, f32[14,128,384]{2,1,0:T(8,128)}, f32[2,384,128]{2,1,0:T(8,128)S(1)}, f32[8,384]{1,0:T(8,128)S(1)}, f32[384,128]{1,0:T(8,128)}) custom-call(s32[4096]{0:T(1024)} %slot_hbm.3, s32[1,8]{1,0:T(1,128)} %sizes_hbm.3, f32[4096,384]{1,0:T(8,128)} %v_hbm.1, f32[8,512,128]{2,1,0:T(8,128)} %basis_hbm.3, ...), custom_call_target="tpu_custom_call" | custom-call | flops 7000000000 | bytes 28000000 | tf_op jit(solution)/shard_map/rows_up/pallas_call | solution.py:200
  20.5 1.7 %collective-permute-start = (f32[2,384,128]{2,1,0:T(8,128)S(1)}, f32[2,384,128]{2,1,0:T(8,128)S(1)}, u32[]{:S(2)}, u32[]{:S(2)}) collective-permute-start(f32[2,384,128]{2,1,0:T(8,128)S(1)} %get-tuple-element.20.pay_ref), channel_id=1, source_target_pairs={{0,1},{1,0},{2,3},{3,2},{4,5},{5,4},{6,7},{7,6},{8,9},{9,8},{10,11... | collective-permute-start | bytes 1179656 | tf_op jit(solution)/shard_map/ppermute | solution.py:560
  22.2 4.7 %all-to-all-start = ((f32[8,48,128]{2,1,0:T(8,128)}), f32[8,48,128]{2,1,0:T(8,128)S(1)}, u32[]{:S(2)}, u32[]{:S(2)}) async-start(f32[8,48,128]{2,1,0:T(8,128)} %bitcast.5), calls=%async_computation | async-start | bytes 393216 | tf_op jit(solution)/shard_map/all_to_all | solution.py:563
  26.9 1.9 %chains.1 = (f32[128,128]{1,0:T(8,128)S(1)}, f32[128,384]{1,0:T(8,128)S(1)}, f32[256,128]{1,0:T(8,128)S(1)}, f32[384,128]{1,0:T(8,128)S(1)}, f32[512,128]{1,0:T(8,128)S(1)}, /*index=5*/f32[128,128]{1,0:T(8,128)S(1)}) custom-call(s32[1]{0:T(128)} %bitcast.me, f32[15,128,128]{2,1,0:T(8,128)} %bitcast.12, f32[5,128,128]{2,1,0:T(8,128)} %bitcast.16, ...), custom_call_target="tpu_custom_call" | custom-call | flops 100000000 | bytes 1000000 | tf_op jit(solution)/shard_map/chains/pallas_call | solution.py:422
  28.7 0.0 collective-permute-done.got_ref
  28.7 0.2 after_core.1.pair2_ref
  28.9 1.5 %collective-permute-start.1 = (f32[2,192,128]{2,1,0:T(8,128)S(1)}, f32[2,192,128]{2,1,0:T(8,128)S(1)}, u32[]{:S(2)}, u32[]{:S(2)}) collective-permute-start(f32[2,192,128]{2,1,0:T(8,128)S(1)} %after_core.1.pair2_ref), channel_id=1, source_target_pairs={{0,2},{1,3},{2,0},{3,1},{4,6},{5,7},{6,4},{7,5},{8,10},{9,11},{10,... | collective-permute-start | bytes 589832 | tf_op jit(solution)/shard_map/ppermute | solution.py:560
  30.4 2.4 %all-to-all-done = f32[8,48,128]{2,1,0:T(8,128)S(1)} async-done(((f32[8,48,128]{2,1,0:T(8,128)}), f32[8,48,128]{2,1,0:T(8,128)S(1)}, u32[]{:S(2)}, u32[]{:S(2)}) %all-to-all-start) | async-done | bytes 196640 | tf_op jit(solution)/shard_map/all_to_all | solution.py:563
  32.8 1.0 %after_y.1 = (f32[768,128]{1,0:T(8,128)}, f32[48,128]{1,0:T(8,128)S(1)}) custom-call(s32[1]{0:T(128)} %bitcast.me, f32[384,128]{1,0:T(8,128)S(1)} %bitcast.10, f32[128,384]{1,0:T(8,128)S(1)} %get-tuple-element.28.a2_ref), custom_call_target="tpu_custom_call" | custom-call | flops 100000000 | bytes 1000000 | tf_op jit(solution)/shard_map/after_y/pallas_call | solution.py:422
  33.8 7.6 %all-to-all-start.1 = ((f32[16,48,128]{2,1,0:T(8,128)}), f32[16,48,128]{2,1,0:T(8,128)S(1)}, u32[]{:S(2)}, u32[]{:S(2)}) async-start(f32[16,48,128]{2,1,0:T(8,128)} %bitcast.7), calls=%async_computation.1 | async-start | bytes 786432 | tf_op jit(solution)/shard_map/all_to_all | solution.py:563
  41.4 0.0 collective-permute-done.1.got_ref.pair_got_ref
  41.4 0.5 collective-permute-start.2
  42.0 6.1 %fields.1 = (f32[8,128,384]{2,1,0:T(8,128)}, f32[8,128,128]{2,1,0:T(8,128)}, f32[8,384]{1,0:T(8,128)S(1)}) custom-call(s32[1]{0:T(128)} %bitcast.me, f32[14,128,384]{2,1,0:T(8,128)} %get-tuple-element.19.call_hbm, f32[15,128,128]{2,1,0:T(8,128)} %bitcast.13, f32[7,128,128]{2,1,0:T(8,128)} %bitcast.17, f32[2,384,128]{2,1,0:T(8,128)S(1)} %get-tuple-element.20.pay_ref, ...), custom_call_target="tpu_custom_call" | custom-call | flops 2000000000 | bytes 8000000 | tf_op jit(solution)/shard_map/fields/pallas_call | solution.py:282
  48.1 2.2 %all-to-all-done.1 = f32[16,48,128]{2,1,0:T(8,128)S(1)} async-done(((f32[16,48,128]{2,1,0:T(8,128)}), f32[16,48,128]{2,1,0:T(8,128)S(1)}, u32[]{:S(2)}, u32[]{:S(2)}) %all-to-all-start.1) | async-done | bytes 393248 | tf_op jit(solution)/shard_map/all_to_all | solution.py:563
  50.3 0.0 collective-permute-done.2.quad_got_ref
  50.3 1.3 %after_top.1 = f32[8,56,128]{2,1,0:T(8,128)} custom-call(s32[1]{0:T(128)} %bitcast.me, f32[768,128]{1,0:T(8,128)S(1)} %bitcast.9, f32[512,128]{1,0:T(8,128)S(1)} %get-tuple-element.30.m3_ref, f32[128,128]{1,0:T(8,128)S(1)} %get-tuple-element.31.side2_ref, f32[192,128]{1,0:T(8,128)S(1)} %after_pair.1.c2_ref, ...), custom_call_target="tpu_custom_call" | custom-call | flops 100000000 | bytes 1000000 | tf_op jit(solution)/shard_map/after_top/pallas_call | solution.py:422
  51.6 5.5 %all-to-all-start.2 = ((f32[8,56,128]{2,1,0:T(8,128)}), f32[8,56,128]{2,1,0:T(8,128)S(1)}, u32[]{:S(2)}, u32[]{:S(2)}) async-start(f32[8,56,128]{2,1,0:T(8,128)} %after_top.1), calls=%async_computation.2 | async-start | bytes 458752 | tf_op jit(solution)/shard_map/all_to_all | solution.py:563
  57.0 0.2 pair_field.1.own_ref
  57.3 0.2 collective-permute-start.3
  57.4 5.8 %all-to-all-done.2.inc3_ref.got_ref = f32[8,56,128]{2,1,0:T(8,128)S(1)} async-done(((f32[8,56,128]{2,1,0:T(8,128)}), f32[8,56,128]{2,1,0:T(8,128)S(1)}, u32[]{:S(2)}, u32[]{:S(2)}) %all-to-all-start.2) | async-done | bytes 229408 | tf_op jit(solution)/shard_map/all_to_all | solution.py:563
  63.2 0.6 part_share.1
  63.9 4.9 %all-to-all-start.3 = ((f32[16,8,128]{2,1,0:T(8,128)}), f32[16,8,128]{2,1,0:T(8,128)S(1)}, u32[]{:S(2)}, u32[]{:S(2)}) async-start(f32[16,8,128]{2,1,0:T(8,128)} %part_share.1), calls=%async_computation.3 | async-start | bytes 131072 | tf_op jit(solution)/shard_map/all_to_all | solution.py:563
  68.8 0.0 collective-permute-done.3.other_ref
  68.8 13.9 %rows_down.1 = f32[4096,384]{1,0:T(8,128)} custom-call(s32[1]{0:T(128)} %bitcast.me, s32[4096]{0:T(1024)} %slot_hbm.3, s32[1,8]{1,0:T(1,128)} %sizes_hbm.3, f32[8,512,128]{2,1,0:T(8,128)} %basis_hbm.3, f32[8,512,384]{2,1,0:T(8,128)} %get-tuple-element.18.part_hbm, f32[8,128,384]{2,1,0:T(8,128)} %get-tuple-element.25.local_hbm, ...), custom_call_target="tpu_custom_call" | custom-call | flops 2000000000 | bytes 16000000 | tf_op jit(solution)/shard_map/rows_down/pallas_call | solution.py:520
  82.7 0.0 all-to-all-done.3.got_ref
  82.7 0.6 all_share.1
  (1 shorter events, 0.0 us)
Async XLA Ops:
  20.5 8.2 %collective-permute-start = (f32[2,384,128]{2,1,0:T(8,128)S(1)}, f32[2,384,128]{2,1,0:T(8,128)S(1)}, u32[]{:S(2)}, u32[]{:S(2)}) collective-permute-start(f32[2,384,128]{2,1,0:T(8,128)S(1)} %get-tuple-element.20.pay_ref), channel_id=1, source_target_pairs={{0,1},{1,0},{2,3},{3,2},{4,5},{5,4},{6,7},{7,6},{8,9},{9,8},{10,11... | collective-permute-start | bytes 1179656 | tf_op jit(solution)/shard_map/ppermute | solution.py:560
  22.2 10.6 %all-to-all-start = ((f32[8,48,128]{2,1,0:T(8,128)}), f32[8,48,128]{2,1,0:T(8,128)S(1)}, u32[]{:S(2)}, u32[]{:S(2)}) async-start(f32[8,48,128]{2,1,0:T(8,128)} %bitcast.5), calls=%async_computation | async-start | bytes 393216 | tf_op jit(solution)/shard_map/all_to_all | solution.py:563
  28.9 12.5 %collective-permute-start.1 = (f32[2,192,128]{2,1,0:T(8,128)S(1)}, f32[2,192,128]{2,1,0:T(8,128)S(1)}, u32[]{:S(2)}, u32[]{:S(2)}) collective-permute-start(f32[2,192,128]{2,1,0:T(8,128)S(1)} %after_core.1.pair2_ref), channel_id=1, source_target_pairs={{0,2},{1,3},{2,0},{3,1},{4,6},{5,7},{6,4},{7,5},{8,10},{9,11},{10,... | collective-permute-start | bytes 589832 | tf_op jit(solution)/shard_map/ppermute | solution.py:560
  33.8 16.5 %all-to-all-start.1 = ((f32[16,48,128]{2,1,0:T(8,128)}), f32[16,48,128]{2,1,0:T(8,128)S(1)}, u32[]{:S(2)}, u32[]{:S(2)}) async-start(f32[16,48,128]{2,1,0:T(8,128)} %bitcast.7), calls=%async_computation.1 | async-start | bytes 786432 | tf_op jit(solution)/shard_map/all_to_all | solution.py:563
  41.4 8.9 %collective-permute-start.2 = (f32[192,128]{1,0:T(8,128)S(1)}, f32[192,128]{1,0:T(8,128)S(1)}, u32[]{:S(2)}, u32[]{:S(2)}) collective-permute-start(f32[192,128]{1,0:T(8,128)S(1)} %after_pair.1.c2_ref), channel_id=1, source_target_pairs={{0,4},{1,5},{2,6},{3,7},{4,0},{5,1},{6,2},{7,3},{8,12},{9,13},{10,... | collective-permute-start | bytes 294920 | tf_op jit(solution)/shard_map/ppermute | solution.py:560
  51.6 11.7 %all-to-all-start.2 = ((f32[8,56,128]{2,1,0:T(8,128)}), f32[8,56,128]{2,1,0:T(8,128)S(1)}, u32[]{:S(2)}, u32[]{:S(2)}) async-start(f32[8,56,128]{2,1,0:T(8,128)} %after_top.1), calls=%async_computation.2 | async-start | bytes 458752 | tf_op jit(solution)/shard_map/all_to_all | solution.py:563
  57.3 11.5 %collective-permute-start.3 = (f32[192,128]{1,0:T(8,128)S(1)}, f32[192,128]{1,0:T(8,128)S(1)}, u32[]{:S(2)}, u32[]{:S(2)}) collective-permute-start(f32[192,128]{1,0:T(8,128)S(1)} %pair_field.1.own_ref), channel_id=1, source_target_pairs={{0,1},{1,0},{2,3},{3,2},{4,5},{5,4},{6,7},{7,6},{8,9},{9,8},{10,11... | collective-permute-start | bytes 294920 | tf_op jit(solution)/shard_map/ppermute | solution.py:560
  63.9 18.9 %all-to-all-start.3 = ((f32[16,8,128]{2,1,0:T(8,128)}), f32[16,8,128]{2,1,0:T(8,128)S(1)}, u32[]{:S(2)}, u32[]{:S(2)}) async-start(f32[16,8,128]{2,1,0:T(8,128)} %part_share.1), calls=%async_computation.3 | async-start | bytes 131072 | tf_op jit(solution)/shard_map/all_to_all | solution.py:563

commit v5 on v4

--- a/solution.py
+++ b/solution.py
@@ -233,14 +233,13 @@
 
 
 def fields_kernel(
-    me, call_hbm, trans_hbm, coup_hbm,
+    me, call_hbm, coup_hbm,
     pay_ref, got_ref, pair2_ref, pair_got_ref, c2_ref, m0_ref, m1_ref, near_ref,
-    inc_ref, tmat_ref, curv_ref, call_ref, trans_ref, coup_ref, z, sem,
+    field_hbm, curv_ref, call_ref, coup_ref, field_ref, z, sem,
 ):
     copies = [
         pltpu.make_async_copy(call_hbm, call_ref, sem.at[0]),
-        pltpu.make_async_copy(trans_hbm, trans_ref, sem.at[1]),
-        pltpu.make_async_copy(coup_hbm, coup_ref, sem.at[2]),
+        pltpu.make_async_copy(coup_hbm, coup_ref, sem.at[1]),
     ]
     for c in copies:
         c.start()
@@ -251,54 +250,97 @@
         c.wait()
     total = jnp.zeros((1, V), F32)
     starts = (0, 8, 12)
-    fields = [None] * 14
     pair = 0
+    outs = []
     for height in range(3):
         for m in range(4 >> height):
             a = starts[height] + 2 * m
             bm = split(coup_ref[pair])
             ca, cb = call_ref[a], call_ref[a + 1]
-            fields[a] = dot3s([(bm, split(cb))], 1, 0)
-            fields[a + 1] = dot3s([(bm, split(ca))], 0, 0)
-            total += 2.0 * jnp.sum(ca * fields[a], axis=0, keepdims=True)
+            left = dot3s([(bm, split(cb))], 1, 0)
+            field_ref[a] = left
+            field_ref[a + 1] = dot3s([(bm, split(ca))], 0, 0)
+            total += 2.0 * jnp.sum(ca * left, axis=0, keepdims=True)
             pair += 1
+        if height != 1:
+            cp = pltpu.make_async_copy(
+                field_ref.at[pl.ds(0, 8) if height == 0 else pl.ds(8, 6)],
+                field_hbm.at[pl.ds(0, 8) if height == 0 else pl.ds(8, 6)],
+                sem.at[2 + height // 2],
+            )
+            cp.start()
+            outs.append(cp)
     curv_ref[...] = near_ref[...] + row_sums(z[...]) + jnp.broadcast_to(total, (8, V))
-    top = [split(fields[12 + m]) for m in range(2)]
-    tops = [split(trans_ref[12 + m]) for m in range(2)]
-    for m in range(4):
-        w = split(trans_ref[8 + m])
-        mid = split(fields[8 + m] + dot3s([(w, top[m // 2])], 1, 0))
-        tmid = split(dot3s([(w, tops[m // 2])], 1, 0))
-        for n in (2 * m, 2 * m + 1):
-            wl = split(trans_ref[n])
-            inc_ref[n] = fields[n] + dot3s([(wl, mid)], 1, 0)
-            tmat_ref[n] = dot3s([(wl, tmid)], 1, 0)
-
-
-def fields(me, call, trans, coup, *rest):
+    for cp in outs:
+        cp.wait()
+
+
+def fields(me, call, coup, *rest):
     vmem = pl.BlockSpec(memory_space=pltpu.VMEM)
     hbm = pl.BlockSpec(memory_space=pltpu.HBM)
     smem = pl.BlockSpec(memory_space=pltpu.SMEM)
     return pl.pallas_call(
         fields_kernel,
-        out_shape=(
-            pltpu.HBM((NL, R, V), F32),
-            pltpu.HBM((NL, R, R), F32),
-            jax.ShapeDtypeStruct((8, V), F32),
-        ),
-        in_specs=[smem, hbm, hbm, hbm] + [vmem] * len(rest),
-        out_specs=(vmem, vmem, vmem),
+        out_shape=(pltpu.HBM((14, R, V), F32), jax.ShapeDtypeStruct((8, V), F32)),
+        in_specs=[smem, hbm, hbm] + [vmem] * len(rest),
+        out_specs=(hbm, vmem),
+        scratch_shapes=[
+            pltpu.VMEM((14, R, V), F32),
+            pltpu.VMEM((NL - 1, R, R), F32),
+            pltpu.VMEM((14, R, V), F32),
+            pltpu.VMEM((V, R), F32),
+            pltpu.SemaphoreType.DMA((4,)),
+        ],
+        compiler_params=pltpu.CompilerParams(vmem_limit_bytes=24 * MIB),
+        cost_estimate=pl.CostEstimate(flops=2 * 10**9, bytes_accessed=16 * 10**6, transcendentals=0),
+        name="fields",
+    )(me, far(call), far(coup), *rest)
+
+
+def paths_kernel(field_hbm, trans_hbm, after_ref, inc_hbm, tmat_hbm, field, trans, inc, tmat, sem):
+    copies = [
+        pltpu.make_async_copy(trans_hbm, trans, sem.at[0]),
+        pltpu.make_async_copy(field_hbm, field, sem.at[1]),
+    ]
+    for c in copies:
+        c.start()
+    copies[0].wait()
+    tops = [split(trans[12 + m]) for m in range(2)]
+    for m in range(4):
+        tmid = split(dot3s([(split(trans[8 + m]), tops[m // 2])], 1, 0))
+        for n in (2 * m, 2 * m + 1):
+            tmat[n] = dot3s([(split(trans[n]), tmid)], 1, 0)
+    outs = [pltpu.make_async_copy(tmat, tmat_hbm, sem.at[2]), pltpu.make_async_copy(inc, inc_hbm, sem.at[3])]
+    outs[0].start()
+    copies[1].wait()
+    top = [split(field[12 + m]) for m in range(2)]
+    for m in range(4):
+        mid = split(field[8 + m] + dot3s([(split(trans[8 + m]), top[m // 2])], 1, 0))
+        for n in (2 * m, 2 * m + 1):
+            inc[n] = field[n] + dot3s([(split(trans[n]), mid)], 1, 0)
+    outs[1].start()
+    for cp in outs:
+        cp.wait()
+
+
+def paths(field, trans, after):
+    hbm = pl.BlockSpec(memory_space=pltpu.HBM)
+    return pl.pallas_call(
+        paths_kernel,
+        out_shape=(pltpu.HBM((NL, R, V), F32), pltpu.HBM((NL, R, R), F32)),
+        in_specs=[hbm, hbm, pl.BlockSpec(memory_space=pl.ANY)],
+        out_specs=(hbm, hbm),
         scratch_shapes=[
             pltpu.VMEM((14, R, V), F32),
             pltpu.VMEM((2 * NL - 1, R, R), F32),
-            pltpu.VMEM((NL - 1, R, R), F32),
-            pltpu.VMEM((V, R), F32),
-            pltpu.SemaphoreType.DMA((3,)),
+            pltpu.VMEM((NL, R, V), F32),
+            pltpu.VMEM((NL, R, R), F32),
+            pltpu.SemaphoreType.DMA((4,)),
         ],
         compiler_params=pltpu.CompilerParams(vmem_limit_bytes=24 * MIB),
-        cost_estimate=pl.CostEstimate(flops=2 * 10**9, bytes_accessed=8 * 10**6, transcendentals=0),
-        name="fields",
-    )(me, far(call), far(trans), far(coup), *rest)
+        cost_estimate=pl.CostEstimate(flops=10**9, bytes_accessed=6 * 10**6, transcendentals=0),
+        name="paths",
+    )(far(field), far(trans), after)
 
 
 def chains_kernel(
@@ -348,7 +390,7 @@
     pair2_ref[1] = dot3(c1, a1_ref[...])
 
 
-def after_y_kernel(me, got_ref, a2_ref, send_ref, c3_ref):
+def after_y_kernel(me, got_ref, a2_ref, pair2_ref, send_ref, c3_ref):
     c3 = got_ref[0:QUART]
     for n in range(1, 8):
         c3 = c3 + got_ref[n * QUART : (n + 1) * QUART]
@@ -588,20 +630,19 @@
     (pair2,) = small(after_core_kernel, [(2, HALF, R)], "after_core", 10**8)(me, pay, core_got, a1)
     pair_got = swap(pair2, 1)
     top_send, c3 = small(after_y_kernel, [(16 * QUART, R), (QUART, R)], "after_y", 10**8)(
-        me, y_got, a2
+        me, y_got, a2, pair2
     )
     top_got = exchange(top_send, (3, 4, 5, 6))
     (c2,) = small(after_pair_kernel, [(HALF, R)], "after_pair", 10**6)(pair2, pair_got)
     quad_got = swap(c2, 2)
-    local, tmat, curv = fields(
-        me, call, trans, coup, pay, core_got, pair2, pair_got, c2, m0, m1, curv
-    )
+    field, curv = fields(me, call, coup, pay, core_got, pair2, pair_got, c2, m0, m1, curv)
     (field1,) = small(pair_field_kernel, [(HALF, R)], "pair_field", 10**8)(pair_got, quad_got, m1)
     field1_got = swap(field1, 0)
     (inc3,) = small(
         after_top_kernel, [(8, QUART + 8, R)], "after_top", 10**8, [pltpu.VMEM((V, R), F32)]
     )(me, top_got, m3, side2, c2, quad_got, c3, curv)
     inc3_got = exchange(inc3, (0, 1, 2))
+    local, tmat = paths(field, trans, field1)
     (share,) = small(part_share_kernel, [(16, 8, R)], "part_share", 10**5)(inc3_got)
     share = exchange(share, (3, 4, 5, 6))
     products = rows_down(

time: 84 us -> 82.6 us (0.983)
  waiting for transfers between devices: 10.4 us -> 7.39 us
  Pallas kernels: 45.7 us -> 48.7 us
  starting transfers between devices: 26.5 us -> 25.3 us
    all_to_all x4, waiting for transfers between devices: 10.3 us -> 7.03 us  [exchange(): lax.all_to_all(value, 'leaf', 0, 0, axis_index_groups=groups_of(bits, cou...]
    pallas_call x1 -> x2, Pallas kernels: 6.13 us -> 9.08 us  [the longest x1 4.92 us: paths(): pl.pallas_call(paths_kernel, out_shape=(pltpu.HBM((NL, R, V), F32), pltpu...]
    all_to_all x4, starting transfers between devices: 22.7 us -> 21.4 us  [exchange(): lax.all_to_all(value, 'leaf', 0, 0, axis_index_groups=groups_of(bits, cou...]
  transfers between devices with their start and end apart: 8 -> 8, of which waited for: 3 -> 4; matrix products, arithmetic and copies ran while one was open for 0% -> 0% of each run, Pallas kernels for 29% -> 33%
where the time goes in v5:
time: 82.6 us; the launch traced here: 82.1 us
  Pallas kernels  48.7 us (59%)
  starting transfers between devices  25.3 us (31%)
  waiting for transfers between devices  7.39 us (9%)
    all_to_all x4, starting transfers between devices, exchange(): lax.all_to_all(value, 'leaf', 0, 0, axis_index_groups=groups_of(bits, cou...  21.4 us
    pallas_call x1, Pallas kernels, rows_up(): pl.pallas_call(rows_up_kernel, out_shape=(pltpu.HBM((NL, LEAF, V), F32),...  19.9 us
    pallas_call x1, Pallas kernels, rows_down(): pl.pallas_call(rows_down_kernel, out_shape=pltpu.HBM((ROWS, V), F32), in_...  13.9 us
    all_to_all x4, waiting for transfers between devices, exchange(): lax.all_to_all(value, 'leaf', 0, 0, axis_index_groups=groups_of(bits, cou...  7.03 us
    pallas_call x8, Pallas kernels, call(): pl.pallas_call(body, out_shape=tuple((jax.ShapeDtypeStruct(o, F32) for o...  5.76 us
    pallas_call x1, Pallas kernels, paths(): pl.pallas_call(paths_kernel, out_shape=(pltpu.HBM((NL, R, V), F32), pltpu...  4.92 us
    pallas_call x1, Pallas kernels, fields(): pl.pallas_call(fields_kernel, out_shape=(pltpu.HBM((14, R, V), F32), jax....  4.16 us
    ppermute x4, starting transfers between devices, swap(): lax.ppermute(value, 'leaf', [(s, s ^ 1 << level) for s in range(count)])  3.83 us
  transfers between devices with their start and end apart: 8, of which 4 were waited for; matrix products, arithmetic and copies ran while one was open for 0% of the time, Pallas kernels for 33%

profile of v5, /device:TPU:1, one launch (start us, length us, event | category | flops | bytes accessed | tf_op | source)
XLA Modules:
  0.0 82.1 jit_solution(1315353598020930316)
XLA Ops:
  0.6 19.9 %rows_up.1 = (f32[8,512,384]{2,1,0:T(8,128)}, f32[14,128,384]{2,1,0:T(8,128)}, f32[2,384,128]{2,1,0:T(8,128)S(1)}, f32[8,384]{1,0:T(8,128)S(1)}, f32[384,128]{1,0:T(8,128)}) custom-call(s32[4096]{0:T(1024)} %slot_hbm.3, s32[1,8]{1,0:T(1,128)} %sizes_hbm.3, f32[4096,384]{1,0:T(8,128)} %v_hbm.1, f32[8,512,128]{2,1,0:T(8,128)} %basis_hbm.3, ...), custom_call_target="tpu_custom_call" | custom-call | flops 7000000000 | bytes 28000000 | tf_op jit(solution)/shard_map/rows_up/pallas_call | solution.py:200
  20.6 1.6 %collective-permute-start = (f32[2,384,128]{2,1,0:T(8,128)S(1)}, f32[2,384,128]{2,1,0:T(8,128)S(1)}, u32[]{:S(2)}, u32[]{:S(2)}) collective-permute-start(f32[2,384,128]{2,1,0:T(8,128)S(1)} %get-tuple-element.21.pay_ref), channel_id=1, source_target_pairs={{0,1},{1,0},{2,3},{3,2},{4,5},{5,4},{6,7},{7,6},{8,9},{9,8},{10,11... | collective-permute-start | bytes 1179656 | tf_op jit(solution)/shard_map/ppermute | solution.py:602
  22.2 4.7 %all-to-all-start = ((f32[8,48,128]{2,1,0:T(8,128)}), f32[8,48,128]{2,1,0:T(8,128)S(1)}, u32[]{:S(2)}, u32[]{:S(2)}) async-start(f32[8,48,128]{2,1,0:T(8,128)} %bitcast.5), calls=%async_computation | async-start | bytes 393216 | tf_op jit(solution)/shard_map/all_to_all | solution.py:605
  26.9 1.8 %chains.1 = (f32[128,128]{1,0:T(8,128)S(1)}, f32[128,384]{1,0:T(8,128)S(1)}, f32[256,128]{1,0:T(8,128)S(1)}, f32[384,128]{1,0:T(8,128)S(1)}, f32[512,128]{1,0:T(8,128)S(1)}, /*index=5*/f32[128,128]{1,0:T(8,128)S(1)}) custom-call(s32[1]{0:T(128)} %bitcast.me, f32[15,128,128]{2,1,0:T(8,128)} %bitcast.12, f32[5,128,128]{2,1,0:T(8,128)} %bitcast.16, ...), custom_call_target="tpu_custom_call" | custom-call | flops 100000000 | bytes 1000000 | tf_op jit(solution)/shard_map/chains/pallas_call | solution.py:464
  28.7 0.0 collective-permute-done.got_ref
  28.8 0.2 after_core.1.pair2_ref
  29.0 1.5 %collective-permute-start.1 = (f32[2,192,128]{2,1,0:T(8,128)S(1)}, f32[2,192,128]{2,1,0:T(8,128)S(1)}, u32[]{:S(2)}, u32[]{:S(2)}) collective-permute-start(f32[2,192,128]{2,1,0:T(8,128)S(1)} %after_core.1.pair2_ref), channel_id=1, source_target_pairs={{0,2},{1,3},{2,0},{3,1},{4,6},{5,7},{6,4},{7,5},{8,10},{9,11},{10,... | collective-permute-start | bytes 589832 | tf_op jit(solution)/shard_map/ppermute | solution.py:602
  30.4 2.4 %all-to-all-done = f32[8,48,128]{2,1,0:T(8,128)S(1)} async-done(((f32[8,48,128]{2,1,0:T(8,128)}), f32[8,48,128]{2,1,0:T(8,128)S(1)}, u32[]{:S(2)}, u32[]{:S(2)}) %all-to-all-start) | async-done | bytes 196640 | tf_op jit(solution)/shard_map/all_to_all | solution.py:605
  32.8 1.0 %after_y.1 = (f32[768,128]{1,0:T(8,128)}, f32[48,128]{1,0:T(8,128)S(1)}) custom-call(s32[1]{0:T(128)} %bitcast.me, f32[384,128]{1,0:T(8,128)S(1)} %bitcast.10, f32[128,384]{1,0:T(8,128)S(1)} %get-tuple-element.30.a2_ref, f32[2,192,128]{2,1,0:T(8,128)S(1)} %after_core.1.pair2_ref), custom_call_target="tpu_custom_call" | custom-call | flops 100000000 | bytes 1000000 | tf_op jit(solution)/shard_map/after_y/pallas_call | solution.py:464
  33.8 7.6 %all-to-all-start.1 = ((f32[16,48,128]{2,1,0:T(8,128)}), f32[16,48,128]{2,1,0:T(8,128)S(1)}, u32[]{:S(2)}, u32[]{:S(2)}) async-start(f32[16,48,128]{2,1,0:T(8,128)} %bitcast.7), calls=%async_computation.1 | async-start | bytes 786432 | tf_op jit(solution)/shard_map/all_to_all | solution.py:605
  41.4 0.0 collective-permute-done.1.got_ref.pair_got_ref
  41.4 0.5 collective-permute-start.2
  42.0 4.2 %fields.1 = (f32[14,128,384]{2,1,0:T(8,128)}, f32[8,384]{1,0:T(8,128)S(1)}) custom-call(s32[1]{0:T(128)} %bitcast.me, f32[14,128,384]{2,1,0:T(8,128)} %get-tuple-element.20.call_hbm, f32[7,128,128]{2,1,0:T(8,128)} %bitcast.17, f32[2,384,128]{2,1,0:T(8,128)S(1)} %get-tuple-element.21.pay_ref, f32[2,384,128]{2,1,0:T(8,128)S(1)} %collective-permute-done.got_ref, ...), custom_call_target="tpu_custom_call" | custom-call | flops 2000000000 | bytes 16000000 | tf_op jit(solution)/shard_map/fields/pallas_call | solution.py:282
  46.1 0.4 collective-permute-done.2.quad_got_ref
  46.5 3.8 %all-to-all-done.1 = f32[16,48,128]{2,1,0:T(8,128)S(1)} async-done(((f32[16,48,128]{2,1,0:T(8,128)}), f32[16,48,128]{2,1,0:T(8,128)S(1)}, u32[]{:S(2)}, u32[]{:S(2)}) %all-to-all-start.1) | async-done | bytes 393248 | tf_op jit(solution)/shard_map/all_to_all | solution.py:605
  50.3 1.3 %after_top.1 = f32[8,56,128]{2,1,0:T(8,128)} custom-call(s32[1]{0:T(128)} %bitcast.me, f32[768,128]{1,0:T(8,128)S(1)} %bitcast.9, f32[512,128]{1,0:T(8,128)S(1)} %get-tuple-element.32.m3_ref, f32[128,128]{1,0:T(8,128)S(1)} %get-tuple-element.33.side2_ref, f32[192,128]{1,0:T(8,128)S(1)} %after_pair.1.c2_ref, ...), custom_call_target="tpu_custom_call" | custom-call | flops 100000000 | bytes 1000000 | tf_op jit(solution)/shard_map/after_top/pallas_call | solution.py:464
  51.5 5.5 %all-to-all-start.2 = ((f32[8,56,128]{2,1,0:T(8,128)}), f32[8,56,128]{2,1,0:T(8,128)S(1)}, u32[]{:S(2)}, u32[]{:S(2)}) async-start(f32[8,56,128]{2,1,0:T(8,128)} %after_top.1), calls=%async_computation.2 | async-start | bytes 458752 | tf_op jit(solution)/shard_map/all_to_all | solution.py:605
  57.0 0.2 pair_field.1.after_ref.own_ref
  57.2 0.2 collective-permute-start.3
  57.4 4.9 %paths.1 = (f32[8,128,384]{2,1,0:T(8,128)}, f32[8,128,128]{2,1,0:T(8,128)}) custom-call(f32[14,128,384]{2,1,0:T(8,128)} %get-tuple-element.26.field_hbm, f32[15,128,128]{2,1,0:T(8,128)} %bitcast.13, f32[192,128]{1,0:T(8,128)S(1)} %pair_field.1.after_ref.own_ref), custom_call_target="tpu_custom_call" | custom-call | flops 1000000000 | bytes 6000000 | tf_op jit(solution)/shard_map/paths/pallas_call | solution.py:328
  62.3 0.9 %all-to-all-done.2.inc3_ref.got_ref = f32[8,56,128]{2,1,0:T(8,128)S(1)} async-done(((f32[8,56,128]{2,1,0:T(8,128)}), f32[8,56,128]{2,1,0:T(8,128)S(1)}, u32[]{:S(2)}, u32[]{:S(2)}) %all-to-all-start.2) | async-done | bytes 229408 | tf_op jit(solution)/shard_map/all_to_all | solution.py:605
  63.2 0.6 part_share.1
  63.8 3.7 %all-to-all-start.3 = ((f32[16,8,128]{2,1,0:T(8,128)}), f32[16,8,128]{2,1,0:T(8,128)S(1)}, u32[]{:S(2)}, u32[]{:S(2)}) async-start(f32[16,8,128]{2,1,0:T(8,128)} %part_share.1), calls=%async_computation.3 | async-start | bytes 131072 | tf_op jit(solution)/shard_map/all_to_all | solution.py:605
  67.6 0.0 collective-permute-done.3.other_ref
  67.6 13.9 %rows_down.1 = f32[4096,384]{1,0:T(8,128)} custom-call(s32[1]{0:T(128)} %bitcast.me, s32[4096]{0:T(1024)} %slot_hbm.3, s32[1,8]{1,0:T(1,128)} %sizes_hbm.3, f32[8,512,128]{2,1,0:T(8,128)} %basis_hbm.3, f32[8,512,384]{2,1,0:T(8,128)} %get-tuple-element.19.part_hbm, f32[8,128,384]{2,1,0:T(8,128)} %get-tuple-element.27.local_hbm, ...), custom_call_target="tpu_custom_call" | custom-call | flops 2000000000 | bytes 16000000 | tf_op jit(solution)/shard_map/rows_down/pallas_call | solution.py:562
  81.5 0.0 all-to-all-done.3.got_ref
  81.5 0.6 all_share.1
  (1 shorter events, 0.0 us)
Async XLA Ops:
  20.6 8.2 %collective-permute-start = (f32[2,384,128]{2,1,0:T(8,128)S(1)}, f32[2,384,128]{2,1,0:T(8,128)S(1)}, u32[]{:S(2)}, u32[]{:S(2)}) collective-permute-start(f32[2,384,128]{2,1,0:T(8,128)S(1)} %get-tuple-element.21.pay_ref), channel_id=1, source_target_pairs={{0,1},{1,0},{2,3},{3,2},{4,5},{5,4},{6,7},{7,6},{8,9},{9,8},{10,11... | collective-permute-start | bytes 1179656 | tf_op jit(solution)/shard_map/ppermute | solution.py:602
  22.2 10.6 %all-to-all-start = ((f32[8,48,128]{2,1,0:T(8,128)}), f32[8,48,128]{2,1,0:T(8,128)S(1)}, u32[]{:S(2)}, u32[]{:S(2)}) async-start(f32[8,48,128]{2,1,0:T(8,128)} %bitcast.5), calls=%async_computation | async-start | bytes 393216 | tf_op jit(solution)/shard_map/all_to_all | solution.py:605
  29.0 12.4 %collective-permute-start.1 = (f32[2,192,128]{2,1,0:T(8,128)S(1)}, f32[2,192,128]{2,1,0:T(8,128)S(1)}, u32[]{:S(2)}, u32[]{:S(2)}) collective-permute-start(f32[2,192,128]{2,1,0:T(8,128)S(1)} %after_core.1.pair2_ref), channel_id=1, source_target_pairs={{0,2},{1,3},{2,0},{3,1},{4,6},{5,7},{6,4},{7,5},{8,10},{9,11},{10,... | collective-permute-start | bytes 589832 | tf_op jit(solution)/shard_map/ppermute | solution.py:602
  33.8 16.5 %all-to-all-start.1 = ((f32[16,48,128]{2,1,0:T(8,128)}), f32[16,48,128]{2,1,0:T(8,128)S(1)}, u32[]{:S(2)}, u32[]{:S(2)}) async-start(f32[16,48,128]{2,1,0:T(8,128)} %bitcast.7), calls=%async_computation.1 | async-start | bytes 786432 | tf_op jit(solution)/shard_map/all_to_all | solution.py:605
  41.4 5.1 %collective-permute-start.2 = (f32[192,128]{1,0:T(8,128)S(1)}, f32[192,128]{1,0:T(8,128)S(1)}, u32[]{:S(2)}, u32[]{:S(2)}) collective-permute-start(f32[192,128]{1,0:T(8,128)S(1)} %after_pair.1.c2_ref), channel_id=1, source_target_pairs={{0,4},{1,5},{2,6},{3,7},{4,0},{5,1},{6,2},{7,3},{8,12},{9,13},{10,... | collective-permute-start | bytes 294920 | tf_op jit(solution)/shard_map/ppermute | solution.py:602
  51.5 11.7 %all-to-all-start.2 = ((f32[8,56,128]{2,1,0:T(8,128)}), f32[8,56,128]{2,1,0:T(8,128)S(1)}, u32[]{:S(2)}, u32[]{:S(2)}) async-start(f32[8,56,128]{2,1,0:T(8,128)} %after_top.1), calls=%async_computation.2 | async-start | bytes 458752 | tf_op jit(solution)/shard_map/all_to_all | solution.py:605
  57.2 10.3 %collective-permute-start.3 = (f32[192,128]{1,0:T(8,128)S(1)}, f32[192,128]{1,0:T(8,128)S(1)}, u32[]{:S(2)}, u32[]{:S(2)}) collective-permute-start(f32[192,128]{1,0:T(8,128)S(1)} %pair_field.1.after_ref.own_ref), channel_id=1, source_target_pairs={{0,1},{1,0},{2,3},{3,2},{4,5},{5,4},{6,7},{7,6},{8,9},{9,8},{10,11... | collective-permute-start | bytes 294920 | tf_op jit(solution)/shard_map/ppermute | solution.py:602
  63.8 17.7 %all-to-all-start.3 = ((f32[16,8,128]{2,1,0:T(8,128)}), f32[16,8,128]{2,1,0:T(8,128)S(1)}, u32[]{:S(2)}, u32[]{:S(2)}) async-start(f32[16,8,128]{2,1,0:T(8,128)} %part_share.1), calls=%async_computation.3 | async-start | bytes 131072 | tf_op jit(solution)/shard_map/all_to_all | solution.py:605

commit v6 on v5

--- a/solution.py
+++ b/solution.py
@@ -17,7 +17,7 @@
 S = 4
 MB = 128
 BT = 16
-UN = 32
+UN = 64
 F32 = jnp.float32
 BF16 = jnp.bfloat16
 MIB = 1 << 20
@@ -168,6 +168,9 @@
         if leaf == 3:
             for cp in nears[4:]:
                 cp.wait()
+    cp = pltpu.make_async_copy(call_ref.at[pl.ds(0, NL)], call_hbm.at[pl.ds(0, NL)], osem.at[NL + 1])
+    cp.start()
+    outs.append(cp)
     copies[3].wait()
     copies[4].wait()
     offset, at = 0, NL
@@ -182,7 +185,7 @@
                 at += 1
         offset += len(coeffs)
         coeffs = [split(c) for c in parents]
-    cp = pltpu.make_async_copy(call_ref, call_hbm, osem.at[NL])
+    cp = pltpu.make_async_copy(call_ref.at[pl.ds(NL, 6)], call_hbm.at[pl.ds(NL, 6)], osem.at[NL])
     cp.start()
     outs.append(cp)
     curv_ref[...] = jnp.broadcast_to(total, (8, V))
@@ -224,7 +227,7 @@
             pltpu.SemaphoreType.DMA((5,)),
             pltpu.SemaphoreType.DMA((NL,)),
             pltpu.SemaphoreType.DMA((NL,)),
-            pltpu.SemaphoreType.DMA((NL + 1,)),
+            pltpu.SemaphoreType.DMA((NL + 2,)),
         ],
         compiler_params=pltpu.CompilerParams(vmem_limit_bytes=50 * MIB),
         cost_estimate=pl.CostEstimate(flops=7 * 10**9, bytes_accessed=28 * 10**6, transcendentals=0),

time: 82.6 us -> 82.1 us (level)
  no operation moved by 1% of the time
where the time goes in v6:
time: 82.1 us; the launch traced here: 81.6 us
  Pallas kernels  48.4 us (59%)
  starting transfers between devices  25 us (30%)
  waiting for transfers between devices  7.39 us (9%)
    all_to_all x4, starting transfers between devices, exchange(): lax.all_to_all(value, 'leaf', 0, 0, axis_index_groups=groups_of(bits, cou...  21.4 us
    pallas_call x1, Pallas kernels, rows_up(): pl.pallas_call(rows_up_kernel, out_shape=(pltpu.HBM((NL, LEAF, V), F32),...  19.6 us
    pallas_call x1, Pallas kernels, rows_down(): pl.pallas_call(rows_down_kernel, out_shape=pltpu.HBM((ROWS, V), F32), in_...  13.9 us
    all_to_all x4, waiting for transfers between devices, exchange(): lax.all_to_all(value, 'leaf', 0, 0, axis_index_groups=groups_of(bits, cou...  7.03 us
    pallas_call x8, Pallas kernels, call(): pl.pallas_call(body, out_shape=tuple((jax.ShapeDtypeStruct(o, F32) for o...  5.77 us
    pallas_call x1, Pallas kernels, paths(): pl.pallas_call(paths_kernel, out_shape=(pltpu.HBM((NL, R, V), F32), pltpu...  4.92 us
    pallas_call x1, Pallas kernels, fields(): pl.pallas_call(fields_kernel, out_shape=(pltpu.HBM((14, R, V), F32), jax....  4.16 us
    ppermute x4, starting transfers between devices, swap(): lax.ppermute(value, 'leaf', [(s, s ^ 1 << level) for s in range(count)])  3.67 us
  transfers between devices with their start and end apart: 8, of which 4 were waited for; matrix products, arithmetic and copies ran while one was open for 0% of the time, Pallas kernels for 33%

profile of v6, /device:TPU:1, one launch (start us, length us, event | category | flops | bytes accessed | tf_op | source)
XLA Modules:
  0.0 81.6 jit_solution(4643305750839707870)
XLA Ops:
  0.6 19.6 %rows_up.1 = (f32[8,512,384]{2,1,0:T(8,128)}, f32[14,128,384]{2,1,0:T(8,128)}, f32[2,384,128]{2,1,0:T(8,128)S(1)}, f32[8,384]{1,0:T(8,128)S(1)}, f32[384,128]{1,0:T(8,128)}) custom-call(s32[4096]{0:T(1024)} %slot_hbm.3, s32[1,8]{1,0:T(1,128)} %sizes_hbm.3, f32[4096,384]{1,0:T(8,128)} %v_hbm.1, f32[8,512,128]{2,1,0:T(8,128)} %basis_hbm.3, ...), custom_call_target="tpu_custom_call" | custom-call | flops 7000000000 | bytes 28000000 | tf_op jit(solution)/shard_map/rows_up/pallas_call | solution.py:203
  20.3 1.5 %collective-permute-start = (f32[2,384,128]{2,1,0:T(8,128)S(1)}, f32[2,384,128]{2,1,0:T(8,128)S(1)}, u32[]{:S(2)}, u32[]{:S(2)}) collective-permute-start(f32[2,384,128]{2,1,0:T(8,128)S(1)} %get-tuple-element.21.pay_ref), channel_id=1, source_target_pairs={{0,1},{1,0},{2,3},{3,2},{4,5},{5,4},{6,7},{7,6},{8,9},{9,8},{10,11... | collective-permute-start | bytes 1179656 | tf_op jit(solution)/shard_map/ppermute | solution.py:605
  21.8 4.7 %all-to-all-start = ((f32[8,48,128]{2,1,0:T(8,128)}), f32[8,48,128]{2,1,0:T(8,128)S(1)}, u32[]{:S(2)}, u32[]{:S(2)}) async-start(f32[8,48,128]{2,1,0:T(8,128)} %bitcast.5), calls=%async_computation | async-start | bytes 393216 | tf_op jit(solution)/shard_map/all_to_all | solution.py:608
  26.4 1.9 %chains.1 = (f32[128,128]{1,0:T(8,128)S(1)}, f32[128,384]{1,0:T(8,128)S(1)}, f32[256,128]{1,0:T(8,128)S(1)}, f32[384,128]{1,0:T(8,128)S(1)}, f32[512,128]{1,0:T(8,128)S(1)}, /*index=5*/f32[128,128]{1,0:T(8,128)S(1)}) custom-call(s32[1]{0:T(128)} %bitcast.me, f32[15,128,128]{2,1,0:T(8,128)} %bitcast.12, f32[5,128,128]{2,1,0:T(8,128)} %bitcast.16, ...), custom_call_target="tpu_custom_call" | custom-call | flops 100000000 | bytes 1000000 | tf_op jit(solution)/shard_map/chains/pallas_call | solution.py:467
  28.3 0.0 collective-permute-done.got_ref
  28.3 0.2 after_core.1.pair2_ref
  28.5 1.5 %collective-permute-start.1 = (f32[2,192,128]{2,1,0:T(8,128)S(1)}, f32[2,192,128]{2,1,0:T(8,128)S(1)}, u32[]{:S(2)}, u32[]{:S(2)}) collective-permute-start(f32[2,192,128]{2,1,0:T(8,128)S(1)} %after_core.1.pair2_ref), channel_id=1, source_target_pairs={{0,2},{1,3},{2,0},{3,1},{4,6},{5,7},{6,4},{7,5},{8,10},{9,11},{10,... | collective-permute-start | bytes 589832 | tf_op jit(solution)/shard_map/ppermute | solution.py:605
  30.0 2.4 %all-to-all-done = f32[8,48,128]{2,1,0:T(8,128)S(1)} async-done(((f32[8,48,128]{2,1,0:T(8,128)}), f32[8,48,128]{2,1,0:T(8,128)S(1)}, u32[]{:S(2)}, u32[]{:S(2)}) %all-to-all-start) | async-done | bytes 196640 | tf_op jit(solution)/shard_map/all_to_all | solution.py:608
  32.3 1.0 %after_y.1 = (f32[768,128]{1,0:T(8,128)}, f32[48,128]{1,0:T(8,128)S(1)}) custom-call(s32[1]{0:T(128)} %bitcast.me, f32[384,128]{1,0:T(8,128)S(1)} %bitcast.10, f32[128,384]{1,0:T(8,128)S(1)} %get-tuple-element.30.a2_ref, f32[2,192,128]{2,1,0:T(8,128)S(1)} %after_core.1.pair2_ref), custom_call_target="tpu_custom_call" | custom-call | flops 100000000 | bytes 1000000 | tf_op jit(solution)/shard_map/after_y/pallas_call | solution.py:467
  33.3 7.5 %all-to-all-start.1 = ((f32[16,48,128]{2,1,0:T(8,128)}), f32[16,48,128]{2,1,0:T(8,128)S(1)}, u32[]{:S(2)}, u32[]{:S(2)}) async-start(f32[16,48,128]{2,1,0:T(8,128)} %bitcast.7), calls=%async_computation.1 | async-start | bytes 786432 | tf_op jit(solution)/shard_map/all_to_all | solution.py:608
  40.9 0.0 collective-permute-done.1.got_ref.pair_got_ref
  40.9 0.5 collective-permute-start.2
  41.4 4.2 %fields.1 = (f32[14,128,384]{2,1,0:T(8,128)}, f32[8,384]{1,0:T(8,128)S(1)}) custom-call(s32[1]{0:T(128)} %bitcast.me, f32[14,128,384]{2,1,0:T(8,128)} %get-tuple-element.20.call_hbm, f32[7,128,128]{2,1,0:T(8,128)} %bitcast.17, f32[2,384,128]{2,1,0:T(8,128)S(1)} %get-tuple-element.21.pay_ref, f32[2,384,128]{2,1,0:T(8,128)S(1)} %collective-permute-done.got_ref, ...), custom_call_target="tpu_custom_call" | custom-call | flops 2000000000 | bytes 16000000 | tf_op jit(solution)/shard_map/fields/pallas_call | solution.py:285
  45.6 0.3 collective-permute-done.2.quad_got_ref
  45.9 3.8 %all-to-all-done.1 = f32[16,48,128]{2,1,0:T(8,128)S(1)} async-done(((f32[16,48,128]{2,1,0:T(8,128)}), f32[16,48,128]{2,1,0:T(8,128)S(1)}, u32[]{:S(2)}, u32[]{:S(2)}) %all-to-all-start.1) | async-done | bytes 393248 | tf_op jit(solution)/shard_map/all_to_all | solution.py:608
  49.8 1.3 %after_top.1 = f32[8,56,128]{2,1,0:T(8,128)} custom-call(s32[1]{0:T(128)} %bitcast.me, f32[768,128]{1,0:T(8,128)S(1)} %bitcast.9, f32[512,128]{1,0:T(8,128)S(1)} %get-tuple-element.32.m3_ref, f32[128,128]{1,0:T(8,128)S(1)} %get-tuple-element.33.side2_ref, f32[192,128]{1,0:T(8,128)S(1)} %after_pair.1.c2_ref, ...), custom_call_target="tpu_custom_call" | custom-call | flops 100000000 | bytes 1000000 | tf_op jit(solution)/shard_map/after_top/pallas_call | solution.py:467
  51.0 5.5 %all-to-all-start.2 = ((f32[8,56,128]{2,1,0:T(8,128)}), f32[8,56,128]{2,1,0:T(8,128)S(1)}, u32[]{:S(2)}, u32[]{:S(2)}) async-start(f32[8,56,128]{2,1,0:T(8,128)} %after_top.1), calls=%async_computation.2 | async-start | bytes 458752 | tf_op jit(solution)/shard_map/all_to_all | solution.py:608
  56.5 0.2 pair_field.1.after_ref.own_ref
  56.7 0.2 collective-permute-start.3
  56.9 4.9 %paths.1 = (f32[8,128,384]{2,1,0:T(8,128)}, f32[8,128,128]{2,1,0:T(8,128)}) custom-call(f32[14,128,384]{2,1,0:T(8,128)} %get-tuple-element.26.field_hbm, f32[15,128,128]{2,1,0:T(8,128)} %bitcast.13, f32[192,128]{1,0:T(8,128)S(1)} %pair_field.1.after_ref.own_ref), custom_call_target="tpu_custom_call" | custom-call | flops 1000000000 | bytes 6000000 | tf_op jit(solution)/shard_map/paths/pallas_call | solution.py:331
  61.8 0.9 %all-to-all-done.2.inc3_ref.got_ref = f32[8,56,128]{2,1,0:T(8,128)S(1)} async-done(((f32[8,56,128]{2,1,0:T(8,128)}), f32[8,56,128]{2,1,0:T(8,128)S(1)}, u32[]{:S(2)}, u32[]{:S(2)}) %all-to-all-start.2) | async-done | bytes 229408 | tf_op jit(solution)/shard_map/all_to_all | solution.py:608
  62.7 0.6 part_share.1
  63.3 3.7 %all-to-all-start.3 = ((f32[16,8,128]{2,1,0:T(8,128)}), f32[16,8,128]{2,1,0:T(8,128)S(1)}, u32[]{:S(2)}, u32[]{:S(2)}) async-start(f32[16,8,128]{2,1,0:T(8,128)} %part_share.1), calls=%async_computation.3 | async-start | bytes 131072 | tf_op jit(solution)/shard_map/all_to_all | solution.py:608
  67.0 0.0 collective-permute-done.3.other_ref
  67.0 13.9 %rows_down.1 = f32[4096,384]{1,0:T(8,128)} custom-call(s32[1]{0:T(128)} %bitcast.me, s32[4096]{0:T(1024)} %slot_hbm.3, s32[1,8]{1,0:T(1,128)} %sizes_hbm.3, f32[8,512,128]{2,1,0:T(8,128)} %basis_hbm.3, f32[8,512,384]{2,1,0:T(8,128)} %get-tuple-element.19.part_hbm, f32[8,128,384]{2,1,0:T(8,128)} %get-tuple-element.27.local_hbm, ...), custom_call_target="tpu_custom_call" | custom-call | flops 2000000000 | bytes 16000000 | tf_op jit(solution)/shard_map/rows_down/pallas_call | solution.py:565
  81.0 0.0 all-to-all-done.3.got_ref
  81.0 0.6 all_share.1
  (1 shorter events, 0.0 us)
Async XLA Ops:
  20.3 8.0 %collective-permute-start = (f32[2,384,128]{2,1,0:T(8,128)S(1)}, f32[2,384,128]{2,1,0:T(8,128)S(1)}, u32[]{:S(2)}, u32[]{:S(2)}) collective-permute-start(f32[2,384,128]{2,1,0:T(8,128)S(1)} %get-tuple-element.21.pay_ref), channel_id=1, source_target_pairs={{0,1},{1,0},{2,3},{3,2},{4,5},{5,4},{6,7},{7,6},{8,9},{9,8},{10,11... | collective-permute-start | bytes 1179656 | tf_op jit(solution)/shard_map/ppermute | solution.py:605
  21.8 10.6 %all-to-all-start = ((f32[8,48,128]{2,1,0:T(8,128)}), f32[8,48,128]{2,1,0:T(8,128)S(1)}, u32[]{:S(2)}, u32[]{:S(2)}) async-start(f32[8,48,128]{2,1,0:T(8,128)} %bitcast.5), calls=%async_computation | async-start | bytes 393216 | tf_op jit(solution)/shard_map/all_to_all | solution.py:608
  28.5 12.4 %collective-permute-start.1 = (f32[2,192,128]{2,1,0:T(8,128)S(1)}, f32[2,192,128]{2,1,0:T(8,128)S(1)}, u32[]{:S(2)}, u32[]{:S(2)}) collective-permute-start(f32[2,192,128]{2,1,0:T(8,128)S(1)} %after_core.1.pair2_ref), channel_id=1, source_target_pairs={{0,2},{1,3},{2,0},{3,1},{4,6},{5,7},{6,4},{7,5},{8,10},{9,11},{10,... | collective-permute-start | bytes 589832 | tf_op jit(solution)/shard_map/ppermute | solution.py:605
  33.3 16.4 %all-to-all-start.1 = ((f32[16,48,128]{2,1,0:T(8,128)}), f32[16,48,128]{2,1,0:T(8,128)S(1)}, u32[]{:S(2)}, u32[]{:S(2)}) async-start(f32[16,48,128]{2,1,0:T(8,128)} %bitcast.7), calls=%async_computation.1 | async-start | bytes 786432 | tf_op jit(solution)/shard_map/all_to_all | solution.py:608
  40.9 5.1 %collective-permute-start.2 = (f32[192,128]{1,0:T(8,128)S(1)}, f32[192,128]{1,0:T(8,128)S(1)}, u32[]{:S(2)}, u32[]{:S(2)}) collective-permute-start(f32[192,128]{1,0:T(8,128)S(1)} %after_pair.1.c2_ref), channel_id=1, source_target_pairs={{0,4},{1,5},{2,6},{3,7},{4,0},{5,1},{6,2},{7,3},{8,12},{9,13},{10,... | collective-permute-start | bytes 294920 | tf_op jit(solution)/shard_map/ppermute | solution.py:605
  51.0 11.7 %all-to-all-start.2 = ((f32[8,56,128]{2,1,0:T(8,128)}), f32[8,56,128]{2,1,0:T(8,128)S(1)}, u32[]{:S(2)}, u32[]{:S(2)}) async-start(f32[8,56,128]{2,1,0:T(8,128)} %after_top.1), calls=%async_computation.2 | async-start | bytes 458752 | tf_op jit(solution)/shard_map/all_to_all | solution.py:608
  56.7 10.3 %collective-permute-start.3 = (f32[192,128]{1,0:T(8,128)S(1)}, f32[192,128]{1,0:T(8,128)S(1)}, u32[]{:S(2)}, u32[]{:S(2)}) collective-permute-start(f32[192,128]{1,0:T(8,128)S(1)} %pair_field.1.after_ref.own_ref), channel_id=1, source_target_pairs={{0,1},{1,0},{2,3},{3,2},{4,5},{5,4},{6,7},{7,6},{8,9},{9,8},{10,11... | collective-permute-start | bytes 294920 | tf_op jit(solution)/shard_map/ppermute | solution.py:605
  63.3 17.7 %all-to-all-start.3 = ((f32[16,8,128]{2,1,0:T(8,128)}), f32[16,8,128]{2,1,0:T(8,128)S(1)}, u32[]{:S(2)}, u32[]{:S(2)}) async-start(f32[16,8,128]{2,1,0:T(8,128)} %part_share.1), calls=%async_computation.3 | async-start | bytes 131072 | tf_op jit(solution)/shard_map/all_to_all | solution.py:608
